TPU v7x, 32 devices: a whole 2x2x4 slice. The times are simulated.
32 devices in a mesh: dp: 16 (over z, y, x), tensor: 2 (over core).
Axes of the slice: x: 2, y: 2, z: 4, core: 2. Of those that a mesh axis runs over, the one named last changes fastest.
Arguments:
- tokens: bfloat16 [32768, 768], P(('dp', 'tensor')), may hold values from -6 to 6
- grad_out: bfloat16 [32768, 768], P(('dp', 'tensor')), may hold values from -6 to 6
- prefix: int32 [32], P('dp'), may hold values from 102 to 512
- pre_gain: float32 [768], replicated, may hold values from 0.5 to 1.5
- pre_bias: float32 [768], replicated, may hold values from -1 to 1
- qkv_weight: bfloat16 [768, 3, 768], P(None, None, 'tensor'), may hold values from -0.21875 to 0.21875
- qv_bias: float32 [2, 768], P(None, 'tensor'), may hold values from -1.5 to 1.5
- sub_gain: float32 [768], P('tensor'), may hold values from 0.5 to 1.5
- sub_bias: float32 [768], P('tensor'), may hold values from -1 to 1
- out_weight: bfloat16 [768, 768], P('tensor'), may hold values from -0.375 to 0.375
- out_bias: float32 [768], replicated, may hold values from -1 to 1
- ffn_gain: float32 [768], replicated, may hold values from 0.5 to 1.5
- ffn_bias: float32 [768], replicated, may hold values from -1 to 1
- up_weight: bfloat16 [768, 3072], P(None, 'tensor'), may hold values from -0.375 to 0.375
- up_bias: float32 [3072], P('tensor'), may hold values from -2.5 to 2.5
- inner_gain: float32 [3072], P('tensor'), may hold values from 0.5 to 1.5
- inner_bias: float32 [3072], P('tensor'), may hold values from -1 to 1
- down_weight: bfloat16 [3072, 768], P('tensor'), may hold values from -0.1875 to 0.1875
- down_bias: float32 [768], replicated, may hold values from -1 to 1
Outputs:
- output: bfloat16 [32768, 768], P(('dp', 'tensor'))
- input_grad: float32 [32768, 768], P(('dp', 'tensor'))
- grad_pre_gain: float32 [768], replicated
- grad_pre_bias: float32 [768], replicated
- grad_qkv_weight: float32 [768, 3, 768], P(None, None, 'tensor')
- grad_qv_bias: float32 [2, 768], P(None, 'tensor')
- grad_sub_gain: float32 [768], P('tensor')
- grad_sub_bias: float32 [768], P('tensor')
- grad_out_weight: float32 [768, 768], P('tensor')
- grad_out_bias: float32 [768], replicated
- grad_ffn_gain: float32 [768], replicated
- grad_ffn_bias: float32 [768], replicated
- grad_up_weight: float32 [768, 3072], P(None, 'tensor')
- grad_up_bias: float32 [3072], P('tensor')
- grad_inner_gain: float32 [3072], P('tensor')
- grad_inner_bias: float32 [3072], P('tensor')
- grad_down_weight: float32 [3072, 768], P('tensor')
- grad_down_bias: float32 [768], replicated
All inputs are finite; a program needn't handle non-finite values.
Results may differ from a plain program's by a relative error of at most 0.013.
Values may be sent and summed in bfloat16 or wider, within the bound.
A program may use at most 192 MiB of HBM per device.

v0:
```python
import jax
import jax.numpy as jnp
from jax import lax
from jax.sharding import PartitionSpec as P

D = 768
HEAD_DIM = 64
FF = 3072
SEQ_LEN = 1024
QBLOCK = 512


norm_eps = 1e-05


def layer_norm(values, norm_gain, norm_bias):
    centre = values - jnp.mean(values, axis=-1, keepdims=True)
    spread = jnp.mean(centre * centre, axis=-1, keepdims=True)
    return centre * lax.rsqrt(spread + norm_eps) * norm_gain + norm_bias


def gelu_exact(values):
    return jax.nn.gelu(values, approximate=False)


def gather_rows(values):
    return lax.all_gather(values, "tensor", axis=0, tiled=True)


def scatter_rows(left_rows, project):
    return lax.psum_scatter(project(left_rows), "tensor", scatter_dimension=0, tiled=True)


def right_product(left_rows, weight):
    return jnp.dot(left_rows, weight, preferred_element_type=jnp.float32)


def back_product(left_rows, weight):
    return lax.dot_general(
        left_rows, weight, (((1,), (1,)), ((), ())), preferred_element_type=jnp.float32
    )


def left_product(first_rows, second_rows):
    return lax.dot_general(
        first_rows, second_rows, (((0,), (0,)), ((), ())), preferred_element_type=jnp.float32
    )


def split_norm(values, features):
    row_mean = lax.psum(jnp.sum(values, axis=-1), "tensor") / features
    centred = values - row_mean[:, None]
    spread = lax.psum(jnp.sum(centred * centred, axis=-1), "tensor") / features
    inv_scale = lax.rsqrt(spread + norm_eps)
    return (centred * inv_scale[:, None], inv_scale)


def split_norm_back(grad_normed, normed, inv_scale, features):
    grad_total, cross_total = lax.psum(
        (jnp.sum(grad_normed, axis=-1), jnp.sum(grad_normed * normed, axis=-1)), "tensor"
    )
    return inv_scale[:, None] * (
        grad_normed - grad_total[:, None] / features - normed * (cross_total[:, None] / features)
    )


def masked_scores(query_block, key_seq, row_start, prefix_len):
    block_rows = query_block.shape[0]
    head_count = query_block.shape[1] // HEAD_DIM
    query_heads = query_block.reshape(block_rows, head_count, HEAD_DIM)
    key_heads = key_seq.reshape(key_seq.shape[0], head_count, HEAD_DIM)
    scores = jnp.einsum(
        "qhd,khd->hqk", query_heads, key_heads, preferred_element_type=jnp.float32
    ) * HEAD_DIM ** (-0.5)
    query_pos = row_start + lax.iota(jnp.int32, block_rows)
    key_pos = lax.iota(jnp.int32, key_seq.shape[0])
    visible = (key_pos[None, :] <= query_pos[:, None]) | (key_pos[None, :] < prefix_len)
    return jnp.where(visible[None], scores, -1e30)


def body(
    tokens,
    grad_out,
    prefix,
    pre_gain,
    pre_bias,
    qkv_weight,
    qv_bias,
    sub_gain,
    sub_bias,
    out_weight,
    out_bias,
    ffn_gain,
    ffn_bias,
    up_weight,
    up_bias,
    inner_gain,
    inner_bias,
    down_weight,
    down_bias,
):
    residual = tokens.astype(jnp.float32)
    normed_one, pullback_one = jax.vjp(layer_norm, residual, pre_gain, pre_bias)
    whole_one = gather_rows(normed_one.astype(jnp.bfloat16))
    projected = jnp.einsum("ld,dcn->lcn", whole_one, qkv_weight, preferred_element_type=jnp.float32)
    queries = (projected[:, 0] + qv_bias[0]).astype(jnp.bfloat16)
    key_rows = projected[:, 1].astype(jnp.bfloat16)
    value_rows = (projected[:, 2] + qv_bias[1]).astype(jnp.bfloat16)
    group_rows = whole_one.shape[0]
    local_width = queries.shape[1]
    head_count = local_width // HEAD_DIM
    seq_count = group_rows // SEQ_LEN
    blocks_per_seq = SEQ_LEN // QBLOCK
    score_scale = HEAD_DIM ** (-0.5)

    def forward_block(block_index):
        seq_index = block_index // blocks_per_seq
        row_start = block_index % blocks_per_seq * QBLOCK
        seq_base = seq_index * SEQ_LEN
        query_block = lax.dynamic_slice_in_dim(queries, seq_base + row_start, QBLOCK, 0)
        key_seq = lax.dynamic_slice_in_dim(key_rows, seq_base, SEQ_LEN, 0)
        value_seq = lax.dynamic_slice_in_dim(value_rows, seq_base, SEQ_LEN, 0)
        scores = masked_scores(query_block, key_seq, row_start, prefix[seq_index])
        row_peak = jnp.max(scores, axis=-1, keepdims=True)
        weights_exp = jnp.exp(scores - row_peak)
        row_total = jnp.sum(weights_exp, axis=-1, keepdims=True)
        weights = weights_exp / row_total
        value_heads = value_seq.reshape(SEQ_LEN, head_count, HEAD_DIM)
        mixed_heads = jnp.einsum(
            "hqk,khd->qhd",
            weights.astype(jnp.bfloat16),
            value_heads,
            preferred_element_type=jnp.float32,
        )
        return (mixed_heads.reshape(QBLOCK, local_width), (row_peak + jnp.log(row_total))[..., 0])

    attended, log_sums = lax.map(
        forward_block, jnp.arange(seq_count * blocks_per_seq, dtype=jnp.int32)
    )
    attended = attended.reshape(group_rows, local_width)
    normed_two, scale_two = split_norm(attended, D)
    branch_in = (normed_two * sub_gain + sub_bias).astype(jnp.bfloat16)
    attn_sum = scatter_rows(branch_in, lambda part_rows: right_product(part_rows, out_weight))
    middle = residual + attn_sum + out_bias
    normed_three, pullback_three = jax.vjp(layer_norm, middle, ffn_gain, ffn_bias)
    whole_three = gather_rows(normed_three.astype(jnp.bfloat16))
    hidden = right_product(whole_three, up_weight) + up_bias
    activated, pullback_gelu = jax.vjp(gelu_exact, hidden)
    normed_four, scale_four = split_norm(activated, FF)
    ffn_in = (normed_four * inner_gain + inner_bias).astype(jnp.bfloat16)
    ffn_sum = scatter_rows(ffn_in, lambda part_rows: right_product(part_rows, down_weight))
    output = (middle + ffn_sum + down_bias).astype(jnp.bfloat16)
    grad_end = grad_out.astype(jnp.float32)
    grad_down_bias = jnp.sum(grad_end, axis=0)
    grad_whole = gather_rows(grad_end.astype(jnp.bfloat16))
    grad_down_weight = left_product(ffn_in, grad_whole)
    grad_inner_in = back_product(grad_whole, down_weight)
    grad_inner_gain = jnp.sum(grad_inner_in * normed_four, axis=0)
    grad_inner_bias = jnp.sum(grad_inner_in, axis=0)
    grad_activated = split_norm_back(grad_inner_in * inner_gain, normed_four, scale_four, FF)
    grad_hidden = pullback_gelu(grad_activated)[0]
    grad_up_bias = jnp.sum(grad_hidden, axis=0)
    grad_hidden_low = grad_hidden.astype(jnp.bfloat16)
    grad_up_weight = left_product(whole_three, grad_hidden_low)
    grad_ffn_norm = scatter_rows(
        grad_hidden_low, lambda part_rows: back_product(part_rows, up_weight)
    )
    grad_mid_norm, grad_ffn_gain, grad_ffn_bias = pullback_three(grad_ffn_norm)
    grad_middle = grad_end + grad_mid_norm
    grad_out_bias = jnp.sum(grad_middle, axis=0)
    grad_mid_whole = gather_rows(grad_middle.astype(jnp.bfloat16))
    grad_out_weight = left_product(branch_in, grad_mid_whole)
    grad_branch = back_product(grad_mid_whole, out_weight)
    grad_sub_gain = jnp.sum(grad_branch * normed_two, axis=0)
    grad_sub_bias = jnp.sum(grad_branch, axis=0)
    grad_attended = split_norm_back(grad_branch * sub_gain, normed_two, scale_two, D).astype(
        jnp.bfloat16
    )

    def backward_seq(seq_index):
        seq_base = seq_index * SEQ_LEN
        key_seq = lax.dynamic_slice_in_dim(key_rows, seq_base, SEQ_LEN, 0)
        value_seq = lax.dynamic_slice_in_dim(value_rows, seq_base, SEQ_LEN, 0)
        key_heads = key_seq.reshape(SEQ_LEN, head_count, HEAD_DIM)
        value_heads = value_seq.reshape(SEQ_LEN, head_count, HEAD_DIM)
        prefix_len = prefix[seq_index]

        def one_block(running, block_num):
            key_grad, value_grad = running
            row_start = block_num * QBLOCK
            query_block = lax.dynamic_slice_in_dim(queries, seq_base + row_start, QBLOCK, 0)
            query_heads = query_block.reshape(QBLOCK, head_count, HEAD_DIM)
            out_grad = lax.dynamic_slice_in_dim(
                grad_attended, seq_base + row_start, QBLOCK, 0
            ).reshape(QBLOCK, head_count, HEAD_DIM)
            block_lse = log_sums[seq_index * blocks_per_seq + block_num]
            scores = masked_scores(query_block, key_seq, row_start, prefix_len)
            weights = jnp.exp(scores - block_lse[..., None])
            value_grad = value_grad + jnp.einsum(
                "hqk,qhd->khd",
                weights.astype(jnp.bfloat16),
                out_grad,
                preferred_element_type=jnp.float32,
            )
            weight_grad = jnp.einsum(
                "qhd,khd->hqk", out_grad, value_heads, preferred_element_type=jnp.float32
            )
            score_grad = weights * (
                weight_grad - jnp.sum(weights * weight_grad, axis=-1, keepdims=True)
            )
            score_low = score_grad.astype(jnp.bfloat16)
            query_grad = (
                jnp.einsum("hqk,khd->qhd", score_low, key_heads, preferred_element_type=jnp.float32)
                * score_scale
            )
            key_grad = (
                key_grad
                + jnp.einsum(
                    "hqk,qhd->khd", score_low, query_heads, preferred_element_type=jnp.float32
                )
                * score_scale
            )
            return ((key_grad, value_grad), query_grad.reshape(QBLOCK, local_width))

        zeros_heads = jnp.zeros((SEQ_LEN, head_count, HEAD_DIM), jnp.float32)
        (key_grad, value_grad), query_grads = lax.scan(
            one_block, (zeros_heads, zeros_heads), jnp.arange(blocks_per_seq, dtype=jnp.int32)
        )
        return (
            query_grads.reshape(SEQ_LEN, local_width),
            key_grad.reshape(SEQ_LEN, local_width),
            value_grad.reshape(SEQ_LEN, local_width),
        )

    query_grad, key_grad, value_grad = lax.map(backward_seq, jnp.arange(seq_count, dtype=jnp.int32))
    query_grad = query_grad.reshape(group_rows, local_width)
    key_grad = key_grad.reshape(group_rows, local_width)
    value_grad = value_grad.reshape(group_rows, local_width)
    grad_qv_bias = jnp.stack([jnp.sum(query_grad, axis=0), jnp.sum(value_grad, axis=0)])
    grad_proj = jnp.stack([query_grad, key_grad, value_grad], axis=1).astype(jnp.bfloat16)
    grad_qkv_weight = jnp.einsum(
        "ld,lcn->dcn", whole_one, grad_proj, preferred_element_type=jnp.float32
    )
    flat_grad = grad_proj.reshape(group_rows, 3 * local_width)
    flat_weight = qkv_weight.reshape(qkv_weight.shape[0], 3 * local_width)
    grad_pre_norm = scatter_rows(flat_grad, lambda part_rows: back_product(part_rows, flat_weight))
    grad_tok_norm, grad_pre_gain, grad_pre_bias = pullback_one(grad_pre_norm)
    input_grad = grad_middle + grad_tok_norm
    (
        grad_qkv_weight,
        grad_qv_bias,
        grad_sub_gain,
        grad_sub_bias,
        grad_out_weight,
        grad_up_weight,
        grad_up_bias,
        grad_inner_gain,
        grad_inner_bias,
        grad_down_weight,
    ) = lax.psum(
        (
            grad_qkv_weight,
            grad_qv_bias,
            grad_sub_gain,
            grad_sub_bias,
            grad_out_weight,
            grad_up_weight,
            grad_up_bias,
            grad_inner_gain,
            grad_inner_bias,
            grad_down_weight,
        ),
        "dp",
    )
    grad_pre_gain, grad_pre_bias, grad_out_bias, grad_ffn_gain, grad_ffn_bias, grad_down_bias = (
        lax.psum(
            (
                grad_pre_gain,
                grad_pre_bias,
                grad_out_bias,
                grad_ffn_gain,
                grad_ffn_bias,
                grad_down_bias,
            ),
            ("dp", "tensor"),
        )
    )
    return (
        output,
        input_grad,
        grad_pre_gain,
        grad_pre_bias,
        grad_qkv_weight,
        grad_qv_bias,
        grad_sub_gain,
        grad_sub_bias,
        grad_out_weight,
        grad_out_bias,
        grad_ffn_gain,
        grad_ffn_bias,
        grad_up_weight,
        grad_up_bias,
        grad_inner_gain,
        grad_inner_bias,
        grad_down_weight,
        grad_down_bias,
    )


def solution(mesh):
    return jax.shard_map(
        body,
        mesh=mesh,
        in_specs=(
            P(("dp", "tensor"), None),
            P(("dp", "tensor"), None),
            P("dp"),
            P(),
            P(),
            P(None, None, "tensor"),
            P(None, "tensor"),
            P("tensor"),
            P("tensor"),
            P("tensor", None),
            P(),
            P(),
            P(),
            P(None, "tensor"),
            P("tensor"),
            P("tensor"),
            P("tensor"),
            P("tensor", None),
            P(),
        ),
        out_specs=(
            P(("dp", "tensor"), None),
            P(("dp", "tensor"), None),
            P(),
            P(),
            P(None, None, "tensor"),
            P(None, "tensor"),
            P("tensor"),
            P("tensor"),
            P("tensor", None),
            P(),
            P(),
            P(),
            P(None, "tensor"),
            P("tensor"),
            P("tensor"),
            P("tensor"),
            P("tensor", None),
            P(),
        ),
        check_vma=False,
    )
```

profile of v0, /device:TPU:0, one launch (start us, length us, event | category | flops | bytes accessed | tf_op | source)
XLA Modules:
  0.0 1060.7 jit_solution(7124680951872722405)
XLA Ops:
  14.3 14.9 %all-gather.5.cloned.1.call-done = bf16[2048,768]{1,0:T(8,128)(2,1)} async-done(((bf16[1024,768]{1,0:T(8,128)(2,1)}), bf16[2048,768]{1,0:T(8,128)(2,1)}) %all-gather.5.cloned.1.call-update) | async-done | bytes 3145744 | tf_op jit(solution)/shard_map/all_gather | solution.py:27
  47.5 84.4 %while.45 = (s32[]{:T(128)}, f32[4,512,384]{1,2,0:T(8,128)}, f32[4,6,512]{2,1,0:T(8,128)}, s32[4]{0:T(128)S(1)}, bf16[2048,384]{0,1:T(8,128)(2,1)}, /*index=5*/s...) while((s32[]{:T(128)}, f32[4,512,384]{1,2,0:T(8,128)}, ...), condition=%wide.region_5.6_spmd, body=%wide.region_2.5_spmd.sunk | while | flops 844102144 | bytes 51359252 | solution.py:137
  154.9 14.2 %reduce-scatter.5.cloned.1.call-done = f32[1024,768]{1,0:T(8,128)} async-done(((f32[2048,768]{1,0:T(8,128)}), f32[1024,768]{1,0:T(8,128)}) %reduce-scatter.5.cloned.1.call-update) | async-done | bytes 3145744 | tf_op jit(solution)/shard_map/reduce_scatter | solution.py:31
  175.9 8.9 all-gather.9.cloned.1.call-done
  184.8 10.7 %fusion.63 = (f32[1536]{0:T(1024)}, f32[2048,1536]{1,0:T(8,128)}) fusion(bf16[2048,768]{1,0:T(8,128)(2,1)} %all-gather.9.cloned.1.call-done, bf16[1536,768]{1,0:T(8,128)(2,1)} %param.42), kind=kOutput, calls=%fused_computation.148 | convolution fusion | flops 4834982400 | bytes 18094080 | tf_op jit(solution)/shard_map/dot_general | solution.py:39
  195.5 12.8 %copy.42 = f32[2048,1536]{0,1:T(8,128)} copy(f32[2048,1536]{1,0:T(8,128)} %get-tuple-element.548) | data formatting | bytes 25165824 | tf_op jit(solution)/shard_map/dot_general | solution.py:39
  208.4 36.6 %fusion.57 = (f32[2048]{0:T(1024)S(1)}, f32[2048,1536]{0,1:T(8,128)}, f32[2048,1536]{0,1:T(8,128)}, f32[2048,1536]{0,1:T(8,128)}) fusion(f32[1536]{0:T(1024)S(1)} %copy-done.53, bf16[2048,768]{1,0:T(8,128)(2,1)} %all-gather.7.cloned.1.call-done, bf16[768,1536]{1,0:T(8,128)(2,1)S(1)} %copy-done), kind=kOutput, calls=%fused_computation.144 | convolution fusion | flops 5039454208 | bytes 43268096 | tf_op jit(solution)/shard_map/dot_general | solution.py:35
  255.8 10.6 %multiply_reduce_fusion.1 = (f32[1536]{0:T(1024)}, f32[2048]{0:T(1024)S(1)}, f32[2048]{0:T(1024)S(1)}) fusion(f32[2048,1536]{0,1:T(8,128)} %copy.42, f32[2048,1536]{0,1:T(8,128)} %get-tuple-element.522, f32[2048]{0:T(1024)S(1)} %add_rsqrt_fusion, f32[2048]{0:T(1024)S(1)} %broadcast_multiply_fusion.2, f32[1536]{0:T(1024)S(1)} %copy-done.48), kind=kLoop, calls=%fused_computation.43 | loop fusion | flops 25160192 | bytes 25210880 | tf_op jit(solution)/shard_map/reduce_sum | solution.py:158
  270.0 21.3 %fusion.55 = (f32[1536]{0:T(1024)}, bf16[2048,1536]{0,1:T(8,128)(2,1)S(1)}, bf16[2048,1536]{0,1:T(8,128)(2,1)}) fusion(f32[2048,1536]{0,1:T(8,128)} %get-tuple-element.523, f32[2048]{0:T(1024)S(1)} %get-tuple-element.549, f32[2048,1536]{0,1:T(8,128)} %get-tuple-element.522, f32[2048]{0:T(1024)S(1)} %broadcast_multiply_fusion.2, ...), kind=kLoop, calls=%fused_computation.142 | loop fusion | flops 81787392 | bytes 62971904 | tf_op jit(solution)/shard_map/reduce_sum | solution.py:162
  294.0 7.0 fusion.44
  302.7 10.0 fusion.66
  320.7 14.1 %reduce-scatter.7.cloned.1.call-done = f32[1024,768]{1,0:T(8,128)} async-done(((f32[2048,768]{1,0:T(8,128)}), f32[1024,768]{1,0:T(8,128)}) %reduce-scatter.7.cloned.1.call-update) | async-done | bytes 3145744 | tf_op jit(solution)/shard_map/reduce_scatter | solution.py:31
  343.6 14.2 %all-gather.11.cloned.1.call-done = bf16[2048,768]{1,0:T(8,128)(2,1)} async-done(((bf16[1024,768]{1,0:T(8,128)(2,1)}), bf16[2048,768]{1,0:T(8,128)(2,1)}) %all-gather.11.cloned.1.call-update) | async-done | bytes 3145744 | tf_op jit(solution)/shard_map/all_gather | solution.py:27
  357.8 7.3 multiply_reduce_fusion.6
  374.5 224.9 %while.47 = (s32[]{:T(128)}, f32[2,1024,384]{2,1,0:T(8,128)}, bf16[2,1024,384]{1,2,0:T(8,128)(2,1)}, f32[2,1024,384]{1,2,0:T(8,128)}, s32[2]{0:T(128)}, /*index=...) while((s32[]{:T(128)}, f32[2,1024,384]{2,1,0:T(8,128)}, ...), condition=%wide.region_33.34_spmd, body=%wide.region_29.33_spmd.sunk | while | flops 2063661568 | bytes 200372720 | solution.py:235
  382.7 99.2 %while.48 = (s32[]{:T(128)}, f32[1024,6,64]{0,2,1:T(8,128)}, f32[1024,6,64]{0,2,1:T(8,128)}, f32[2,512,384]{2,1,0:T(8,128)}, s32[2]{0:T(128)S(1)}, /*index=5*/s3...) while((s32[]{:T(128)}, f32[1024,6,64]{0,2,1:T(8,128)}, ...), condition=%wide.region_32.32_spmd.clone, body=%wide.region_30.31_spmd.clone.sunk | while | flops 2063661568 | bytes 181496816 | solution.py:226
  394.2 11.4 %multiply_reduce_fusion.13 = (f32[6,512]{1,0:T(8,128)S(1)}, f32[6,512,1024]{2,1,0:T(8,128)}) fusion(f32[6,512,1024]{2,1,0:T(8,128)} %fusion.137, f32[6,512]{1,0:T(8,128)S(1)} %dynamic-slice_bitcast_fusion.2, pred[512,1024]{1,0:T(8,128)(4,1)S(1)} %fusion.138, bf16[512,6,64]{0,2,1:T(8,128)(2,1)S(1)} %bitcast.181, ...), kind=kOutput, calls=%fused_computation.18.clone.1 | convolution fusion | flops 418378752 | bytes 26894336 | tf_op jit(solution)/shard_map/while/body/eval_jaxpr/while/body/eval_jaxpr/qhd,khd->hqk/dot_general | solution.py:205
  406.8 6.9 multiply_convert_fusion.3
  424.1 7.7 bitcast_add_fusion.5
  443.3 11.4 %multiply_reduce_fusion.13 = (f32[6,512]{1,0:T(8,128)S(1)}, f32[6,512,1024]{2,1,0:T(8,128)}) fusion(f32[6,512,1024]{2,1,0:T(8,128)} %fusion.137, f32[6,512]{1,0:T(8,128)S(1)} %dynamic-slice_bitcast_fusion.2, pred[512,1024]{1,0:T(8,128)(4,1)S(1)} %fusion.138, bf16[512,6,64]{0,2,1:T(8,128)(2,1)S(1)} %bitcast.181, ...), kind=kOutput, calls=%fused_computation.18.clone.1 | convolution fusion | flops 418378752 | bytes 26894336 | tf_op jit(solution)/shard_map/while/body/eval_jaxpr/while/body/eval_jaxpr/qhd,khd->hqk/dot_general | solution.py:205
  473.7 8.2 bitcast_add_fusion.5
  495.1 99.2 %while.48 = (s32[]{:T(128)}, f32[1024,6,64]{0,2,1:T(8,128)}, f32[1024,6,64]{0,2,1:T(8,128)}, f32[2,512,384]{2,1,0:T(8,128)}, s32[2]{0:T(128)S(1)}, /*index=5*/s3...) while((s32[]{:T(128)}, f32[1024,6,64]{0,2,1:T(8,128)}, ...), condition=%wide.region_32.32_spmd.clone, body=%wide.region_30.31_spmd.clone.sunk | while | flops 2063661568 | bytes 181496816 | solution.py:226
  506.6 11.4 %multiply_reduce_fusion.13 = (f32[6,512]{1,0:T(8,128)S(1)}, f32[6,512,1024]{2,1,0:T(8,128)}) fusion(f32[6,512,1024]{2,1,0:T(8,128)} %fusion.137, f32[6,512]{1,0:T(8,128)S(1)} %dynamic-slice_bitcast_fusion.2, pred[512,1024]{1,0:T(8,128)(4,1)S(1)} %fusion.138, bf16[512,6,64]{0,2,1:T(8,128)(2,1)S(1)} %bitcast.181, ...), kind=kOutput, calls=%fused_computation.18.clone.1 | convolution fusion | flops 418378752 | bytes 26894336 | tf_op jit(solution)/shard_map/while/body/eval_jaxpr/while/body/eval_jaxpr/qhd,khd->hqk/dot_general | solution.py:205
  536.5 7.7 bitcast_add_fusion.5
  555.7 11.4 %multiply_reduce_fusion.13 = (f32[6,512]{1,0:T(8,128)S(1)}, f32[6,512,1024]{2,1,0:T(8,128)}) fusion(f32[6,512,1024]{2,1,0:T(8,128)} %fusion.137, f32[6,512]{1,0:T(8,128)S(1)} %dynamic-slice_bitcast_fusion.2, pred[512,1024]{1,0:T(8,128)(4,1)S(1)} %fusion.138, bf16[512,6,64]{0,2,1:T(8,128)(2,1)S(1)} %bitcast.181, ...), kind=kOutput, calls=%fused_computation.18.clone.1 | convolution fusion | flops 418378752 | bytes 26894336 | tf_op jit(solution)/shard_map/while/body/eval_jaxpr/while/body/eval_jaxpr/qhd,khd->hqk/dot_general | solution.py:205
  586.1 8.2 bitcast_add_fusion.5
  608.6 9.5 convolution_bitcast_fusion
  618.2 9.7 fusion.42
  627.9 9.9 fusion.68
  648.4 82.5 %all-reduce.1 = (f32[2,384]{1,0:T(2,128)}, f32[384]{0:T(512)}, f32[384]{0:T(512)}, f32[1536]{0:T(1024)}, f32[1536]{0:T(1024)}, /*index=5*/f32[1536]{0:T(1024)}) all-reduce(f32[2,384]{1,0:T(2,128)S(1)} %pad_maximum_fusion.3, f32[384]{0:T(512)S(1)} %copy-done.64, f32[384]{0:T(512)S(1)} %copy-done.65, ...), channel_id=1, replica_groups=mesh['dp'=16,'tensor'=2] {'dp'}, use_global_device_ids=true, to_apply=%region_44.45 | all-reduce | flops 6144 | bytes 49152 | tf_op jit(solution)/shard_map/psum | solution.py:260
  739.1 40.0 %all-reduce = (f32[768]{0:T(1024)}, f32[768]{0:T(1024)}, f32[768]{0:T(1024)}, f32[768]{0:T(1024)}, f32[768]{0:T(1024)}, /*index=5*/f32[768]{0:T(1024)}) all-reduce(f32[768]{0:T(1024)S(1)} %get-tuple-element.420, f32[768]{0:T(1024)S(1)} %get-tuple-element.425, ...), channel_id=1, replica_groups=mesh['dp'=16,'tensor'=2] {'dp','tensor'}, use_global_device_ids=true, to_apply=%region_38.39 | all-reduce | flops 4608 | bytes 36864 | tf_op jit(solution)/shard_map/psum | solution.py:276
  779.1 264.0 %all-reduce.7.cloned.1.call-done = (f32[768,3,384]{2,0,1:T(8,128)}, f32[384,768]{1,0:T(8,128)}, f32[768,1536]{1,0:T(8,128)}, f32[1536,768]{1,0:T(8,128)}) async-done(((f32[768,3,384]{2,0,1:T(8,128)}, f32[384,768]{1,0:T(8,128)}, f32[768,1536]{1,0:T(8,128)}, f32[1536,768]{1,0:T(8,128)}), (f32[768,3,384]{2,0,1:T(8,128)}, f32[384,768]{1,0:T(8,128)}, f32[768,1536]{1,0:T(8,128)}, ...) | async-done | bytes 14155792 | tf_op jit(solution)/shard_map/psum | solution.py:260
  (413 shorter events, 340.2 us)
Async XLA Ops:
  7.2 201.2 %copy-start = (bf16[768,1536]{1,0:T(8,128)(2,1)S(1)}, bf16[768,1536]{1,0:T(8,128)(2,1)}, u32[]{:S(2)}) copy-start(bf16[768,1536]{1,0:T(8,128)(2,1)} %param.38) | copy-start | bytes 7077892
  7.2 22.0 %all-gather.5.cloned.1.call-start = ((), (), s32[]{:S(2)}) async-start(), calls=%async_computation.4 | async-start | bytes 4718592 | tf_op jit(solution)/shard_map/all_gather | solution.py:27
  14.2 154.9 %reduce-scatter.5.cloned.1.call-start = ((), (), s32[]{:S(2)}) async-start(), calls=%async_computation.5 | async-start | bytes 9437184 | tf_op jit(solution)/shard_map/reduce_scatter | solution.py:31
  153.7 15.4 %copy-start.59 = (f32[768]{0:T(1024)S(1)}, f32[768]{0:T(1024)}, u32[]{:S(2)}) copy-start(f32[768]{0:T(1024)} %param.35) | copy-start | bytes 9220
  153.7 31.1 %all-gather.9.cloned.1.call-start = ((), (), s32[]{:S(2)}) async-start(), calls=%async_computation.8 | async-start | bytes 4718592 | tf_op jit(solution)/shard_map/all_gather | solution.py:27
  154.4 53.9 %all-gather.7.cloned.1.call-start = ((), (), s32[]{:S(2)}) async-start(), calls=%async_computation.6 | async-start | bytes 4718592 | tf_op jit(solution)/shard_map/all_gather | solution.py:27
  175.9 140.7 %reduce-scatter.9.cloned.1.call-start = ((), (), s32[]{:S(2)}) async-start(), calls=%async_computation.9 | async-start | bytes 9437184 | tf_op jit(solution)/shard_map/reduce_scatter | solution.py:31
  195.5 12.8 %copy-start.53 = (f32[1536]{0:T(1024)S(1)}, f32[1536]{0:T(1024)}, u32[]{:S(2)}) copy-start(f32[1536]{0:T(1024)} %param.39) | copy-start | bytes 18436
  255.8 14.2 %copy-start.54 = (f32[1536]{0:T(1024)S(1)}, f32[1536]{0:T(1024)}, u32[]{:S(2)}) copy-start(f32[1536]{0:T(1024)} %param.41) | copy-start | bytes 18436
  301.1 33.7 %reduce-scatter.7.cloned.1.call-start = ((), (), s32[]{:S(2)}) async-start(), calls=%async_computation.7 | async-start | bytes 9437184 | tf_op jit(solution)/shard_map/reduce_scatter | solution.py:31
  312.8 22.0 %copy-start.61 = (f32[768]{0:T(1024)S(1)}, f32[768]{0:T(1024)}, u32[]{:S(2)}) copy-start(f32[768]{0:T(1024)} %param.43) | copy-start | bytes 9220
  312.8 45.0 %all-gather.11.cloned.1.call-start = ((), (), s32[]{:S(2)}) async-start(), calls=%async_computation.10 | async-start | bytes 4718592 | tf_op jit(solution)/shard_map/all_gather | solution.py:27
  320.7 21.1 %copy-start.13 = (bf16[1024,768]{1,0:T(8,128)(2,1)S(1)}, bf16[1024,768]{1,0:T(8,128)(2,1)}, u32[]{:S(2)}) copy-start(bf16[1024,768]{1,0:T(8,128)(2,1)} %param.26) | copy-start | bytes 4718596
  341.9 16.0 %copy-start.25 = (bf16[384,768]{1,0:T(8,128)(2,1)S(1)}, bf16[384,768]{1,0:T(8,128)(2,1)}, u32[]{:S(2)}) copy-start(bf16[384,768]{1,0:T(8,128)(2,1)} %param.34) | copy-start | bytes 1769476
  341.9 16.0 %copy-start.29 = (f32[2048]{0:T(1024)S(1)}, f32[2048]{0:T(1024)}, u32[]{:S(2)}) copy-start(f32[2048]{0:T(1024)} %copy-done.28) | copy-start | bytes 24580
  341.9 16.0 %copy-start.33 = (f32[2048]{0:T(1024)S(1)}, f32[2048]{0:T(1024)}, u32[]{:S(2)}) copy-start(f32[2048]{0:T(1024)} %copy-done.32) | copy-start | bytes 24580
  341.9 16.0 %copy-start.56 = (f32[384]{0:T(512)S(1)}, f32[384]{0:T(512)}, u32[]{:S(2)}) copy-start(f32[384]{0:T(512)} %param.32) | copy-start | bytes 4612
  343.5 387.4 %reduce-scatter.11.cloned.1.call-start = ((), (), s32[]{:S(2)}) async-start(), calls=%async_computation.11 | async-start | bytes 9437184 | tf_op jit(solution)/shard_map/reduce_scatter | solution.py:31
  382.7 11.4 %copy-start.3 = (bf16[1024,6,64]{0,2,1:T(8,128)(2,1)}, bf16[1024,6,64]{0,2,1:T(8,128)(2,1)S(1)}, u32[]{:S(2)}) copy-start(bf16[1024,6,64]{0,2,1:T(8,128)(2,1)S(1)} %get-tuple-element.860) | copy-start | bytes 2359300 | tf_op jit(solution)/shard_map/while/body/eval_jaxpr/while
  394.2 12.6 %slice-start.2 = ((s8[12582912]{0:T(1024)(128)(4,1)}), s8[4194304]{0:T(1024)(128)(4,1)S(1)}, s32[]{:S(2)}) async-start(s8[12582912]{0:T(1024)(128)(4,1)} %bitcast.173), calls=%async_computation.15 | async-start | bytes 8388608 | tf_op jit(solution)/shard_map/while/body/eval_jaxpr/while
  443.3 12.6 %slice-start.2 = ((s8[12582912]{0:T(1024)(128)(4,1)}), s8[4194304]{0:T(1024)(128)(4,1)S(1)}, s32[]{:S(2)}) async-start(s8[12582912]{0:T(1024)(128)(4,1)} %bitcast.173), calls=%async_computation.15 | async-start | bytes 8388608 | tf_op jit(solution)/shard_map/while/body/eval_jaxpr/while
  495.1 11.4 %copy-start.3 = (bf16[1024,6,64]{0,2,1:T(8,128)(2,1)}, bf16[1024,6,64]{0,2,1:T(8,128)(2,1)S(1)}, u32[]{:S(2)}) copy-start(bf16[1024,6,64]{0,2,1:T(8,128)(2,1)S(1)} %get-tuple-element.860) | copy-start | bytes 2359300 | tf_op jit(solution)/shard_map/while/body/eval_jaxpr/while
  506.5 11.4 %slice-start = ((s8[12582912]{0:T(1024)(128)(4,1)}), s8[4194304]{0:T(1024)(128)(4,1)S(1)}, s32[]{:S(2)}) async-start(s8[12582912]{0:T(1024)(128)(4,1)} %bitcast.173), calls=%async_computation.13 | async-start | bytes 8388608 | tf_op jit(solution)/shard_map/while/body/eval_jaxpr/while
  506.5 12.6 %slice-start.2 = ((s8[12582912]{0:T(1024)(128)(4,1)}), s8[4194304]{0:T(1024)(128)(4,1)S(1)}, s32[]{:S(2)}) async-start(s8[12582912]{0:T(1024)(128)(4,1)} %bitcast.173), calls=%async_computation.15 | async-start | bytes 8388608 | tf_op jit(solution)/shard_map/while/body/eval_jaxpr/while
  555.6 11.4 %slice-start = ((s8[12582912]{0:T(1024)(128)(4,1)}), s8[4194304]{0:T(1024)(128)(4,1)S(1)}, s32[]{:S(2)}) async-start(s8[12582912]{0:T(1024)(128)(4,1)} %bitcast.173), calls=%async_computation.13 | async-start | bytes 8388608 | tf_op jit(solution)/shard_map/while/body/eval_jaxpr/while
  555.7 12.6 %slice-start.2 = ((s8[12582912]{0:T(1024)(128)(4,1)}), s8[4194304]{0:T(1024)(128)(4,1)S(1)}, s32[]{:S(2)}) async-start(s8[12582912]{0:T(1024)(128)(4,1)} %bitcast.173), calls=%async_computation.15 | async-start | bytes 8388608 | tf_op jit(solution)/shard_map/while/body/eval_jaxpr/while
  618.1 425.0 %all-reduce.7.cloned.1.call-start = ((), (), s32[]{:S(2)}) async-start(), calls=%async_computation.12 | async-start | bytes 28311552 | tf_op jit(solution)/shard_map/psum | solution.py:260
  647.7 83.2 %copy-start.7 = (bf16[1024,768]{1,0:T(8,128)(2,1)S(1)}, bf16[1024,768]{1,0:T(8,128)(2,1)}, u32[]{:S(2)}) copy-start(bf16[1024,768]{1,0:T(8,128)(2,1)} %param.25) | copy-start | bytes 4718596
  647.7 83.2 %copy-start.27 = (f32[1024]{0:T(1024)S(1)}, f32[1024]{0:T(1024)}, u32[]{:S(2)}) copy-start(f32[1024]{0:T(1024)} %copy-done.26) | copy-start | bytes 12292
  647.7 83.2 %copy-start.35 = (f32[768]{0:T(1024)S(1)}, f32[768]{0:T(1024)}, u32[]{:S(2)}) copy-start(f32[768]{0:T(1024)} %param.28) | copy-start | bytes 9220
  647.8 86.1 %copy-start.41 = (f32[1024]{0:T(1024)S(1)}, f32[1024]{0:T(1024)}, u32[]{:S(2)}) copy-start(f32[1024]{0:T(1024)} %copy-done.40) | copy-start | bytes 12292
  647.8 86.2 %copy-start.37 = (f32[1024]{0:T(1024)S(1)}, f32[1024]{0:T(1024)}, u32[]{:S(2)}) copy-start(f32[1024]{0:T(1024)} %copy-done.36) | copy-start | bytes 12292
  (77 other events, 367.0 us)
Sparse Core Ops, SparseCore 0:
  14.3 14.8 all-gather.4
  153.8 15.1 reduce-scatter.4
  170.6 14.1 all-gather.8
  186.8 13.2 all-gather.6
  301.2 15.3 reduce-scatter.8
  318.7 16.0 reduce-scatter.6
  343.6 14.1 all-gather.10
  618.2 15.2 reduce-scatter.10
  647.9 395.1 all-reduce.6
where the time goes:
time: 1070 us; the launch traced here: 1060 us
  waiting for transfers between devices  335 us (31%)
  matrix products  286 us (27%)
  blocking collectives  140 us (13%)
  other arithmetic  138 us (13%)
  local copies, waits for them, and re-layouts  124 us (12%)
  loops' own time  23.1 us (2%)
  between operations  14.7 us (1%)
    psum x1, waiting for transfers between devices, body(): lax.psum((grad_qkv_weight, grad_qv_bias, grad_sub_gain, grad_sub_bias, gr...  264 us
    psum x1, blocking collectives, body(): lax.psum((grad_qkv_weight, grad_qv_bias, grad_sub_gain, grad_sub_bias, gr...  82.5 us
    dot_general x3, matrix products, right_product(): return jnp.dot(left_rows, weight, preferred_element_type=jnp.float32)  51.1 us
    dot_general x4, matrix products, one_block(): jnp.einsum('qhd,khd->hqk', out_grad, value_heads, preferred_element_type=...  45.5 us
    psum x1, blocking collectives, body(): lax.psum((grad_pre_gain, grad_pre_bias, grad_out_bias, grad_ffn_gain, gra...  40 us
    dot_general x8, matrix products, masked_scores(): jnp.einsum('qhd,khd->hqk', query_heads, key_heads, preferred_element_type...  39.6 us
    all_gather x4, waiting for transfers between devices, gather_rows(): return lax.all_gather(values, 'tensor', axis=0, tiled=True)  38 us
    dot_general x4, matrix products, back_product(): lax.dot_general(left_rows, weight, (((1,), (1,)), ((), ())), preferred_el...  34.5 us
  transfers between devices with their start and end apart: 9, of which 7 were waited for; matrix products, arithmetic and copies ran while one was open for 7% of the time, Pallas kernels for 0%

commit v1 on v0

v1 whole, which is shorter than its diff:
```python
import functools
import jax
import jax.numpy as jnp
from jax import lax
from jax.sharding import PartitionSpec as P
from jax.experimental import pallas as pl
from jax.experimental.pallas import tpu as pltpu

D = 768
HEAD_DIM = 64
PREFIX_MAX = 512
EPS = 1e-05
F32 = jnp.float32
BF16 = jnp.bfloat16
QB = 512


def nn(a, b):
    return lax.dot_general(a, b, (((1,), (0,)), ((), ())), preferred_element_type=F32)


def nt(a, b):
    return lax.dot_general(a, b, (((1,), (1,)), ((), ())), preferred_element_type=F32)


def tn(a, b):
    return lax.dot_general(a, b, (((0,), (0,)), ((), ())), preferred_element_type=F32)


def halves(v):
    left = lax.broadcasted_iota(jnp.int32, v.shape, 1) < HEAD_DIM
    zero = jnp.zeros_like(v)
    return jnp.where(left, v, zero), jnp.where(left, zero, v)


def spans(start, length, block):
    last = min(length, max(start + block, PREFIX_MAX))
    out = []
    if start:
        out.append((0, start, False))
    out.append((start, last, True))
    return out


def masked(scores, key_start, query_start, prefix):
    key_pos = key_start + lax.broadcasted_iota(jnp.int32, scores.shape, 0)
    query_pos = query_start + lax.broadcasted_iota(jnp.int32, scores.shape, 1)
    seen = key_pos <= query_pos
    if key_start < PREFIX_MAX:
        seen = seen | (key_pos < prefix)
    return jnp.where(seen, scores, -1e30)


def attn_fwd_kernel(prefix_ref, q_ref, k_ref, v_ref, o_ref, lse_ref):
    length = q_ref.shape[0]
    prefix = prefix_ref[0]
    keys = halves(k_ref[...])
    value_t = v_ref[...].T
    for start in range(0, length, QB):
        query = q_ref[start : start + QB, :] * jnp.asarray(HEAD_DIM**-0.5, BF16)
        parts = []
        for head in range(2):
            scores = []
            for first, last, mask in spans(start, length, QB):
                s = nt(keys[head][first:last], query)
                scores.append(masked(s, first, start, prefix) if mask else s)
            peak = functools.reduce(jnp.maximum, [jnp.max(s, axis=0, keepdims=True) for s in scores])
            total = jnp.zeros_like(peak)
            mixed = jnp.zeros((HEAD_DIM, QB), F32)
            rows = slice(head * HEAD_DIM, (head + 1) * HEAD_DIM)
            for s, (first, last, _) in zip(scores, spans(start, length, QB)):
                w = jnp.exp(s - peak)
                total = total + jnp.sum(w, axis=0, keepdims=True)
                mixed = mixed + nn(value_t[rows, first:last], w.astype(BF16))
            parts.append(mixed / total)
            lse_ref[0, head : head + 1, start : start + QB] = peak + jnp.log(total)
        o_ref[start : start + QB, :] = jnp.concatenate(parts, axis=0).T


def attn_fwd(prefix, qkv):
    length = qkv.shape[0]
    pairs = D // 128
    col = lambda c: pl.BlockSpec((length, 128), lambda i, c=c: (0, c * pairs + i))
    return pl.pallas_call(
        attn_fwd_kernel,
        grid=(pairs,),
        in_specs=[pl.BlockSpec(memory_space=pltpu.SMEM), col(0), col(1), col(2)],
        out_specs=[
            pl.BlockSpec((length, 128), lambda i: (0, i)),
            pl.BlockSpec((1, 8, length), lambda i: (i, 0, 0)),
        ],
        out_shape=[
            jax.ShapeDtypeStruct((length, D), F32),
            jax.ShapeDtypeStruct((pairs, 8, length), F32),
        ],
        name="attn_fwd",
    )(prefix, qkv, qkv, qkv)


def attn_bwd_kernel(prefix_ref, q_ref, k_ref, v_ref, o_ref, g_ref, lse_ref, dq_ref, dk_ref, dv_ref, bias_ref):
    length = q_ref.shape[0]
    prefix = prefix_ref[0]
    scale = HEAD_DIM**-0.5
    keys = halves(k_ref[...])
    values = halves(v_ref[...])
    key_t = k_ref[...].T
    delta_t = (o_ref[...] * g_ref[...].astype(F32)).T
    dk = [jnp.zeros((b - a, 128), F32) for a, b in zip(range(0, length, QB), range(QB, length + 1, QB))]
    dv = list(dk)
    qsum = jnp.zeros((8, 128), F32)
    for start in range(0, length, QB):
        cols = slice(start, start + QB)
        query = q_ref[cols, :] * jnp.asarray(scale, BF16)
        query_half = halves(query)
        grad = g_ref[cols, :]
        grad_half = halves(grad)
        parts = []
        for head in range(2):
            rows = slice(head * HEAD_DIM, (head + 1) * HEAD_DIM)
            lse = lse_ref[0, head : head + 1, cols]
            delta = jnp.sum(delta_t[rows, cols], axis=0, keepdims=True)
            dq = jnp.zeros((HEAD_DIM, QB), F32)
            for first in range(0, length, QB):
                live = [s for s in spans(start, length, QB) if s[0] <= first < s[1]]
                if not live:
                    continue
                last = first + QB
                s = nt(keys[head][first:last], query)
                if live[0][2]:
                    s = masked(s, first, start, prefix)
                w = jnp.exp(s - lse)
                dp = nt(values[head][first:last], grad)
                ds = (w * (dp - delta)).astype(BF16)
                b = first // QB
                dv[b] = dv[b] + nn(w.astype(BF16), grad_half[head])
                dk[b] = dk[b] + nn(ds, query_half[head])
                dq = dq + nn(key_t[rows, first:last], ds)
            parts.append(dq)
        dq = jnp.concatenate(parts, axis=0).T * scale
        qsum = qsum + jnp.sum(dq.reshape(QB // 8, 8, 128), axis=0)
        dq_ref[cols, :] = dq.astype(BF16)
    vsum = jnp.zeros((8, 128), F32)
    for b in range(length // QB):
        cols = slice(b * QB, (b + 1) * QB)
        dk_ref[cols, :] = dk[b].astype(BF16)
        dv_ref[cols, :] = dv[b].astype(BF16)
        vsum = vsum + jnp.sum(dv[b].reshape(QB // 8, 8, 128), axis=0)
    bias_ref[0:1, :] = jnp.sum(qsum, axis=0, keepdims=True)
    bias_ref[1:2, :] = jnp.sum(vsum, axis=0, keepdims=True)


def attn_bwd(prefix, qkv, attended, grad_attended, lse):
    length = qkv.shape[0]
    pairs = D // 128
    col = lambda c: pl.BlockSpec((length, 128), lambda i, c=c: (0, c * pairs + i))
    one = pl.BlockSpec((length, 128), lambda i: (0, i))
    return pl.pallas_call(
        attn_bwd_kernel,
        grid=(pairs,),
        in_specs=[
            pl.BlockSpec(memory_space=pltpu.SMEM), col(0), col(1), col(2), one, one,
            pl.BlockSpec((1, 8, length), lambda i: (i, 0, 0)),
        ],
        out_specs=[one, one, one, pl.BlockSpec((8, 128), lambda i: (0, i))],
        out_shape=[jax.ShapeDtypeStruct((length, D), BF16)] * 3 + [jax.ShapeDtypeStruct((8, D), F32)],
        name="attn_bwd",
    )(prefix, qkv, qkv, qkv, attended, grad_attended, lse)


def normed(v):
    centre = v - jnp.mean(v, axis=-1, keepdims=True)
    inv = lax.rsqrt(jnp.mean(centre * centre, axis=-1, keepdims=True) + EPS)
    return centre * inv, inv


def normed_back(e, xhat, inv):
    return inv * (e - jnp.mean(e, axis=-1, keepdims=True) - xhat * jnp.mean(e * xhat, axis=-1, keepdims=True))


def colsum(v):
    rows, cols = v.shape
    return jnp.sum(v.reshape(rows // 8, 8, cols), axis=0)


def mid_kernel(
    x_ref, att_ref, g_ref, vec_ref, wide_ref, wo_ref, wu_ref, wd_ref,
    out_ref, n2_ref, n3_ref, n4_ref, gh_ref, gm_ref, gml_ref, ga_ref, svec_ref, swide_ref,
    act_ref, slope_ref,
):
    @pl.when(pl.program_id(0) == 0)
    def _():
        svec_ref[...] = jnp.zeros_like(svec_ref)
        swide_ref[...] = jnp.zeros_like(swide_ref)

    sub_gain, sub_bias, out_bias, ffn_gain, ffn_bias, down_bias = [vec_ref[i : i + 1, :] for i in range(6)]
    up_bias, inner_gain, inner_bias = [wide_ref[i : i + 1, :] for i in range(3)]
    xhat2, inv2 = normed(att_ref[...])
    n2 = (xhat2 * sub_gain + sub_bias).astype(BF16)
    n2_ref[...] = n2
    middle = x_ref[...].astype(F32) + nn(n2, wo_ref[...]) + out_bias
    xhat3, inv3 = normed(middle)
    n3 = (xhat3 * ffn_gain + ffn_bias).astype(BF16)
    n3_ref[...] = n3
    hidden = nn(n3, wu_ref[...]) + up_bias
    half = 0.5 + 0.5 * lax.erf(hidden * (2.0**-0.5))
    act_ref[...] = hidden * half
    slope_ref[...] = half + hidden * (jnp.exp(-0.5 * hidden * hidden) * 0.3989422804014327)
    xhat4, inv4 = normed(act_ref[...])
    n4 = (xhat4 * inner_gain + inner_bias).astype(BF16)
    n4_ref[...] = n4
    act_ref[...] = xhat4
    out_ref[...] = (middle + nn(n4, wd_ref[...]) + down_bias).astype(BF16)
    g = g_ref[...]
    e = nt(g, wd_ref[...])
    xhat4 = act_ref[...]
    swide_ref[1] += colsum(e * xhat4)
    swide_ref[2] += colsum(e)
    gh = normed_back(e * inner_gain, xhat4, inv4) * slope_ref[...]
    swide_ref[0] += colsum(gh)
    ghl = gh.astype(BF16)
    gh_ref[...] = ghl
    gf = g.astype(F32)
    e = nt(ghl, wu_ref[...])
    svec_ref[3] += colsum(e * xhat3)
    svec_ref[4] += colsum(e)
    gm = gf + normed_back(e * ffn_gain, xhat3, inv3)
    svec_ref[2] += colsum(gm)
    svec_ref[5] += colsum(gf)
    gm_ref[...] = gm
    gml = gm.astype(BF16)
    gml_ref[...] = gml
    e = nt(gml, wo_ref[...])
    svec_ref[0] += colsum(e * xhat2)
    svec_ref[1] += colsum(e)
    ga_ref[...] = normed_back(e * sub_gain, xhat2, inv2).astype(BF16)


def middle_stage(x, att, g, vecs, wides, wo, wu, wd, block=256):
    rows = x.shape[0]
    ff = wu.shape[1]
    row = lambda n: pl.BlockSpec((block, n), lambda i: (i, 0))
    whole = lambda s: pl.BlockSpec(s, lambda i: (0,) * len(s), pipeline_mode=pl.Buffered(1))
    sds = jax.ShapeDtypeStruct
    return pl.pallas_call(
        mid_kernel,
        grid=(rows // block,),
        in_specs=[row(D), row(D), row(D), whole(vecs.shape), whole(wides.shape), whole(wo.shape), whole(wu.shape), whole(wd.shape)],
        out_specs=[row(D), row(D), row(D), row(ff), row(ff), row(D), row(D), row(D), whole((6, 8, D)), whole((3, 8, ff))],
        out_shape=[
            sds((rows, D), BF16), sds((rows, D), BF16), sds((rows, D), BF16), sds((rows, ff), BF16), sds((rows, ff), BF16),
            sds((rows, D), F32), sds((rows, D), BF16), sds((rows, D), BF16), sds((6, 8, D), F32), sds((3, 8, ff), F32),
        ],
        scratch_shapes=[pltpu.VMEM((block, ff), F32), pltpu.VMEM((block, ff), F32)],
        compiler_params=pltpu.CompilerParams(vmem_limit_bytes=62 * 2**20),
        name="middle_stage",
    )(x, att, g, vecs, wides, wo, wu, wd)


def layer(tokens, grad_out, prefix, pre_gain, pre_bias, wqkv, q_bias, v_bias, vecs, wides, wo, wu, wd):
    x = tokens.astype(F32)
    xhat1, inv1 = normed(x)
    n1 = (xhat1 * pre_gain + pre_bias).astype(BF16)
    bias = jnp.concatenate([q_bias, jnp.zeros_like(q_bias), v_bias])
    qkv = (nn(n1, wqkv) + bias).astype(BF16)
    attended, lse = attn_fwd(prefix, qkv)
    out, n2, n3, n4, gh, gm, gml, ga, svec, swide = middle_stage(tokens, attended, grad_out, vecs, wides, wo, wu, wd)
    dq, dk, dv, dbias = attn_bwd(prefix, qkv, attended, ga, lse)
    g_down = tn(n4, grad_out)
    g_up = tn(n3, gh)
    g_out = tn(n2, gml)
    gproj = jnp.concatenate([dq, dk, dv], axis=1)
    g_qkv = tn(n1, gproj)
    e = nt(gproj, wqkv)
    g_pre_gain = jnp.sum(e * xhat1, axis=0)
    g_pre_bias = jnp.sum(e, axis=0)
    input_grad = gm + normed_back(e * pre_gain, xhat1, inv1)
    return out, input_grad, g_pre_gain, g_pre_bias, g_qkv, dbias[:2], jnp.sum(svec, 1), jnp.sum(swide, 1), g_out, g_up, g_down


def swap(value):
    return lax.ppermute(value, "tensor", ((0, 1), (1, 0)))


def pair_sum(grad, axis):
    size = grad.shape[axis] // 2
    own = lax.slice_in_dim(grad, 0, size, axis=axis)
    other = lax.slice_in_dim(grad, size, 2 * size, axis=axis)
    return own + swap(other.astype(BF16)).astype(F32)


def body(
    tokens, grad_out, prefix, pre_gain, pre_bias, qkv_weight, qv_bias, sub_gain, sub_bias, out_weight, out_bias,
    ffn_gain, ffn_bias, up_weight, up_bias, inner_gain, inner_bias, down_weight, down_bias,
):
    side = lax.axis_index("tensor")
    local = lax.dynamic_slice_in_dim(prefix, side, 1)
    both = lambda v, axis: jnp.concatenate([v, swap(v)], axis=axis)
    wqkv = both(qkv_weight, 2).reshape(D, 3 * D)
    wo = both(out_weight, 0)
    wu = both(up_weight, 1)
    wd = both(down_weight, 0)
    half, ff_half = D // 2, up_bias.shape[0]
    small = jnp.concatenate([qv_bias.reshape(-1), sub_gain, sub_bias, up_bias, inner_gain, inner_bias])
    far = swap(small)
    cut = lambda start, size: jnp.concatenate([small[start : start + size], far[start : start + size]])
    q_bias, v_bias, sgain, sbias = [cut(i * half, half) for i in range(4)]
    ub, ig, ib = [cut(4 * half + i * ff_half, ff_half) for i in range(3)]
    vecs = jnp.stack([sgain, sbias, out_bias, ffn_gain, ffn_bias, down_bias])
    wides = jnp.stack([ub, ig, ib])
    out, input_grad, g_pre_gain, g_pre_bias, g_qkv, g_qv, g_vec, g_wide, g_out, g_up, g_down = layer(
        tokens, grad_out, local, pre_gain, pre_bias, wqkv, q_bias, v_bias, vecs, wides, wo, wu, wd
    )
    g_qkv = pair_sum(g_qkv.reshape(D, 3, D), 2)
    g_out = pair_sum(g_out, 0)
    g_up = pair_sum(g_up, 1)
    g_down = pair_sum(g_down, 0)
    split = jnp.concatenate([g_qv.reshape(2, 2, half), g_vec[:2].reshape(2, 2, half)])
    split = jnp.concatenate([split.transpose(1, 0, 2).reshape(2, -1), g_wide.reshape(3, 2, ff_half).transpose(1, 0, 2).reshape(2, -1)], axis=1)
    split = split[0] + swap(split[1])
    full = jnp.concatenate([jnp.stack([g_pre_gain, g_pre_bias]), g_vec[2:]])
    g_down, g_up = lax.psum((g_down, g_up), "dp")
    g_qkv, g_out, split = lax.psum((g_qkv, g_out, split), "dp")
    full = lax.psum(full, ("dp", "tensor"))
    r = lambda i: split[i * half : (i + 1) * half]
    w = lambda i: split[4 * half + i * ff_half : 4 * half + (i + 1) * ff_half]
    return (
        out, input_grad, full[0], full[1], g_qkv, jnp.stack([r(0), r(1)]), r(2), r(3), g_out, full[2], full[3], full[4],
        g_up, w(0), w(1), w(2), g_down, full[5],
    )


def solution(mesh):
    rows = P(("dp", "tensor"), None)
    wide, tall, vec, whole = P(None, "tensor"), P("tensor", None), P("tensor"), P()
    cube = P(None, None, "tensor")
    return jax.shard_map(
        body,
        mesh=mesh,
        in_specs=(
            rows, rows, P("dp"), whole, whole, cube, wide, vec, vec, tall, whole, whole, whole, wide, vec, vec, vec, tall, whole,
        ),
        out_specs=(
            rows, rows, whole, whole, cube, wide, vec, vec, tall, whole, whole, whole, wide, vec, vec, vec, tall, whole,
        ),
        check_vma=False,
    )
```

time: 1070 us -> 601 us (0.56)
  matrix products: 286 us -> 35.9 us
  other arithmetic: 138 us -> 32.1 us
  Pallas kernels: 0 us -> 94.4 us
  local copies, waits for them, and re-layouts: 124 us -> 33.8 us
  waiting for transfers between devices: 335 us -> 255 us
  loops' own time: 23.1 us -> 0 us
  blocking collectives: 140 us -> 124 us
    dot_general x40 -> x6, matrix products: 286 us -> 35.9 us  [the longest x4 20.7 us: tn(): lax.dot_general(a, b, (((0,), (0,)), ((), ())), preferred_element_type=F32)]
    pallas_call x0 -> x3, Pallas kernels: none -> 94.4 us  [the longest x1 44.6 us: middle_stage(): pl.pallas_call(mid_kernel, grid=(rows // block,), in_specs=[row(D), row(D...]
    reduce_sum x20 -> x4, other arithmetic: 85.9 us -> 1 us  [the longest x1 0.6 us: normed(): inv = lax.rsqrt(jnp.mean(centre * centre, axis=-1, keepdims=True) + EPS)]
    convert_element_type x10 -> x0, other arithmetic: 40.4 us -> none  [the longest x4 27.4 us: one_block(): score_low = score_grad.astype(jnp.bfloat16)]
    all_gather x4 -> x0, waiting for transfers between devices: 38 us -> none  [gather_rows(): return lax.all_gather(values, 'tensor', axis=0, tiled=True)]
    dynamic_slice x32 -> x1, local copies, waits for them, and re-layouts: 36.5 us -> 0.59 us  [body(): local = lax.dynamic_slice_in_dim(prefix, side, 1)]
    reduce_scatter x4 -> x0, waiting for transfers between devices: 32 us -> none  [scatter_rows(): lax.psum_scatter(project(left_rows), 'tensor', scatter_dimension=0, tiled...]
    dynamic_update_slice x16 -> x0, local copies, waits for them, and re-layouts: 23.2 us -> none  [the longest x4 10 us: body(): lax.map(backward_seq, jnp.arange(seq_count, dtype=jnp.int32))]
  transfers between devices with their start and end apart: 9 -> 11, of which waited for: 7 -> 2; matrix products, arithmetic and copies ran while one was open for 7% -> 10% of each run, Pallas kernels for 0% -> 3%
where the time goes in v1:
time: 601 us; the launch traced here: 594 us
  waiting for transfers between devices  255 us (42%)
  blocking collectives  124 us (21%)
  Pallas kernels  94.4 us (16%)
  matrix products  35.9 us (6%)
  local copies, waits for them, and re-layouts  33.8 us (6%)
  other arithmetic  32.1 us (5%)
  between operations  15.1 us (3%)
    psum x1, waiting for transfers between devices, body(): g_qkv, g_out, split = lax.psum((g_qkv, g_out, split), 'dp')  254 us
    psum x1, blocking collectives, body(): g_qkv, g_out, split = lax.psum((g_qkv, g_out, split), 'dp')  78.4 us
    psum x1, blocking collectives, body(): full = lax.psum(full, ('dp', 'tensor'))  46.1 us
    pallas_call x1, Pallas kernels, middle_stage(): pl.pallas_call(mid_kernel, grid=(rows // block,), in_specs=[row(D), row(D...  44.6 us
    pallas_call x1, Pallas kernels, attn_bwd(): pl.pallas_call(attn_bwd_kernel, grid=(pairs,), in_specs=[pl.BlockSpec(mem...  29.8 us
    unnamed x76, local copies, waits for them, and re-layouts  27.4 us
    dot_general x4, matrix products, tn(): lax.dot_general(a, b, (((0,), (0,)), ((), ())), preferred_element_type=F32)  20.7 us
    pallas_call x1, Pallas kernels, attn_fwd(): pl.pallas_call(attn_fwd_kernel, grid=(pairs,), in_specs=[pl.BlockSpec(mem...  20 us
  transfers between devices with their start and end apart: 11, of which 2 were waited for; matrix products, arithmetic and copies ran while one was open for 10% of the time, Pallas kernels for 3%

profile of v1, /device:TPU:0, one launch (start us, length us, event | category | flops | bytes accessed | tf_op | source)
XLA Modules:
  0.0 594.0 jit_solution(12402438684603895545)
XLA Ops:
  12.3 2.6 copy.40
  19.1 2.3 pad_maximum_fusion.3.wo_ref
  21.4 1.7 pad_maximum_fusion.2
  23.1 1.8 copy-done.2
  24.9 5.9 add_convert_fusion.q_ref.k_ref.v_ref
  30.8 20.0 %attn_fwd.1 = (f32[1024,768]{1,0:T(8,128)}, f32[6,8,1024]{2,1,0:T(8,128)}) custom-call(s32[1]{0:T(128)} %dynamic_slice.3.prefix_ref, bf16[1024,2304]{1,0:T(8,128)(2,1)} %add_convert_fusion.q_ref.k_ref.v_ref, bf16[1024,2304]{1,0:T(8,128)(2,1)} %add_convert_fusion.q_ref.k_ref.v_ref, bf16[1024,2304]{1,0:T(8,128)(2,1)} %add_convert_fusion.q_ref.k_ref.v_ref), custom_call_target="tpu_custom_call" | custom-call | tf_op jit(solution)/shard_map/attn_fwd/pallas_call | solution.py:84
  50.8 4.5 pad_maximum_fusion.wu_ref
  55.3 4.2 pad_maximum_fusion.1.wd_ref
  59.5 44.6 %middle_stage.1 = (bf16[1024,768]{1,0:T(8,128)(2,1)}, bf16[1024,768]{1,0:T(8,128)(2,1)}, bf16[1024,768]{1,0:T(8,128)(2,1)}, bf16[1024,3072]{1,0:T(8,128)(2,1)}, ...) custom-call(bf16[1024,768]{1,0:T(8,128)(2,1)} %x_ref.1, ...), custom_call_target="tpu_custom_call" | custom-call | tf_op jit(solution)/shard_map/middle_stage/pallas_call | solution.py:244
  104.1 29.8 %attn_bwd.1 = (bf16[1024,768]{1,0:T(8,128)(2,1)}, bf16[1024,768]{1,0:T(8,128)(2,1)}, bf16[1024,768]{1,0:T(8,128)(2,1)}, f32[8,768]{1,0:T(8,128)}) custom-call(s32[1]{0:T(128)} %dynamic_slice.3.prefix_ref, bf16[1024,2304]{1,0:T(8,128)(2,1)} %add_convert_fusion.q_ref.k_ref.v_ref, bf16[1024,2304]{1,0:T(8,128)(2,1)} %add_convert_fusion.q_ref.k_ref.v_ref, ...), custom_call_target="tpu_custom_call" | custom-call | tf_op jit(solution)/shard_map/attn_bwd/pallas_call | solution.py:157
  133.9 1.7 constant_dynamic-update-slice_fusion.4
  136.4 0.9 copy-done.1
  137.3 4.5 fusion.15
  142.2 1.1 copy-done.23
  143.3 5.2 fusion.23
  149.0 0.9 copy-done.7
  149.9 7.7 %fusion.24 = f32[3072,768]{1,0:T(8,128)S(1)} fusion(bf16[1024,3072]{1,0:T(8,128)(2,1)} %get-tuple-element.49, bf16[1024,768]{1,0:T(8,128)(2,1)S(1)} %copy-done.7), kind=kOutput, calls=%fused_computation.76 | convolution fusion | flops 4831838208 | bytes 17301504 | tf_op jit(solution)/shard_map/dot_general | solution.py:27
  157.9 3.3 fusion.22
  161.8 1.6 collective-permute-done.7
  163.4 1.1 slice_add_fusion.3
  164.6 2.2 slice_add_fusion.2
  166.8 4.6 slice_add_fusion.1
  171.5 4.4 slice_add_fusion
  178.3 9.3 %fusion.12 = (f32[768]{0:T(1024)S(1)}, f32[1024]{0:T(1024)S(1)}, f32[1024]{0:T(1024)S(1)}, f32[768]{0:T(1024)S(1)}, f32[1024,768]{1,0:T(8,128)}) fusion(bf16[1024,768]{1,0:T(8,128)(2,1)S(1)} %copy-done.1, f32[1024]{0:T(1024)S(1)} %add_rsqrt_fusion, f32[1024]{0:T(1024)S(1)} %broadcast_multiply_fusion.2, f32[768]{0:T(1024)S(1)} %copy-done.18, ...), kind=kOutput, calls=%fused_computation.24 | convolution fusion | flops 3631739392 | bytes 13001728 | tf_op jit(solution)/shard_map/dot_general | solution.py:23
  187.6 46.1 %psum.42 = f32[6,768]{1,0:T(8,128)S(1)} all-reduce(f32[6,768]{1,0:T(8,128)S(1)} %pad_maximum_fusion.6), channel_id=1, replica_groups=mesh['dp'=16,'tensor'=2] {'dp','tensor'}, use_global_device_ids=true, to_apply=%region_7.0 | all-reduce | flops 4608 | bytes 36864 | tf_op jit(solution)/shard_map/psum | solution.py:323
  233.8 4.6 fusion.11
  239.1 78.4 %psum.44 = f32[6144]{0:T(1024)S(1)} all-reduce(f32[6144]{0:T(1024)S(1)} %add.69), channel_id=1, replica_groups=mesh['dp'=16,'tensor'=2] {'dp'}, use_global_device_ids=true, to_apply=%region_10.0 | all-reduce | flops 6144 | bytes 49152 | tf_op jit(solution)/shard_map/psum | solution.py:322
  319.2 253.5 %all-reduce.3.cloned.1.call-done = (f32[768,3,384]{0,2,1:T(8,128)}, f32[384,768]{1,0:T(8,128)}, f32[768,1536]{1,0:T(8,128)}, f32[1536,768]{1,0:T(8,128)}) async-done(((f32[768,3,384]{0,2,1:T(8,128)}, f32[384,768]{1,0:T(8,128)}, f32[768,1536]{1,0:T(8,128)}, f32[1536,768]{1,0:T(8,128)}), (f32[768,3,384]{0,2,1:T(8,128)}, f32[384,768]{1,0:T(8,128)}, f32[768,1536]{1,0:T(8,128)}, ...) | async-done | bytes 14155792 | tf_op jit(solution)/shard_map/psum | solution.py:322
  572.7 5.2 copy.42
  578.0 1.0 copy.61
  579.0 5.5 copy.62
  584.5 2.2 copy.63
  (139 shorter events, 16.3 us)
Async XLA Ops:
  7.2 8.7 %copy-start.15 = (f32[2,384]{1,0:T(2,128)S(1)}, f32[2,384]{1,0:T(2,128)}, u32[]{:S(2)}) copy-start(f32[2,384]{1,0:T(2,128)} %param.25) | copy-start | bytes 9220
  7.2 8.8 %copy-start = (bf16[1024,768]{1,0:T(8,128)(2,1)S(1)}, bf16[1024,768]{1,0:T(8,128)(2,1)}, u32[]{:S(2)}) copy-start(bf16[1024,768]{1,0:T(8,128)(2,1)} %x_ref.1) | copy-start | bytes 4718596
  7.2 565.5 %all-reduce.3.cloned.1.call-start = ((), (), s32[]{:S(2)}) async-start(), calls=%async_computation | async-start | bytes 28311552 | tf_op jit(solution)/shard_map/psum | solution.py:322
  11.6 5.3 copy-start.19
  11.6 5.4 copy-start.20
  11.6 5.4 copy-start.21
  11.6 5.4 copy-start.22
  11.6 5.4 copy-start.25
  11.6 6.1 %copy-start.16 = (f32[384]{0:T(512)S(1)}, f32[384]{0:T(512)}, u32[]{:S(2)}) copy-start(f32[384]{0:T(512)} %param.26) | copy-start | bytes 4612
  11.6 6.1 %copy-start.17 = (f32[384]{0:T(512)S(1)}, f32[384]{0:T(512)}, u32[]{:S(2)}) copy-start(f32[384]{0:T(512)} %param.27) | copy-start | bytes 4612
  11.6 6.7 %copy-start.12 = (f32[1536]{0:T(1024)S(1)}, f32[1536]{0:T(1024)}, u32[]{:S(2)}) copy-start(f32[1536]{0:T(1024)} %param.35) | copy-start | bytes 18436
  11.6 6.7 %copy-start.13 = (f32[1536]{0:T(1024)S(1)}, f32[1536]{0:T(1024)}, u32[]{:S(2)}) copy-start(f32[1536]{0:T(1024)} %param.33) | copy-start | bytes 18436
  11.6 6.7 %copy-start.14 = (f32[1536]{0:T(1024)S(1)}, f32[1536]{0:T(1024)}, u32[]{:S(2)}) copy-start(f32[1536]{0:T(1024)} %param.34) | copy-start | bytes 18436
  11.7 5.9 collective-permute-start.1
  12.2 6.8 %collective-permute-start.2 = (bf16[384,768]{1,0:T(8,128)(2,1)}, bf16[384,768]{1,0:T(8,128)(2,1)}, u32[]{:S(2)}, u32[]{:S(2)}) collective-permute-start(bf16[384,768]{1,0:T(8,128)(2,1)} %param.28), channel_id=1, source_target_pairs={{0,1},{1,0},{2,3},{3,2},{4,5},{5,4},{6,7},{7,6},{8,9},{9,8},{10,11... | collective-permute-start | bytes 1769480 | tf_op jit(solution)/shard_map/ppermute | solution.py:281
  14.9 6.5 %collective-permute-start = (bf16[768,3,384]{0,2,1:T(8,128)(2,1)S(1)}, bf16[768,3,384]{0,2,1:T(8,128)(2,1)}, u32[]{:S(2)}, u32[]{:S(2)}) collective-permute-start(bf16[768,3,384]{0,2,1:T(8,128)(2,1)S(1)} %copy.40), channel_id=1, source_target_pairs={{0,1},{1,0},{2,3},{3,2},{4,5},{5,4},{6,7},{7,6},{8,9},{9,8},{10,11... | collective-permute-start | bytes 5308424 | tf_op jit(solution)/shard_map/ppermute | solution.py:281
  15.4 35.4 %collective-permute-start.3 = (bf16[768,1536]{1,0:T(8,128)(2,1)}, bf16[768,1536]{1,0:T(8,128)(2,1)}, u32[]{:S(2)}, u32[]{:S(2)}) collective-permute-start(bf16[768,1536]{1,0:T(8,128)(2,1)} %param.32), channel_id=1, source_target_pairs={{0,1},{1,0},{2,3},{3,2},{4,5},{5,4},{6,7},{7,6},{8,9},{9,8},{10,11... | collective-permute-start | bytes 7077896 | tf_op jit(solution)/shard_map/ppermute | solution.py:281
  15.5 39.8 %collective-permute-start.4 = (bf16[1536,768]{1,0:T(8,128)(2,1)}, bf16[1536,768]{1,0:T(8,128)(2,1)}, u32[]{:S(2)}, u32[]{:S(2)}) collective-permute-start(bf16[1536,768]{1,0:T(8,128)(2,1)} %param.36), channel_id=1, source_target_pairs={{0,1},{1,0},{2,3},{3,2},{4,5},{5,4},{6,7},{7,6},{8,9},{9,8},{10,11... | collective-permute-start | bytes 7077896 | tf_op jit(solution)/shard_map/ppermute | solution.py:281
  21.4 3.5 copy-start.24
  30.8 20.0 %copy-start.3 = (bf16[768,1536]{1,0:T(8,128)(2,1)S(1)}, bf16[768,1536]{1,0:T(8,128)(2,1)}, u32[]{:S(2)}) copy-start(bf16[768,1536]{1,0:T(8,128)(2,1)} %param.32) | copy-start | bytes 7077892
  50.8 4.6 copy-start.4
  136.2 6.0 %slice-start.2 = ((s8[6291456]{0:T(1024)(128)(4,1)}), s8[4194304]{0:T(1024)(128)(4,1)S(1)}, s32[]{:S(2)}) async-start(s8[6291456]{0:T(1024)(128)(4,1)} %bitcast.36), calls=%async_computation.3 | async-start | bytes 8388608
  137.3 4.6 copy-start.9
  137.3 4.9 slice-start.3
  142.1 22.5 %collective-permute-start.5 = (bf16[768,3,384]{0,2,1:T(8,128)(2,1)S(1)}, bf16[768,3,384]{0,2,1:T(8,128)(2,1)S(1)}, u32[]{:S(2)}, u32[]{:S(2)}) collective-permute-start(bf16[768,3,384]{0,2,1:T(8,128)(2,1)S(1)} %slice.210), channel_id=1, source_target_pairs={{0,1},{1,0},{2,3},{3,2},{4,5},{5,4},{6,7},{7,6},{8,9},{9,8},{10,11... | collective-permute-start | bytes 5308424 | tf_op jit(solution)/shard_map/ppermute | solution.py:281
  148.8 18.0 %collective-permute-start.8 = (bf16[768,1536]{1,0:T(8,128)(2,1)S(1)}, bf16[768,1536]{1,0:T(8,128)(2,1)}, u32[]{:S(2)}, u32[]{:S(2)}) collective-permute-start(bf16[768,1536]{1,0:T(8,128)(2,1)S(1)} %slice.209), channel_id=1, source_target_pairs={{0,1},{1,0},{2,3},{3,2},{4,5},{5,4},{6,7},{7,6},{8,9},{9,8},{10,11... | collective-permute-start | bytes 7077896 | tf_op jit(solution)/shard_map/ppermute | solution.py:281
  157.8 13.7 %collective-permute-start.9 = (bf16[1536,768]{1,0:T(8,128)(2,1)S(1)}, bf16[1536,768]{1,0:T(8,128)(2,1)}, u32[]{:S(2)}, u32[]{:S(2)}) collective-permute-start(bf16[1536,768]{1,0:T(8,128)(2,1)S(1)} %slice.208), channel_id=1, source_target_pairs={{0,1},{1,0},{2,3},{3,2},{4,5},{5,4},{6,7},{7,6},{8,9},{9,8},{10,11... | collective-permute-start | bytes 7077896 | tf_op jit(solution)/shard_map/ppermute | solution.py:281
  161.3 2.1 collective-permute-start.7
  177.8 61.2 %collective-permute-start.6 = (f32[6144]{0:T(1024)S(1)}, f32[6144]{0:T(1024)S(1)}, u32[]{:S(2)}, u32[]{:S(2)}) collective-permute-start(f32[6144]{0:T(1024)S(1)} %bitcast.35), channel_id=1, source_target_pairs={{0,1},{1,0},{2,3},{3,2},{4,5},{5,4},{6,7},{7,6},{8,9},{9,8},{10,11... | collective-permute-start | bytes 73736 | tf_op jit(solution)/shard_map/ppermute | solution.py:281
  572.7 5.3 copy-start.8
  578.0 6.5 %slice-start = ((s8[4718592]{0:T(1024)(128)(4,1)}), s8[4194304]{0:T(1024)(128)(4,1)S(1)}, s32[]{:S(2)}) async-start(s8[4718592]{0:T(1024)(128)(4,1)} %bitcast.23), calls=%async_computation.1 | async-start | bytes 8388608
  579.0 5.5 slice-start.1
  (9 other events, 16.6 us)
Sparse Core Ops, SparseCore 0:
  176.0 396.6 all-reduce.2

commit v2 on v1

--- a/solution.py
+++ b/solution.py
@@ -1,4 +1,6 @@
 import functools
+import math
+
 import jax
 import jax.numpy as jnp
 from jax import lax
@@ -49,6 +51,11 @@
     if key_start < PREFIX_MAX:
         seen = seen | (key_pos < prefix)
     return jnp.where(seen, scores, -1e30)
+
+
+def head_block(i, c):
+    each = D // 256
+    return i // each * 3 * each + c * each + lax.rem(i, each)
 
 
 def attn_fwd_kernel(prefix_ref, q_ref, k_ref, v_ref, o_ref, lse_ref):
@@ -80,7 +87,7 @@
 def attn_fwd(prefix, qkv):
     length = qkv.shape[0]
     pairs = D // 128
-    col = lambda c: pl.BlockSpec((length, 128), lambda i, c=c: (0, c * pairs + i))
+    col = lambda c: pl.BlockSpec((length, 128), lambda i, c=c: (0, head_block(i, c)))
     return pl.pallas_call(
         attn_fwd_kernel,
         grid=(pairs,),
@@ -152,7 +159,7 @@
 def attn_bwd(prefix, qkv, attended, grad_attended, lse):
     length = qkv.shape[0]
     pairs = D // 128
-    col = lambda c: pl.BlockSpec((length, 128), lambda i, c=c: (0, c * pairs + i))
+    col = lambda c: pl.BlockSpec((length, 128), lambda i, c=c: (0, head_block(i, c)))
     one = pl.BlockSpec((length, 128), lambda i: (0, i))
     return pl.pallas_call(
         attn_bwd_kernel,
@@ -256,76 +263,265 @@
     )(x, att, g, vecs, wides, wo, wu, wd)
 
 
-def layer(tokens, grad_out, prefix, pre_gain, pre_bias, wqkv, q_bias, v_bias, vecs, wides, wo, wu, wd):
+def layer(tokens, grad_out, prefix, pre_gain, pre_bias, wqkv, bias, vecs, wides, wo, wu, wd):
     x = tokens.astype(F32)
     xhat1, inv1 = normed(x)
     n1 = (xhat1 * pre_gain + pre_bias).astype(BF16)
-    bias = jnp.concatenate([q_bias, jnp.zeros_like(q_bias), v_bias])
     qkv = (nn(n1, wqkv) + bias).astype(BF16)
     attended, lse = attn_fwd(prefix, qkv)
     out, n2, n3, n4, gh, gm, gml, ga, svec, swide = middle_stage(tokens, attended, grad_out, vecs, wides, wo, wu, wd)
     dq, dk, dv, dbias = attn_bwd(prefix, qkv, attended, ga, lse)
-    g_down = tn(n4, grad_out)
-    g_up = tn(n3, gh)
-    g_out = tn(n2, gml)
-    gproj = jnp.concatenate([dq, dk, dv], axis=1)
-    g_qkv = tn(n1, gproj)
+    g_down = tn(n4, grad_out).astype(BF16)
+    g_up = tn(n3, gh).astype(BF16)
+    g_out = tn(n2, gml).astype(BF16)
+    h = D // 2
+    gproj = jnp.concatenate([v[:, s] for s in (slice(0, h), slice(h, D)) for v in (dq, dk, dv)], axis=1)
+    g_qkv = tn(n1, gproj).astype(BF16)
     e = nt(gproj, wqkv)
-    g_pre_gain = jnp.sum(e * xhat1, axis=0)
-    g_pre_bias = jnp.sum(e, axis=0)
+    g_pre = jnp.stack([jnp.sum(e * xhat1, axis=0), jnp.sum(e, axis=0)])
     input_grad = gm + normed_back(e * pre_gain, xhat1, inv1)
-    return out, input_grad, g_pre_gain, g_pre_bias, g_qkv, dbias[:2], jnp.sum(svec, 1), jnp.sum(swide, 1), g_out, g_up, g_down
+    return out, input_grad, g_pre, g_qkv, dbias, jnp.sum(svec, 1), jnp.sum(swide, 1), g_out, g_up, g_down
+
+
+def grid_of(count):
+    side = 1
+    while 2 * side**3 < count:
+        side += 1
+    return (2 * side, side, side) if 2 * side**3 == count else (count, 1, 1)
+
+
+class Piece:
+    def __init__(self, dims, first, near, far, total, bufs, sems, place):
+        self.dims, self.first, self.near, self.far, self.total = dims, first, near, far, total
+        self.mine, self.pair, self.land, self.part, self.land2, self.part2, self.land3 = bufs
+        self.sems, self.place = sems, place
+        self.count = 0
+        self.flight = []
+
+    def send(self, src, dst, where):
+        copy = pltpu.make_async_remote_copy(
+            src_ref=src, dst_ref=dst, send_sem=self.sems.at[0, self.count], recv_sem=self.sems.at[1, self.count],
+            device_id=where, device_id_type=pl.DeviceIdType.MESH,
+        )
+        self.count += 1
+        copy.start()
+        self.flight.append(copy)
+
+    def settle(self):
+        for copy in self.flight:
+            copy.wait()
+        self.flight = []
+
+    def device(self, axis, shift):
+        at = list(self.place[:3])
+        at[axis] = lax.rem(at[axis] + shift, self.dims[axis])
+        nz, ny, nx = self.dims
+        return at[axis], ((at[0] * ny + at[1]) * nx + at[2], self.place[3])
+
+    def steps(self):
+        z, y, x = self.place[:3]
+        nz, ny, nx = self.dims
+        one, two = (2, 1) if self.first == "x" else (1, 2)
+        pick1 = lambda ref, p: ref.at[:, :, p] if one == 2 else ref.at[:, p]
+        own1, own2 = (x, y) if one == 2 else (y, x)
+
+        def start():
+            local = pltpu.make_async_copy(self.near, self.mine, self.sems.at[0, self.count])
+            self.count += 1
+            local.start()
+            self.send(self.far, self.pair, (self.place[4], 1 - self.place[3]))
+            self.flight.append(local)
+
+        def pair_add():
+            self.settle()
+            def one_row(i, _):
+                self.mine[i] = (self.mine[i].astype(F32) + self.pair[i].astype(F32)).astype(self.mine.dtype)
+                return 0
+            lax.fori_loop(0, nz, one_row, 0)
+            for s in range(1, self.dims[one]):
+                p, dev = self.device(one, s)
+                self.send(pick1(self.mine, p), self.land.at[s - 1], dev)
+
+        def add_one():
+            self.settle()
+            def one_row(i, _):
+                v = (self.mine[i, :, x] if one == 2 else self.mine[i, y]).astype(F32)
+                for s in range(1, self.dims[one]):
+                    v = v + self.land[s - 1, i].astype(F32)
+                self.part[i] = v.astype(self.part.dtype)
+                return 0
+            lax.fori_loop(0, nz, one_row, 0)
+            for s in range(1, self.dims[two]):
+                p, dev = self.device(two, s)
+                self.send(self.part.at[:, p], self.land2.at[s - 1], dev)
+
+        def add_two():
+            self.settle()
+            def one_row(i, _):
+                v = self.part[i, own2].astype(F32)
+                for s in range(1, self.dims[two]):
+                    v = v + self.land2[s - 1, i].astype(F32)
+                self.part2[i] = v.astype(self.part2.dtype)
+                return 0
+            lax.fori_loop(0, nz, one_row, 0)
+            for s in range(1, nz):
+                p, dev = self.device(0, s)
+                self.send(self.part2.at[p], self.land3.at[s - 1], dev)
+
+        def add_three():
+            self.settle()
+            v = self.part2[z].astype(F32)
+            for s in range(1, nz):
+                v = v + self.land3[s - 1].astype(F32)
+            self.total[z, y, x] = v.astype(self.total.dtype)
+            spread(0, self.total.at[z, y, x])
+
+        def spread(axis, ref):
+            for s in range(1, self.dims[axis]):
+                self.send(ref, ref, self.device(axis, s)[1])
+
+        def wide_two():
+            self.settle()
+            spread(two, self.total.at[:, y, x])
+
+        def wide_one():
+            self.settle()
+            spread(one, self.total.at[:, :, x] if one == 2 else self.total.at[:, y])
+
+        return [start, pair_add, add_one, add_two, add_three, wide_two, wide_one, self.settle]
+
+
+def buffers(dims, rows, width, dtype, first):
+    nz, ny, nx = dims
+    na, nb = (nx, ny) if first == "x" else (ny, nx)
+    tail = (rows, width)
+    shapes = [
+        (nz, ny, nx) + tail, (nz, ny, nx) + tail, (max(na - 1, 1), nz, nb) + tail, (nz, nb) + tail,
+        (max(nb - 1, 1), nz) + tail, (nz,) + tail, (max(nz - 1, 1),) + tail,
+    ]
+    copies = 2 + 2 * (na + nb + nz - 3)
+    return [pltpu.VMEM(s, dtype) for s in shapes] + [pltpu.SemaphoreType.DMA((2, copies))]
+
+
+def reduce_kernel(dims, views, firsts, *refs):
+    count = len(firsts)
+    sources = refs[: len(views)]
+    totals = refs[len(views) : len(views) + count]
+    scratch = refs[len(views) + count :]
+    index, side = lax.axis_index("dp"), lax.axis_index("tensor")
+    nz, ny, nx = dims
+    place = (index // (ny * nx), lax.rem(index // nx, ny), lax.rem(index, nx), side, index)
+    barrier = pltpu.get_barrier_semaphore()
+    peers = [(index, 1 - side)]
+    probe = Piece(dims, "x", None, None, None, [None] * 7, None, place)
+    for axis in range(3):
+        for s in range(1, dims[axis]):
+            peers.append(probe.device(axis, s)[1])
+    for peer in peers:
+        pl.semaphore_signal(barrier, inc=1, device_id=peer, device_id_type=pl.DeviceIdType.MESH)
+    pl.semaphore_wait(barrier, len(peers))
+    plans = []
+    at = 0
+    for source, view in zip(sources, views):
+        for near, far in view(source):
+            plans.append(Piece(dims, firsts[at], near, far, totals[at], scratch[8 * at : 8 * at + 7], scratch[8 * at + 7], place).steps())
+            at += 1
+    slots = len(plans[0]) + (count + 1) // 2 - 1
+    for slot in range(slots):
+        for i, plan in enumerate(plans):
+            if 0 <= slot - i // 2 < len(plan):
+                plan[slot - i // 2]()
+
+
+def all_reduce(dims, grads, small):
+    g_down, g_up, g_qkv, g_out = grads
+    nz, ny, nx = dims
+    parts = nz * ny * nx
+    ff = g_down.shape[0] // 2
+    half = ff // 2
+    rows_d, rows_u, rows_o = half // parts, D // parts, D // 2 // parts
+    cut = 640
+    down = g_down.reshape(2, 2, nz, ny, nx, rows_d, D)
+    up = g_up.reshape(nz, ny, nx, rows_u, 2 * ff)
+    qkv = g_qkv.reshape(nz, ny, nx, rows_u, 3 * D)
+    out = g_out.reshape(2, nz, ny, nx, rows_o, D)
+    cols = lambda r, a, n: r.at[:, :, :, :, a : a + n]
+    wide = 3 * D // 2
+    views = [
+        lambda r: [(r.at[0, 0], r.at[1, 0]), (r.at[0, 1], r.at[1, 1])],
+        lambda r: [(cols(r, 0, half), cols(r, ff, half)), (cols(r, half, half), cols(r, ff + half, half))],
+        lambda r: [(cols(r, 0, cut), cols(r, wide, cut)), (cols(r, cut, wide - cut), cols(r, wide + cut, wide - cut))],
+        lambda r: [(r.at[0], r.at[1])],
+        lambda r: [(r.at[0], r.at[1])],
+    ]
+    sizes = [(rows_d, D, BF16)] * 2 + [(rows_u, half, BF16)] * 2 + [(rows_u, cut, BF16), (rows_u, wide - cut, BF16), (rows_o, D, BF16)]
+    sizes.append(small.shape[-2:] + (F32,))
+    firsts = ["x", "y"] * 3 + ["y", "x"]
+    scratch = []
+    for (r, w, t), first in zip(sizes, firsts):
+        scratch += buffers(dims, r, w, t, first)
+    totals = pl.pallas_call(
+        functools.partial(reduce_kernel, dims, views, firsts),
+        in_specs=[pl.BlockSpec(memory_space=pl.ANY)] * 5,
+        out_specs=[pl.BlockSpec(memory_space=pltpu.VMEM)] * len(sizes),
+        out_shape=[jax.ShapeDtypeStruct((nz, ny, nx, r, w), t) for r, w, t in sizes],
+        scratch_shapes=scratch,
+        compiler_params=pltpu.CompilerParams(collective_id=0, has_side_effects=True, vmem_limit_bytes=60 * 2**20),
+        name="all_reduce",
+    )(down, up, qkv, out, small)
+    flat = [t.reshape(-1, t.shape[-1]) for t in totals]
+    return (
+        jnp.concatenate(flat[:2], axis=0).astype(F32),
+        jnp.concatenate(flat[2:4], axis=1).astype(F32),
+        jnp.concatenate(flat[4:6], axis=1).astype(F32),
+        flat[6].astype(F32),
+        flat[7].reshape(-1),
+    )
 
 
 def swap(value):
     return lax.ppermute(value, "tensor", ((0, 1), (1, 0)))
 
 
-def pair_sum(grad, axis):
-    size = grad.shape[axis] // 2
-    own = lax.slice_in_dim(grad, 0, size, axis=axis)
-    other = lax.slice_in_dim(grad, size, 2 * size, axis=axis)
-    return own + swap(other.astype(BF16)).astype(F32)
-
-
 def body(
-    tokens, grad_out, prefix, pre_gain, pre_bias, qkv_weight, qv_bias, sub_gain, sub_bias, out_weight, out_bias,
+    dims, tokens, grad_out, prefix, pre_gain, pre_bias, qkv_weight, qv_bias, sub_gain, sub_bias, out_weight, out_bias,
     ffn_gain, ffn_bias, up_weight, up_bias, inner_gain, inner_bias, down_weight, down_bias,
 ):
     side = lax.axis_index("tensor")
     local = lax.dynamic_slice_in_dim(prefix, side, 1)
     both = lambda v, axis: jnp.concatenate([v, swap(v)], axis=axis)
-    wqkv = both(qkv_weight, 2).reshape(D, 3 * D)
+    half, ff_half = D // 2, up_bias.shape[0]
+    wqkv = both(qkv_weight.reshape(D, 3 * half), 1)
     wo = both(out_weight, 0)
     wu = both(up_weight, 1)
     wd = both(down_weight, 0)
-    half, ff_half = D // 2, up_bias.shape[0]
-    small = jnp.concatenate([qv_bias.reshape(-1), sub_gain, sub_bias, up_bias, inner_gain, inner_bias])
-    far = swap(small)
-    cut = lambda start, size: jnp.concatenate([small[start : start + size], far[start : start + size]])
-    q_bias, v_bias, sgain, sbias = [cut(i * half, half) for i in range(4)]
+    near = jnp.concatenate([qv_bias.reshape(-1), sub_gain, sub_bias, up_bias, inner_gain, inner_bias])
+    far = swap(near)
+    cut = lambda start, size: jnp.concatenate([near[start : start + size], far[start : start + size]])
+    zero = jnp.zeros((half,), F32)
+    bias = jnp.concatenate([p for v in (near, far) for p in (v[:half], zero, v[half : 2 * half])])
+    sgain, sbias = [cut(i * half, half) for i in (2, 3)]
     ub, ig, ib = [cut(4 * half + i * ff_half, ff_half) for i in range(3)]
     vecs = jnp.stack([sgain, sbias, out_bias, ffn_gain, ffn_bias, down_bias])
     wides = jnp.stack([ub, ig, ib])
-    out, input_grad, g_pre_gain, g_pre_bias, g_qkv, g_qv, g_vec, g_wide, g_out, g_up, g_down = layer(
-        tokens, grad_out, local, pre_gain, pre_bias, wqkv, q_bias, v_bias, vecs, wides, wo, wu, wd
+    out, input_grad, g_pre, g_qkv, g_qv, g_vec, g_wide, g_out, g_up, g_down = layer(
+        tokens, grad_out, local, pre_gain, pre_bias, wqkv, bias, vecs, wides, wo, wu, wd
     )
-    g_qkv = pair_sum(g_qkv.reshape(D, 3, D), 2)
-    g_out = pair_sum(g_out, 0)
-    g_up = pair_sum(g_up, 1)
-    g_down = pair_sum(g_down, 0)
-    split = jnp.concatenate([g_qv.reshape(2, 2, half), g_vec[:2].reshape(2, 2, half)])
-    split = jnp.concatenate([split.transpose(1, 0, 2).reshape(2, -1), g_wide.reshape(3, 2, ff_half).transpose(1, 0, 2).reshape(2, -1)], axis=1)
-    split = split[0] + swap(split[1])
-    full = jnp.concatenate([jnp.stack([g_pre_gain, g_pre_bias]), g_vec[2:]])
-    g_down, g_up = lax.psum((g_down, g_up), "dp")
-    g_qkv, g_out, split = lax.psum((g_qkv, g_out, split), "dp")
-    full = lax.psum(full, ("dp", "tensor"))
-    r = lambda i: split[i * half : (i + 1) * half]
-    w = lambda i: split[4 * half + i * ff_half : 4 * half + (i + 1) * ff_half]
+    shared = jnp.concatenate([g_pre.reshape(-1), g_vec[2:].reshape(-1)])
+    rows = -(-(4 * half + 3 * ff_half + 6 * D) // (128 * 8 * math.prod(dims))) * 8
+    pad = jnp.zeros((rows * 128 * math.prod(dims) - (4 * half + 3 * ff_half + 6 * D),), F32)
+    pack = lambda i: jnp.concatenate(
+        [v[j, i * n : (i + 1) * n] for v, m, n in ((g_qv, 2, half), (g_vec, 2, half), (g_wide, 3, ff_half)) for j in range(m)] + [shared, pad]
+    )
+    small = jnp.stack([pack(0), pack(1)]).reshape((2,) + dims + (rows, 128))
+    g_down, g_up, g_qkv, g_out, small = all_reduce(dims, (g_down, g_up, g_qkv, g_out), small)
+    r = lambda i: small[i * half : (i + 1) * half]
+    w = lambda i: small[4 * half + i * ff_half : 4 * half + (i + 1) * ff_half]
+    base = 4 * half + 3 * ff_half
+    f = lambda i: small[base + i * D : base + (i + 1) * D]
     return (
-        out, input_grad, full[0], full[1], g_qkv, jnp.stack([r(0), r(1)]), r(2), r(3), g_out, full[2], full[3], full[4],
-        g_up, w(0), w(1), w(2), g_down, full[5],
+        out, input_grad, f(0), f(1), g_qkv.reshape(D, 3, half), small[: 2 * half].reshape(2, half), r(2), r(3), g_out,
+        f(2), f(3), f(4), g_up, w(0), w(1), w(2), g_down, f(5),
     )
 
 
@@ -334,7 +530,7 @@
     wide, tall, vec, whole = P(None, "tensor"), P("tensor", None), P("tensor"), P()
     cube = P(None, None, "tensor")
     return jax.shard_map(
-        body,
+        functools.partial(body, grid_of(mesh.shape["dp"])),
         mesh=mesh,
         in_specs=(
             rows, rows, P("dp"), whole, whole, cube, wide, vec, vec, tall, whole, whole, whole, wide, vec, vec, vec, tall, whole,

time: 601 us -> 359 us (0.60)
  waiting for transfers between devices: 255 us -> 0.01 us
  Pallas kernels: 94.4 us -> 238 us
  blocking collectives: 124 us -> 0 us
  between operations: 15.1 us -> 1.67 us
  matrix products: 35.9 us -> 42.7 us
  local copies, waits for them, and re-layouts: 33.8 us -> 40 us
    psum x1 -> x0, waiting for transfers between devices: 254 us -> none  [body(): g_qkv, g_out, split = lax.psum((g_qkv, g_out, split), 'dp')]
    pallas_call x0 -> x1, Pallas kernels: none -> 143 us  [all_reduce(): pl.pallas_call(functools.partial(reduce_kernel, dims, views, firsts), in_...]
    psum x2 -> x0, blocking collectives: 124 us -> none  [the longest x1 78.4 us: body(): g_qkv, g_out, split = lax.psum((g_qkv, g_out, split), 'dp')]
    add x5 -> x0, other arithmetic: 12.4 us -> none  [the longest x4 12.4 us: pair_sum(): return own + swap(other.astype(BF16)).astype(F32)]
    convert_element_type x0 -> x3, other arithmetic: none -> 9.51 us  [the longest x1 4.32 us: all_reduce(): jnp.concatenate(flat[:2], axis=0).astype(F32)]
    dot_general x4, matrix products: 20.7 us -> 27.8 us  [tn(): lax.dot_general(a, b, (((0,), (0,)), ((), ())), preferred_element_type=F32)]
    unnamed x76 -> x89, local copies, waits for them, and re-layouts: 27.4 us -> 20.5 us
    concatenate x4 -> x3, other arithmetic: 12.8 us -> 10.9 us  [body(): both = lambda v, axis: jnp.concatenate([v, swap(v)], axis=axis)]
  transfers between devices with their start and end apart: 11 -> 5, of which waited for: 2 -> 0; matrix products, arithmetic and copies ran while one was open for 10% -> 8% of each run, Pallas kernels for 3% -> 6%
where the time goes in v2:
time: 359 us; the launch traced here: 352 us
  Pallas kernels  238 us (66%)
  matrix products  42.7 us (12%)
  local copies, waits for them, and re-layouts  40 us (11%)
  other arithmetic  28.3 us (8%)
    pallas_call x1, Pallas kernels, all_reduce(): pl.pallas_call(functools.partial(reduce_kernel, dims, views, firsts), in_...  143 us
    pallas_call x1, Pallas kernels, middle_stage(): pl.pallas_call(mid_kernel, grid=(rows // block,), in_specs=[row(D), row(D...  44.6 us
    pallas_call x1, Pallas kernels, attn_bwd(): pl.pallas_call(attn_bwd_kernel, grid=(pairs,), in_specs=[pl.BlockSpec(mem...  30 us
    dot_general x4, matrix products, tn(): lax.dot_general(a, b, (((0,), (0,)), ((), ())), preferred_element_type=F32)  27.8 us
    unnamed x89, local copies, waits for them, and re-layouts  20.5 us
    pallas_call x1, Pallas kernels, attn_fwd(): pl.pallas_call(attn_fwd_kernel, grid=(pairs,), in_specs=[pl.BlockSpec(mem...  20 us
    concatenate x3, other arithmetic, body(): both = lambda v, axis: jnp.concatenate([v, swap(v)], axis=axis)  10.9 us
    dot_general x1, matrix products, nt(): lax.dot_general(a, b, (((1,), (1,)), ((), ())), preferred_element_type=F32)  7.56 us
  transfers between devices with their start and end apart: 5, of which 0 were waited for; matrix products, arithmetic and copies ran while one was open for 8% of the time, Pallas kernels for 6%

profile of v2, /device:TPU:0, one launch (start us, length us, event | category | flops | bytes accessed | tf_op | source)
XLA Modules:
  0.0 352.0 jit_solution(3013489677340633019)
XLA Ops:
  4.1 1.3 constant_dynamic-update-slice_fusion.8
  5.4 1.3 constant_dynamic-update-slice_fusion.4
  6.7 1.3 constant_dynamic-update-slice_fusion.22
  8.0 1.3 constant_dynamic-update-slice_fusion.19
  10.0 2.6 copy.37
  24.2 1.4 stack.57.vec_ref
  26.2 2.3 pad_maximum_fusion.6.wo_ref
  28.6 7.4 %add_convert_fusion.q_ref.k_ref.v_ref = bf16[1024,2304]{1,0:T(8,128)(2,1)} fusion(f32[2304]{0:T(1024)} %get-tuple-element.121, bf16[768,1152]{0,1:T(8,128)(2,1)} %collective-permute-done, bf16[768,1152]{0,1:T(8,128)(2,1)S(1)} %bitcast.35, bf16[1024,768]{1,0:T(8,128)(2,1)S(1)} %copy-done, f32[768]{0:T(1024)} %param.23, f32[768]{0:T(1024)} %param.22, ...), kind=kOutput, calls=%fused_computation | convolution fusion | flops 3640393728 | bytes 9853952 | tf_op jit(solution)/shard_map/dot_general | solution.py:21
  36.0 20.0 %attn_fwd.1 = (f32[1024,768]{1,0:T(8,128)}, f32[6,8,1024]{2,1,0:T(8,128)}) custom-call(s32[1]{0:T(128)} %dynamic_slice.3.prefix_ref, bf16[1024,2304]{1,0:T(8,128)(2,1)} %add_convert_fusion.q_ref.k_ref.v_ref, bf16[1024,2304]{1,0:T(8,128)(2,1)} %add_convert_fusion.q_ref.k_ref.v_ref, bf16[1024,2304]{1,0:T(8,128)(2,1)} %add_convert_fusion.q_ref.k_ref.v_ref), custom_call_target="tpu_custom_call" | custom-call | tf_op jit(solution)/shard_map/attn_fwd/pallas_call | solution.py:91
  56.0 4.5 %pad_maximum_fusion.wu_ref = bf16[768,3072]{1,0:T(8,128)(2,1)} fusion(bf16[768,1536]{1,0:T(8,128)(2,1)} %collective-permute-done.3, bf16[768,1536]{1,0:T(8,128)(2,1)S(1)} %copy-done.4), kind=kLoop, calls=%fused_computation.4 | loop fusion | flops 9437184 | bytes 9437184 | tf_op jit(solution)/shard_map/concatenate | solution.py:492
  60.6 4.1 %pad_maximum_fusion.1.wd_ref = bf16[3072,768]{1,0:T(8,128)(2,1)} fusion(bf16[1536,768]{1,0:T(8,128)(2,1)} %collective-permute-done.4, bf16[1536,768]{1,0:T(8,128)(2,1)S(1)} %copy-done.5), kind=kLoop, calls=%fused_computation.5 | loop fusion | flops 9437184 | bytes 9437184 | tf_op jit(solution)/shard_map/concatenate | solution.py:492
  64.6 44.6 %middle_stage.1 = (bf16[1024,768]{1,0:T(8,128)(2,1)}, bf16[1024,768]{1,0:T(8,128)(2,1)}, bf16[1024,768]{1,0:T(8,128)(2,1)}, bf16[1024,3072]{1,0:T(8,128)(2,1)}, ...) custom-call(bf16[1024,768]{1,0:T(8,128)(2,1)} %x_ref.1, ...), custom_call_target="tpu_custom_call" | custom-call | tf_op jit(solution)/shard_map/middle_stage/pallas_call | solution.py:251
  110.3 30.0 %attn_bwd.1 = (bf16[1024,768]{1,0:T(8,128)(2,1)}, bf16[1024,768]{1,0:T(8,128)(2,1)}, bf16[1024,768]{1,0:T(8,128)(2,1)}, f32[8,768]{1,0:T(8,128)}) custom-call(s32[1]{0:T(128)} %dynamic_slice.3.prefix_ref, bf16[1024,2304]{1,0:T(8,128)(2,1)} %add_convert_fusion.q_ref.k_ref.v_ref, bf16[1024,2304]{1,0:T(8,128)(2,1)} %add_convert_fusion.q_ref.k_ref.v_ref, ...), custom_call_target="tpu_custom_call" | custom-call | tf_op jit(solution)/shard_map/attn_bwd/pallas_call | solution.py:164
  141.4 1.4 slice_dynamic-update-slice_fusion.5
  145.5 5.7 %convolution_convert_fusion.2 = bf16[768,2304]{1,0:T(8,128)(2,1)} fusion(bf16[1024,2304]{1,0:T(8,128)(2,1)S(1)} %slice_dynamic-update-slice_fusion, bf16[1024,768]{1,0:T(8,128)(2,1)S(1)} %copy-done.1, f32[768]{0:T(1024)S(1)} %copy-done.27, f32[768]{0:T(1024)S(1)} %copy-done.19, f32[1024]{0:T(1024)S(1)} %add_rsqrt_fusion, f32[1024]{0:T(1024)S(1)} %broadcast_multiply_fusion.2), kind=kOutput, calls=%fused_computation.3 | convolution fusion | flops 3630366720 | bytes 9844736 | tf_op jit(solution)/shard_map/dot_general | solution.py:29
  151.2 7.6 %fusion.12 = (f32[768]{0:T(1024)S(1)}, f32[1024]{0:T(1024)S(1)}, f32[1024]{0:T(1024)S(1)}, f32[768]{0:T(1024)S(1)}, f32[1024,768]{1,0:T(8,128)}) fusion(bf16[1024,768]{1,0:T(8,128)(2,1)S(1)} %copy-done.1, f32[1024]{0:T(1024)S(1)} %add_rsqrt_fusion, f32[1024]{0:T(1024)S(1)} %broadcast_multiply_fusion.2, f32[768]{0:T(1024)S(1)} %copy-done.19, ...), kind=kOutput, calls=%fused_computation.21 | convolution fusion | flops 3638817280 | bytes 13001728 | tf_op jit(solution)/shard_map/dot_general | solution.py:25
  159.1 10.1 %convolution_convert_fusion.1 = bf16[3072,768]{1,0:T(8,128)(2,1)} fusion(bf16[1024,3072]{1,0:T(8,128)(2,1)} %get-tuple-element.50, bf16[1024,768]{1,0:T(8,128)(2,1)S(1)} %copy-done.11), kind=kOutput, calls=%fused_computation.2 | convolution fusion | flops 4834197504 | bytes 12582912 | tf_op jit(solution)/shard_map/dot_general | solution.py:29
  169.8 2.5 convolution_convert_fusion.3
  172.3 9.5 %convolution_convert_fusion = bf16[768,3072]{1,0:T(8,128)(2,1)} fusion(bf16[1024,768]{1,0:T(8,128)(2,1)S(1)} %copy-done.23, bf16[1024,3072]{1,0:T(8,128)(2,1)} %get-tuple-element.52), kind=kOutput, calls=%fused_computation.1 | convolution fusion | flops 4834197504 | bytes 12582912 | tf_op jit(solution)/shard_map/dot_general | solution.py:29
  181.8 143.0 %all_reduce.1 = (bf16[4,2,2,48,768]{4,3,2,1,0:T(8,128)(2,1)}, bf16[4,2,2,48,768]{4,3,2,1,0:T(8,128)(2,1)}, bf16[4,2,2,48,768]{4,3,2,1,0:T(8,128)(2,1)}, bf16[4,2...) custom-call(bf16[2,2,4,2,2,48,768]{6,5,4,3,2,1,0:T(8,128)(2,1)} %bit, ...), custom_call_target="tpu_custom_call" | custom-call | tf_op jit(solution)/shard_map/all_reduce/pallas_call | solution.py:463
  324.8 1.4 fusion.19
  326.2 1.4 fusion.20
  327.6 1.4 fusion.21
  328.9 2.2 copy.38
  331.2 2.3 copy.39
  333.5 1.6 pad_maximum_fusion.5
  335.0 2.6 copy.40
  337.6 2.2 bitcast_convert_fusion
  340.4 4.3 %maximum_convert_fusion.1 = f32[1536,768]{1,0:T(8,128)} fusion(bf16[768,768]{1,0:T(8,128)(2,1)} %bitcast.41, bf16[768,768]{1,0:T(8,128)(2,1)} %bitcast.40), kind=kLoop, calls=%fused_computation.25 | loop fusion | flops 4718592 | bytes 7077888 | tf_op jit(solution)/shard_map/convert_element_type | solution.py:474
  344.7 3.0 maximum_convert_fusion
  347.8 1.5 copy-done.3
  349.3 2.3 fusion.11
  (133 shorter events, 22.3 us)
Async XLA Ops:
  0.7 13.0 %copy-start.18 = (f32[2,384]{1,0:T(2,128)S(1)}, f32[2,384]{1,0:T(2,128)}, u32[]{:S(2)}) copy-start(f32[2,384]{1,0:T(2,128)} %param.25) | copy-start | bytes 9220
  0.7 13.0 %copy-start = (bf16[1024,768]{1,0:T(8,128)(2,1)S(1)}, bf16[1024,768]{1,0:T(8,128)(2,1)}, u32[]{:S(2)}) copy-start(bf16[1024,768]{1,0:T(8,128)(2,1)} %x_ref.1) | copy-start | bytes 4718596
  9.4 5.9 %copy-start.20 = (f32[768]{0:T(1024)S(1)}, f32[768]{0:T(1024)}, u32[]{:S(2)}) copy-start(f32[768]{0:T(1024)} %param.29) | copy-start | bytes 9220
  9.4 6.5 %copy-start.21 = (f32[768]{0:T(1024)S(1)}, f32[768]{0:T(1024)}, u32[]{:S(2)}) copy-start(f32[768]{0:T(1024)} %param.30) | copy-start | bytes 9220
  9.4 7.1 %copy-start.22 = (f32[768]{0:T(1024)S(1)}, f32[768]{0:T(1024)}, u32[]{:S(2)}) copy-start(f32[768]{0:T(1024)} %param.31) | copy-start | bytes 9220
  9.4 16.2 %copy-start.15 = (f32[1536]{0:T(1024)S(1)}, f32[1536]{0:T(1024)}, u32[]{:S(2)}) copy-start(f32[1536]{0:T(1024)} %param.35) | copy-start | bytes 18436
  9.4 16.2 %copy-start.16 = (f32[1536]{0:T(1024)S(1)}, f32[1536]{0:T(1024)}, u32[]{:S(2)}) copy-start(f32[1536]{0:T(1024)} %param.33) | copy-start | bytes 18436
  9.4 16.2 %copy-start.17 = (f32[1536]{0:T(1024)S(1)}, f32[1536]{0:T(1024)}, u32[]{:S(2)}) copy-start(f32[1536]{0:T(1024)} %param.34) | copy-start | bytes 18436
  9.4 10.1 %collective-permute-start.1 = (f32[6144]{0:T(1024)}, f32[6144]{0:T(1024)S(1)}, u32[]{:S(2)}, u32[]{:S(2)}) collective-permute-start(f32[6144]{0:T(1024)} %constant_dynamic-update-slice_fusion.19), channel_id=1, source_target_pairs={{0,1},{1,0},{2,3},{3,2},{4,5},{5,4},{6,7},{7,6},{8,9},{9,8},{10,11... | collective-permute-start | bytes 73736 | tf_op jit(solution)/shard_map/ppermute | solution.py:483
  12.6 16.0 %copy-start.6 = (bf16[768,3,384]{0,2,1:T(8,128)(2,1)}, bf16[768,3,384]{0,2,1:T(8,128)(2,1)S(1)}, u32[]{:S(2)}) copy-start(bf16[768,3,384]{0,2,1:T(8,128)(2,1)S(1)} %copy.37) | copy-start | bytes 5308420
  12.6 16.0 %collective-permute-start = (bf16[768,1152]{0,1:T(8,128)(2,1)S(1)}, bf16[768,1152]{0,1:T(8,128)(2,1)}, u32[]{:S(2)}, u32[]{:S(2)}) collective-permute-start(bf16[768,1152]{0,1:T(8,128)(2,1)S(1)} %bitcast.34), channel_id=1, source_target_pairs={{0,1},{1,0},{2,3},{3,2},{4,5},{5,4},{6,7},{7,6},{8,9},{9,8},{10,11... | collective-permute-start | bytes 5308424 | tf_op jit(solution)/shard_map/ppermute | solution.py:483
  12.7 43.3 %collective-permute-start.3 = (bf16[768,1536]{1,0:T(8,128)(2,1)}, bf16[768,1536]{1,0:T(8,128)(2,1)}, u32[]{:S(2)}, u32[]{:S(2)}) collective-permute-start(bf16[768,1536]{1,0:T(8,128)(2,1)} %param.32), channel_id=1, source_target_pairs={{0,1},{1,0},{2,3},{3,2},{4,5},{5,4},{6,7},{7,6},{8,9},{9,8},{10,11... | collective-permute-start | bytes 7077896 | tf_op jit(solution)/shard_map/ppermute | solution.py:483
  13.2 47.4 %collective-permute-start.4 = (bf16[1536,768]{1,0:T(8,128)(2,1)}, bf16[1536,768]{1,0:T(8,128)(2,1)}, u32[]{:S(2)}, u32[]{:S(2)}) collective-permute-start(bf16[1536,768]{1,0:T(8,128)(2,1)} %param.36), channel_id=1, source_target_pairs={{0,1},{1,0},{2,3},{3,2},{4,5},{5,4},{6,7},{7,6},{8,9},{9,8},{10,11... | collective-permute-start | bytes 7077896 | tf_op jit(solution)/shard_map/ppermute | solution.py:483
  13.2 13.0 %collective-permute-start.2 = (bf16[384,768]{1,0:T(8,128)(2,1)}, bf16[384,768]{1,0:T(8,128)(2,1)}, u32[]{:S(2)}, u32[]{:S(2)}) collective-permute-start(bf16[384,768]{1,0:T(8,128)(2,1)} %param.28), channel_id=1, source_target_pairs={{0,1},{1,0},{2,3},{3,2},{4,5},{5,4},{6,7},{7,6},{8,9},{9,8},{10,11... | collective-permute-start | bytes 1769480 | tf_op jit(solution)/shard_map/ppermute | solution.py:483
  36.0 20.0 %copy-start.4 = (bf16[768,1536]{1,0:T(8,128)(2,1)S(1)}, bf16[768,1536]{1,0:T(8,128)(2,1)}, u32[]{:S(2)}) copy-start(bf16[768,1536]{1,0:T(8,128)(2,1)} %param.32) | copy-start | bytes 7077892
  56.0 4.6 %copy-start.5 = (bf16[1536,768]{1,0:T(8,128)(2,1)S(1)}, bf16[1536,768]{1,0:T(8,128)(2,1)}, u32[]{:S(2)}) copy-start(bf16[1536,768]{1,0:T(8,128)(2,1)} %param.36) | copy-start | bytes 7077892
  110.2 30.9 %copy-start.14 = (f32[3,8,3072]{2,1,0:T(8,128)S(1)}, f32[3,8,3072]{2,1,0:T(8,128)}, u32[]{:S(2)}) copy-start(f32[3,8,3072]{2,1,0:T(8,128)} %get-tuple-element.57) | copy-start | bytes 884740
  140.3 3.8 %copy-start.8 = (bf16[1024,768]{1,0:T(8,128)(2,1)S(1)}, bf16[1024,768]{1,0:T(8,128)(2,1)}, u32[]{:S(2)}) copy-start(bf16[1024,768]{1,0:T(8,128)(2,1)} %get-tuple-element.49) | copy-start | bytes 4718596
  141.3 3.0 copy-start.10
  141.4 3.1 copy-start.9
  144.1 1.4 copy-start.1
  144.1 1.4 copy-start.19
  144.1 1.4 copy-start.27
  145.5 5.7 %copy-start.7 = (bf16[768,3,384]{0,2,1:T(8,128)(2,1)S(1)}, bf16[768,3,384]{0,2,1:T(8,128)(2,1)}, u32[]{:S(2)}) copy-start(bf16[768,3,384]{0,2,1:T(8,128)(2,1)} %copy-done.6) | copy-start | bytes 5308420
  151.2 7.9 %copy-start.11 = (bf16[1024,768]{1,0:T(8,128)(2,1)S(1)}, bf16[1024,768]{1,0:T(8,128)(2,1)}, u32[]{:S(2)}) copy-start(bf16[1024,768]{1,0:T(8,128)(2,1)} %g_ref.1) | copy-start | bytes 4718596
  159.1 10.7 %copy-start.24 = (bf16[1024,768]{1,0:T(8,128)(2,1)S(1)}, bf16[1024,768]{1,0:T(8,128)(2,1)}, u32[]{:S(2)}) copy-start(bf16[1024,768]{1,0:T(8,128)(2,1)} %get-tuple-element.53) | copy-start | bytes 4718596
  159.1 10.7 %copy-start.25 = (bf16[1024,768]{1,0:T(8,128)(2,1)S(1)}, bf16[1024,768]{1,0:T(8,128)(2,1)}, u32[]{:S(2)}) copy-start(bf16[1024,768]{1,0:T(8,128)(2,1)} %get-tuple-element.54) | copy-start | bytes 4718596
  169.8 2.5 copy-start.23
  340.4 4.3 %copy-start.12 = (bf16[4,2,2,48,768]{4,3,2,1,0:T(8,128)(2,1)S(1)}, bf16[4,2,2,48,768]{4,3,2,1,0:T(8,128)(2,1)}, u32[]{:S(2)}) copy-start(bf16[4,2,2,48,768]{4,3,2,1,0:T(8,128)(2,1)} %get-tuple-element.62) | copy-start | bytes 3538948
  340.4 4.3 %copy-start.13 = (bf16[4,2,2,48,768]{4,3,2,1,0:T(8,128)(2,1)S(1)}, bf16[4,2,2,48,768]{4,3,2,1,0:T(8,128)(2,1)}, u32[]{:S(2)}) copy-start(bf16[4,2,2,48,768]{4,3,2,1,0:T(8,128)(2,1)} %get-tuple-element.63) | copy-start | bytes 3538948
  344.7 3.1 copy-start.2
  344.7 4.5 %copy-start.3 = (f32[1024,768]{1,0:T(8,128)S(1)}, f32[1024,768]{1,0:T(8,128)}, u32[]{:S(2)}) copy-start(f32[1024,768]{1,0:T(8,128)} %get-tuple-element.126) | copy-start | bytes 9437188
  (1 other events, 0.6 us)

commit v3 on v2

--- a/solution.py
+++ b/solution.py
@@ -263,24 +263,29 @@
     )(x, att, g, vecs, wides, wo, wu, wd)
 
 
-def layer(tokens, grad_out, prefix, pre_gain, pre_bias, wqkv, bias, vecs, wides, wo, wu, wd):
+def front(tokens, grad_out, prefix, pre_gain, pre_bias, wqkv, bias, vecs, wides, wo, wu, wd):
     x = tokens.astype(F32)
-    xhat1, inv1 = normed(x)
+    xhat1, _ = normed(x)
     n1 = (xhat1 * pre_gain + pre_bias).astype(BF16)
     qkv = (nn(n1, wqkv) + bias).astype(BF16)
     attended, lse = attn_fwd(prefix, qkv)
     out, n2, n3, n4, gh, gm, gml, ga, svec, swide = middle_stage(tokens, attended, grad_out, vecs, wides, wo, wu, wd)
-    dq, dk, dv, dbias = attn_bwd(prefix, qkv, attended, ga, lse)
     g_down = tn(n4, grad_out).astype(BF16)
     g_up = tn(n3, gh).astype(BF16)
     g_out = tn(n2, gml).astype(BF16)
+    return n1, qkv, attended, lse, out, gm, ga, svec, swide, g_down, g_up, g_out
+
+
+def back(prefix, tokens, pre_gain, wqkv, n1, qkv, attended, lse, gm, ga):
+    xhat1, inv1 = normed(tokens.astype(F32))
+    dq, dk, dv, dbias = attn_bwd(prefix, qkv, attended, ga, lse)
     h = D // 2
     gproj = jnp.concatenate([v[:, s] for s in (slice(0, h), slice(h, D)) for v in (dq, dk, dv)], axis=1)
     g_qkv = tn(n1, gproj).astype(BF16)
     e = nt(gproj, wqkv)
     g_pre = jnp.stack([jnp.sum(e * xhat1, axis=0), jnp.sum(e, axis=0)])
     input_grad = gm + normed_back(e * pre_gain, xhat1, inv1)
-    return out, input_grad, g_pre, g_qkv, dbias, jnp.sum(svec, 1), jnp.sum(swide, 1), g_out, g_up, g_down
+    return input_grad, g_pre, g_qkv, dbias
 
 
 def grid_of(count):
@@ -479,6 +484,366 @@
     )
 
 
+class Route:
+    def __init__(self, dims, first, near, far, mine, pair, total, out, bufs, sems):
+        self.dims, self.first, self.near, self.far = dims, first, near, far
+        self.mine, self.pair, self.total, self.out = mine, pair, total, out
+        self.land, self.land2, self.land3 = bufs
+        self.sems = sems
+        self.count = 0
+        self.flight = []
+
+    def launch(self, make):
+        slot = self.count
+        self.count += 1
+        make(slot).start()
+        self.flight.append(lambda: make(slot))
+
+    def remote(self, src, dst, where):
+        self.launch(
+            lambda slot: pltpu.make_async_remote_copy(
+                src_ref=src(), dst_ref=dst(), send_sem=self.sems.at[0, slot], recv_sem=self.sems.at[1, slot],
+                device_id=where(), device_id_type=pl.DeviceIdType.MESH,
+            )
+        )
+
+    def local(self, src, dst):
+        self.launch(lambda slot: pltpu.make_async_copy(src(), dst(), self.sems.at[0, slot]))
+
+    def settle(self):
+        for make in self.flight:
+            make().wait()
+        self.flight = []
+
+    def steps(self, place):
+        z, y, x, side, index = place
+        nz, ny, nx = self.dims
+        plain = self.first == "x"
+        one, two = (2, 1) if plain else (1, 2)
+        own = (z, y, x)
+
+        def peer(axis, shift):
+            return lax.rem(own[axis] + shift, self.dims[axis])
+
+        def device(axis, shift):
+            at = list(own)
+            at[axis] = peer(axis, shift)
+            return ((at[0] * ny + at[1]) * nx + at[2], side)
+
+        def row(ref, i):
+            return ref[i, :, x] if plain else ref[i, y]
+
+        def start():
+            if self.near is not None:
+                self.local(lambda: self.near(), lambda: self.mine())
+            self.remote(lambda: self.far(), lambda: self.pair(), lambda: (index, 1 - side))
+
+        def pair_add():
+            self.settle()
+            mine, pair = self.mine(), self.pair()
+
+            def body(i, _):
+                mine[i] = (mine[i].astype(F32) + pair[i].astype(F32)).astype(mine.dtype)
+                return 0
+
+            lax.fori_loop(0, nz, body, 0)
+            for s in range(1, self.dims[one]):
+                self.remote(
+                    lambda s=s: self.mine().at[:, :, peer(one, s)] if plain else self.mine().at[:, peer(one, s)],
+                    lambda s=s: self.land().at[s - 1],
+                    lambda s=s: device(one, s),
+                )
+
+        def add_one():
+            self.settle()
+            mine, land = self.mine(), self.land()
+
+            def body(i, _):
+                v = row(mine, i).astype(F32)
+                for s in range(1, self.dims[one]):
+                    v = v + land[s - 1, i].astype(F32)
+                if plain:
+                    mine[i, :, x] = v.astype(mine.dtype)
+                else:
+                    mine[i, y] = v.astype(mine.dtype)
+                return 0
+
+            lax.fori_loop(0, nz, body, 0)
+            for s in range(1, self.dims[two]):
+                self.remote(
+                    lambda s=s: self.mine().at[:, peer(two, s), x] if plain else self.mine().at[:, y, peer(two, s)],
+                    lambda s=s: self.land2().at[s - 1],
+                    lambda s=s: device(two, s),
+                )
+
+        def add_two():
+            self.settle()
+            mine, land = self.mine(), self.land2()
+
+            def body(i, _):
+                v = mine[i, y, x].astype(F32)
+                for s in range(1, self.dims[two]):
+                    v = v + land[s - 1, i].astype(F32)
+                mine[i, y, x] = v.astype(mine.dtype)
+                return 0
+
+            lax.fori_loop(0, nz, body, 0)
+            for s in range(1, nz):
+                self.remote(
+                    lambda s=s: self.mine().at[peer(0, s), y, x], lambda s=s: self.land3().at[s - 1], lambda s=s: device(0, s)
+                )
+
+        def spread(axis, view):
+            for s in range(1, self.dims[axis]):
+                self.remote(lambda: view(self.total()), lambda: view(self.total()), lambda s=s: device(axis, s))
+
+        def add_three():
+            self.settle()
+            mine, land, total = self.mine(), self.land3(), self.total()
+            v = mine[z, y, x].astype(F32)
+            for s in range(1, nz):
+                v = v + land[s - 1].astype(F32)
+            total[z, y, x] = v.astype(total.dtype)
+            spread(0, lambda t: t.at[z, y, x])
+
+        def wide_two():
+            self.settle()
+            spread(two, lambda t: t.at[:, y, x])
+
+        def wide_one():
+            self.settle()
+            spread(one, lambda t: t.at[:, :, x] if plain else t.at[:, y])
+
+        def leave():
+            self.settle()
+            self.local(lambda: self.total(), lambda: self.out())
+
+        return [start, pair_add, add_one, add_two, add_three, wide_two, wide_one, leave, self.settle]
+
+
+def route_buffers(dims, rows, width, dtype, first):
+    nz, ny, nx = dims
+    na, nb = (nx, ny) if first == "x" else (ny, nx)
+    tail = (rows, width)
+    shapes = [(max(na - 1, 1), nz, nb) + tail, (max(nb - 1, 1), nz) + tail, (max(nz - 1, 1),) + tail]
+    copies = 3 + 2 * (na + nb + nz - 3)
+    return [pltpu.VMEM(s, dtype) for s in shapes] + [pltpu.SemaphoreType.DMA((2, copies))]
+
+
+PAIRS = D // 128
+BLOCK = 256
+
+
+def tail_kernel(dims, table, late, schedule, count, *refs):
+    (
+        prefix_ref, q_ref, k_ref, v_ref, o_ref, g_ref, lse_ref, n1t_ref, w_ref, x_ref, gm_ref, gain_ref, svec_ref, swide_ref,
+        down_ref, up_ref, outw_ref, ig_ref, odown_ref, oup_ref, oqkv_ref, oout_ref, osmall_ref,
+        gproj, gqkv, bias, sums, small,
+        mdown, mup, mout, pdown, pup, pout, pqkv, psmall, tdown, tup, tqkv, tout, tsmall,
+    ) = refs[:41]
+    scratch = refs[41:]
+    pid = pl.program_id(0)
+    index, side = lax.axis_index("dp"), lax.axis_index("tensor")
+    nz, ny, nx = dims
+    place = (index // (ny * nx), lax.rem(index // nx, ny), lax.rem(index, nx), side, index)
+    half = D // 2
+
+    @pl.when(pid == 0)
+    def _():
+        barrier = pltpu.get_barrier_semaphore()
+        peers = [(index, 1 - side)]
+        for axis in range(3):
+            for s in range(1, dims[axis]):
+                at = list(place[:3])
+                at[axis] = lax.rem(at[axis] + s, dims[axis])
+                peers.append(((at[0] * ny + at[1]) * nx + at[2], side))
+        for peer in peers:
+            pl.semaphore_signal(barrier, inc=1, device_id=peer, device_id_type=pl.DeviceIdType.MESH)
+        pl.semaphore_wait(barrier, len(peers))
+        sums[...] = jnp.zeros_like(sums)
+
+    homes = {
+        "down": (down_ref, mdown, pdown, tdown, odown_ref),
+        "up": (up_ref, mup, pup, tup, oup_ref),
+        "qkv": (gqkv, gqkv, pqkv, tqkv, oqkv_ref),
+        "out": (outw_ref, mout, pout, tout, oout_ref),
+        "small": (small, small, psmall, tsmall, osmall_ref),
+    }
+    plans = []
+    for n, (name, lead, near, width, first) in enumerate(table):
+        src, mine, pair, total, out = homes[name]
+        bufs = scratch[4 * n : 4 * n + 4]
+        cols = lambda r, a, width=width: r.at[:, :, :, :, a : a + width]
+        if name == "down":
+            views = dict(
+                near=lambda s=src, l=lead, c=cols, a=near: c(s.at[0, l], a), far=lambda s=src, l=lead, c=cols, a=near: c(s.at[1, l], a),
+                mine=lambda s=mine, l=lead, c=cols, a=near: c(s.at[l], a), pair=lambda s=pair, l=lead, c=cols, a=near: c(s.at[l], a),
+                total=lambda s=total, l=lead, c=cols, a=near: c(s.at[l], a), out=lambda s=out, l=lead, c=cols, a=near: c(s.at[l], a),
+            )
+        elif name in ("up", "qkv"):
+            size = lead
+            views = dict(
+                near=None if name == "qkv" else (lambda s=src, c=cols, a=near: c(s, a)),
+                far=lambda s=src, c=cols, a=near, n=size: c(s, a + n), mine=lambda s=mine, c=cols, a=near: c(s, a),
+                pair=lambda s=pair, c=cols, a=near: c(s, a), total=lambda s=total, c=cols, a=near: c(s, a),
+                out=lambda s=out, c=cols, a=near: c(s, a),
+            )
+        else:
+            views = dict(
+                near=None if name == "small" else (lambda s=src: s.at[0]), far=lambda s=src: s.at[1],
+                mine=(lambda s=mine: s.at[0]) if name == "small" else (lambda s=mine: s),
+                pair=lambda s=pair: s, total=lambda s=total: s, out=lambda s=out: s,
+            )
+        bufs = [(lambda b=b: b) for b in bufs[:3]] + [bufs[3]]
+        plans.append(Route(dims, first, bufs=bufs[:3], sems=bufs[3], **views).steps(place))
+
+    def advance(step):
+        for n, k in schedule.get(step, ()):
+            plans[n][k]()
+
+    for step in range(count):
+        if schedule.get(step):
+            pl.when(pid == step)(functools.partial(advance, step))
+
+    @pl.when(pid < PAIRS)
+    def _():
+        column = lambda c: gproj.at[:, pl.ds(pl.multiple_of(head_block(pid, c) * 128, 128), 128)]
+        attn_bwd_kernel(
+            prefix_ref, q_ref, k_ref, v_ref, o_ref, g_ref, lse_ref, column(0), column(1), column(2),
+            bias.at[:, pl.ds(pl.multiple_of(pid * 128, 128), 128)],
+        )
+
+    @pl.when(pid == PAIRS)
+    def _():
+        def body(c, _):
+            at = pl.ds(pl.multiple_of(c * D, 128), D)
+            part = nn(n1t_ref[...], gproj[:, at]).astype(BF16)
+            gqkv[:, :, :, :, at] = part.reshape(gqkv.shape[:4] + (D,))
+            return 0
+
+        lax.fori_loop(0, 3, body, 0)
+
+    @pl.when(pid > PAIRS)
+    def _():
+        rows = pl.ds(pl.multiple_of((pid - PAIRS - 1) * BLOCK, BLOCK), BLOCK)
+        e = nt(gproj[rows, :], w_ref[...])
+        xhat, inv = normed(x_ref[...].astype(F32))
+        sums[0] += colsum(e * xhat)
+        sums[1] += colsum(e)
+        ig_ref[...] = gm_ref[...] + normed_back(e * gain_ref[...], xhat, inv)
+
+    @pl.when(pid == count - 1)
+    def _():
+        small[...] = jnp.zeros_like(small)
+        split = [bias[i : i + 1, :] for i in range(2)]
+        split += [jnp.sum(svec_ref[i], axis=0, keepdims=True) for i in range(2)]
+        split += [jnp.sum(swide_ref[i], axis=0, keepdims=True) for i in range(3)]
+        shared = [jnp.sum(sums[i], axis=0, keepdims=True) for i in range(2)]
+        shared += [jnp.sum(svec_ref[i], axis=0, keepdims=True) for i in range(2, 6)]
+        for s in range(2):
+            at = 0
+            for v in [v[:, s * (v.shape[1] // 2) : (s + 1) * (v.shape[1] // 2)] for v in split] + shared:
+                for c in range(v.shape[1] // 128):
+                    p = at // 8
+                    small[s, p // (ny * nx), p // nx % ny, p % nx, at % 8 : at % 8 + 1, :] = v[:, c * 128 : (c + 1) * 128]
+                    at += 1
+        for n, k in late:
+            plans[n][k]()
+
+
+def tail_stage(dims, prefix, qkv, attended, ga, lse, n1t, wqkv, tokens, gm, pre_gain, svec, swide, g_down, g_up, g_out):
+    nz, ny, nx = dims
+    parts = nz * ny * nx
+    length = qkv.shape[0]
+    ff = g_down.shape[0] // 2
+    half = ff // 2
+    rows = D // parts
+    wide = 3 * D // 2
+    small_rows = 8
+    down = g_down.reshape(2, 2, nz, ny, nx, rows, D)
+    up = g_up.reshape(nz, ny, nx, rows, 2 * ff)
+    out = g_out.reshape(2, nz, ny, nx, rows // 2, D)
+    table = []
+    for a in (0, D // 2):
+        table += [("down", 0, a, D // 2, "x"), ("down", 1, a, D // 2, "y")]
+    for a in (0, half // 2):
+        table += [("up", ff, a, half // 2, "x"), ("up", ff, half + a, half // 2, "y")]
+    table += [("out", 0, 0, D, "y")]
+    table += [("qkv", wide, 0, 384, "x"), ("qkv", wide, 640, 256, "y"), ("qkv", wide, 384, 256, "x"), ("qkv", wide, 896, 256, "y")]
+    table += [("small", 0, 0, 128, "x")]
+    groups = [(0, 1), (2, 3), (4, 5), (6, 7), (8,), (9, 10), (11, 12), (13,)]
+    enter = [0, 1, 2, 3, 4, 5, 6, 7]
+    count = PAIRS + 1 + length // BLOCK
+    at_step = [0, 0, 1, 3, 5, 7, 7, 10]
+    schedule, late = {}, []
+    depth = 9
+    for slot in range(enter[-1] + depth):
+        for g, members in enumerate(groups):
+            k = slot - enter[g]
+            if not 0 <= k < depth:
+                continue
+            for n in members:
+                if slot < len(at_step) - 1:
+                    schedule.setdefault(at_step[slot], []).append((n, k))
+                else:
+                    late.append((n, k))
+    sds = jax.ShapeDtypeStruct
+    scratch = [
+        pltpu.VMEM((length, 3 * D), BF16), pltpu.VMEM((nz, ny, nx, rows, 3 * D), BF16), pltpu.VMEM((8, D), F32),
+        pltpu.VMEM((2, 8, D), F32), pltpu.VMEM((2, nz, ny, nx, small_rows, 128), F32),
+    ]
+    shapes = {
+        "down": (2, nz, ny, nx, rows, D), "up": (nz, ny, nx, rows, ff), "out": (nz, ny, nx, rows // 2, D),
+        "qkv": (nz, ny, nx, rows, wide), "small": (nz, ny, nx, small_rows, 128),
+    }
+    kinds = {n: F32 if n == "small" else BF16 for n in shapes}
+    scratch += [pltpu.VMEM(shapes[n], kinds[n]) for n in ("down", "up", "out")]
+    scratch += [pltpu.VMEM(shapes[n], kinds[n]) for n in ("down", "up", "out", "qkv", "small")]
+    scratch += [pltpu.VMEM(shapes[n], kinds[n]) for n in ("down", "up", "qkv", "out", "small")]
+    heights = {"down": rows, "up": rows, "qkv": rows, "out": rows // 2, "small": small_rows}
+    for name, _, _, width, first in table:
+        scratch += route_buffers(dims, heights[name], width, kinds[name], first)
+    pair_at = lambda i: jnp.minimum(i, PAIRS - 1)
+    block_at = lambda i: jnp.maximum(i - PAIRS - 1, 0)
+    col = lambda c: pl.BlockSpec((length, 128), lambda i, c=c: (0, head_block(pair_at(i), c)))
+    one = pl.BlockSpec((length, 128), lambda i: (0, pair_at(i)))
+    block = pl.BlockSpec((BLOCK, D), lambda i: (block_at(i), 0))
+    whole = lambda v: pl.BlockSpec(v.shape, lambda i, n=v.ndim: (0,) * n, pipeline_mode=pl.Buffered(1))
+    hbm = pl.BlockSpec(memory_space=pl.ANY)
+    gain = pre_gain.reshape(1, D)
+    order = ("down", "up", "qkv", "out", "small")
+    results = pl.pallas_call(
+        functools.partial(tail_kernel, dims, table, late, schedule, count),
+        grid=(count,),
+        in_specs=[
+            pl.BlockSpec(memory_space=pltpu.SMEM), col(0), col(1), col(2), one, one,
+            pl.BlockSpec((1, 8, length), lambda i: (pair_at(i), 0, 0)), whole(n1t), whole(wqkv), block, block, whole(gain),
+            whole(svec), whole(swide), hbm, hbm, hbm,
+        ],
+        out_specs=[block] + [hbm] * 5,
+        out_shape=[sds((length, D), F32)] + [sds(shapes[n], kinds[n]) for n in order],
+        scratch_shapes=scratch,
+        compiler_params=pltpu.CompilerParams(collective_id=1, has_side_effects=True, vmem_limit_bytes=63 * 2**20),
+        name="tail_stage",
+    )(prefix, qkv, qkv, qkv, attended, ga, lse, n1t, wqkv, tokens, gm, gain, svec, swide, down, up, out)
+    input_grad, t_down, t_up, t_qkv, t_out, t_small = results
+    return (
+        input_grad, t_down.reshape(ff, D).astype(F32), t_up.reshape(D, ff).astype(F32), t_qkv.reshape(D, wide).astype(F32),
+        t_out.reshape(D // 2, D).astype(F32), t_small.reshape(-1),
+    )
+
+
+def pack_small(dims, g_qv, g_vec, g_wide, g_pre):
+    half, ff_half = D // 2, g_wide.shape[1] // 2
+    shared = jnp.concatenate([g_pre.reshape(-1), g_vec[2:].reshape(-1)])
+    rows = -(-(4 * half + 3 * ff_half + 6 * D) // (128 * 8 * math.prod(dims))) * 8
+    pad = jnp.zeros((rows * 128 * math.prod(dims) - (4 * half + 3 * ff_half + 6 * D),), F32)
+    pack = lambda i: jnp.concatenate(
+        [v[j, i * n : (i + 1) * n] for v, m, n in ((g_qv, 2, half), (g_vec, 2, half), (g_wide, 3, ff_half)) for j in range(m)] + [shared, pad]
+    )
+    return jnp.stack([pack(0), pack(1)]).reshape((2,) + dims + (rows, 128))
+
+
 def swap(value):
     return lax.ppermute(value, "tensor", ((0, 1), (1, 0)))
 
@@ -504,17 +869,17 @@
     ub, ig, ib = [cut(4 * half + i * ff_half, ff_half) for i in range(3)]
     vecs = jnp.stack([sgain, sbias, out_bias, ffn_gain, ffn_bias, down_bias])
     wides = jnp.stack([ub, ig, ib])
-    out, input_grad, g_pre, g_qkv, g_qv, g_vec, g_wide, g_out, g_up, g_down = layer(
+    n1, qkv, attended, lse, out, gm, ga, svec, swide, g_down, g_up, g_out = front(
         tokens, grad_out, local, pre_gain, pre_bias, wqkv, bias, vecs, wides, wo, wu, wd
     )
-    shared = jnp.concatenate([g_pre.reshape(-1), g_vec[2:].reshape(-1)])
-    rows = -(-(4 * half + 3 * ff_half + 6 * D) // (128 * 8 * math.prod(dims))) * 8
-    pad = jnp.zeros((rows * 128 * math.prod(dims) - (4 * half + 3 * ff_half + 6 * D),), F32)
-    pack = lambda i: jnp.concatenate(
-        [v[j, i * n : (i + 1) * n] for v, m, n in ((g_qv, 2, half), (g_vec, 2, half), (g_wide, 3, ff_half)) for j in range(m)] + [shared, pad]
-    )
-    small = jnp.stack([pack(0), pack(1)]).reshape((2,) + dims + (rows, 128))
-    g_down, g_up, g_qkv, g_out, small = all_reduce(dims, (g_down, g_up, g_qkv, g_out), small)
+    if D // 2 % (16 * math.prod(dims) // 2) == 0 and D // math.prod(dims) % 16 == 0:
+        input_grad, g_down, g_up, g_qkv, g_out, small = tail_stage(
+            dims, local, qkv, attended, ga, lse, n1.T, wqkv, tokens, gm, pre_gain, svec, swide, g_down, g_up, g_out
+        )
+    else:
+        input_grad, g_pre, g_qkv, g_qv = back(local, tokens, pre_gain, wqkv, n1, qkv, attended, lse, gm, ga)
+        small = pack_small(dims, g_qv, jnp.sum(svec, 1), jnp.sum(swide, 1), g_pre)
+        g_down, g_up, g_qkv, g_out, small = all_reduce(dims, (g_down, g_up, g_qkv, g_out), small)
     r = lambda i: small[i * half : (i + 1) * half]
     w = lambda i: small[4 * half + i * ff_half : 4 * half + (i + 1) * ff_half]
     base = 4 * half + 3 * ff_half

time: 359 us -> 316 us (0.88)
  Pallas kernels: 238 us -> 214 us
  local copies, waits for them, and re-layouts: 40 us -> 32.2 us
  matrix products: 42.7 us -> 36.2 us
    pallas_call x2 -> x1, Pallas kernels: 173 us -> 149 us  [tail_stage(): pl.pallas_call(functools.partial(tail_kernel, dims, table, late, schedule...]
    dot_general x1 -> x0, matrix products: 7.56 us -> none  [nt(): lax.dot_general(a, b, (((1,), (1,)), ((), ())), preferred_element_type=F32)]
    unnamed x89 -> x64, local copies, waits for them, and re-layouts: 20.5 us -> 14.7 us
    convert_element_type x0 -> x1, local copies, waits for them, and re-layouts: none -> 5.66 us  [tail_stage(): t_qkv.reshape(D, wide).astype(F32)]
    another operation x7, local copies, waits for them, and re-layouts: 4.38 us -> 0.66 us  [body(): vecs = jnp.stack([sgain, sbias, out_bias, ffn_gain, ffn_bias, down_bias])]
    concatenate x3 -> x4, other arithmetic: 10.9 us -> 14.5 us  [body(): both = lambda v, axis: jnp.concatenate([v, swap(v)], axis=axis)]
    dot_general x4 -> x3, matrix products: 27.8 us -> 28.3 us  [tn(): lax.dot_general(a, b, (((0,), (0,)), ((), ())), preferred_element_type=F32)]
  transfers between devices with their start and end apart: 5 -> 5, of which waited for: 0 -> 0; matrix products, arithmetic and copies ran while one was open for 8% -> 10% of each run, Pallas kernels for 6% -> 6%
where the time goes in v3:
time: 316 us; the launch traced here: 310 us
  Pallas kernels  214 us (68%)
  matrix products  36.2 us (11%)
  local copies, waits for them, and re-layouts  32.2 us (10%)
  other arithmetic  25.5 us (8%)
    pallas_call x1, Pallas kernels, tail_stage(): pl.pallas_call(functools.partial(tail_kernel, dims, table, late, schedule...  149 us
    pallas_call x1, Pallas kernels, middle_stage(): pl.pallas_call(mid_kernel, grid=(rows // block,), in_specs=[row(D), row(D...  44.8 us
    dot_general x3, matrix products, tn(): lax.dot_general(a, b, (((0,), (0,)), ((), ())), preferred_element_type=F32)  28.3 us
    pallas_call x1, Pallas kernels, attn_fwd(): pl.pallas_call(attn_fwd_kernel, grid=(pairs,), in_specs=[pl.BlockSpec(mem...  19.9 us
    unnamed x64, local copies, waits for them, and re-layouts  14.7 us
    concatenate x4, other arithmetic, body(): both = lambda v, axis: jnp.concatenate([v, swap(v)], axis=axis)  14.5 us
    dot_general x1, matrix products, nn(): lax.dot_general(a, b, (((1,), (0,)), ((), ())), preferred_element_type=F32)  7.85 us
  transfers between devices with their start and end apart: 5, of which 0 were waited for; matrix products, arithmetic and copies ran while one was open for 10% of the time, Pallas kernels for 6%

profile of v3, /device:TPU:0, one launch (start us, length us, event | category | flops | bytes accessed | tf_op | source)
XLA Modules:
  0.0 310.2 jit_solution(18018847458963979551)
XLA Ops:
  0.7 0.7 reshape.90
  1.4 0.7 constant_dynamic-update-slice_fusion.4
  2.1 0.7 constant_dynamic-update-slice_fusion.2
  2.7 0.7 constant_dynamic-update-slice_fusion
  3.4 0.7 constant_dynamic-update-slice_fusion.9
  4.1 0.7 constant_dynamic-update-slice_fusion.8
  5.4 3.8 %copy.41 = bf16[768,3,384]{0,2,1:T(8,128)(2,1)} copy(bf16[768,3,384]{2,0,1:T(8,128)(2,1)} %param.24) | data formatting | bytes 3538944 | tf_op args[5]
  9.3 3.9 %copy.43 = bf16[768,1152]{1,0:T(8,128)(2,1)} copy(bf16[768,1152]{0,1:T(8,128)(2,1)} %bitcast.27) | data formatting | bytes 3538944 | tf_op jit(solution)/shard_map/reshape | solution.py:859
  14.1 0.8 copy.40
  15.8 1.8 fusion.6.refs_7_
  19.6 0.7 pad_maximum_fusion.4.wide_ref
  20.3 2.3 pad_maximum_fusion.3.wo_ref
  22.6 7.8 %add_convert_fusion.q_ref.k_ref.v_ref.refs_1_.refs_2_.refs_3_ = bf16[1024,2304]{1,0:T(8,128)(2,1)} fusion(f32[2304]{0:T(1024)S(1)} %get-tuple-element.109, bf16[1024,768]{0,1:T(8,128)(2,1)S(1)} %copy.40, f32[768]{0:T(1024)S(1)} %copy-done.15, f32[768]{0:T(1024)S(1)} %copy-done.11, f32[1024]{0:T(1024)S(1)} %add_rsqrt_fusion, ...), kind=kOutput, calls=%fused_computation | convolution fusion | flops 3640393728 | bytes 9853952 | tf_op jit(solution)/shard_map/dot_general | solution.py:21
  30.4 19.9 %attn_fwd.1 = (f32[1024,768]{1,0:T(8,128)}, f32[6,8,1024]{2,1,0:T(8,128)}) custom-call(s32[1]{0:T(128)} %dynamic_slice.3.prefix_ref.refs_0_, bf16[1024,2304]{1,0:T(8,128)(2,1)} %add_convert_fusion.q_ref.k_ref.v_ref.refs_1_.refs_2_.refs_3_, bf16[1024,2304]{1,0:T(8,128)(2,1)} %add_convert_fusion.q_ref.k_ref.v_ref.refs_1_.refs_2_.refs_3_, ...), custom_call_target="tpu_custom_call" | custom-call | tf_op jit(solution)/shard_map/attn_fwd/pallas_call | solution.py:91
  50.3 3.7 %pad_maximum_fusion.2.refs_8_ = bf16[768,2304]{1,0:T(8,128)(2,1)} fusion(bf16[768,1152]{1,0:T(8,128)(2,1)} %collective-permute-done, bf16[768,1152]{1,0:T(8,128)(2,1)S(1)} %copy-done.1), kind=kLoop, calls=%fused_computation.9 | loop fusion | flops 7077888 | bytes 7077888 | tf_op jit(solution)/shard_map/concatenate | solution.py:857
  54.0 4.5 %pad_maximum_fusion.wu_ref = bf16[768,3072]{1,0:T(8,128)(2,1)} fusion(bf16[768,1536]{1,0:T(8,128)(2,1)} %collective-permute-done.3, bf16[768,1536]{1,0:T(8,128)(2,1)S(1)} %copy-done.5), kind=kLoop, calls=%fused_computation.3 | loop fusion | flops 9437184 | bytes 9437184 | tf_op jit(solution)/shard_map/concatenate | solution.py:857
  58.5 4.1 %pad_maximum_fusion.1.wd_ref = bf16[3072,768]{1,0:T(8,128)(2,1)} fusion(bf16[1536,768]{1,0:T(8,128)(2,1)} %collective-permute-done.4, bf16[1536,768]{1,0:T(8,128)(2,1)S(1)} %copy-done.6), kind=kLoop, calls=%fused_computation.4 | loop fusion | flops 9437184 | bytes 9437184 | tf_op jit(solution)/shard_map/concatenate | solution.py:857
  62.5 44.8 %middle_stage.1 = (bf16[1024,768]{1,0:T(8,128)(2,1)}, bf16[1024,768]{1,0:T(8,128)(2,1)}, bf16[1024,768]{1,0:T(8,128)(2,1)}, bf16[1024,3072]{1,0:T(8,128)(2,1)}, ...) custom-call(bf16[1024,768]{1,0:T(8,128)(2,1)} %refs_9_.1, ...), custom_call_target="tpu_custom_call" | custom-call | tf_op jit(solution)/shard_map/middle_stage/pallas_call | solution.py:251
  107.4 9.8 %convolution_convert_fusion.1 = bf16[3072,768]{1,0:T(8,128)(2,1)} fusion(bf16[1024,3072]{1,0:T(8,128)(2,1)} %get-tuple-element.43, bf16[1024,768]{1,0:T(8,128)(2,1)S(1)} %copy-done.7), kind=kOutput, calls=%fused_computation.2 | convolution fusion | flops 4834197504 | bytes 12582912 | tf_op jit(solution)/shard_map/dot_general | solution.py:29
  117.2 2.5 convolution_convert_fusion.2
  119.7 0.7 copy-done.20
  120.4 16.1 %convolution_convert_fusion = bf16[768,3072]{1,0:T(8,128)(2,1)} fusion(bf16[1024,768]{1,0:T(8,128)(2,1)S(1)} %copy-done.21, bf16[1024,3072]{1,0:T(8,128)(2,1)S(1)} %copy-done.20), kind=kOutput, calls=%fused_computation.1 | convolution fusion | flops 4834197504 | bytes 12582912 | tf_op jit(solution)/shard_map/dot_general | solution.py:29
  136.5 148.9 %tail_stage.1 = (f32[1024,768]{1,0:T(8,128)}, bf16[2,4,2,2,48,768]{5,4,3,2,1,0:T(8,128)(2,1)}, bf16[4,2,2,48,1536]{4,3,2,1,0:T(8,128)(2,1)}, bf16[4,2,2,48,1152]...) custom-call(s32[1]{0:T(128)} %dynamic_slice.3.prefix_ref.refs_0_, ...), custom_call_target="tpu_custom_call" | custom-call | tf_op jit(solution)/shard_map/tail_stage/pallas_call | solution.py:815
  285.4 1.4 fusion.10
  286.8 1.4 fusion.9
  288.2 1.4 fusion.8
  290.1 2.2 bitcast_convert_fusion.2
  292.3 5.7 %reshape.96 = f32[768,3,384]{2,1,0:T(4,128)} reshape(bf16[4,2,2,48,1152]{4,3,2,1,0:T(8,128)(2,1)} %get-tuple-element.50) | data formatting | bytes 5308416 | tf_op jit(solution)/shard_map/convert_element_type | solution.py:831
  298.0 4.5 %copy.44 = f32[768,3,384]{2,0,1:T(8,128)} copy(f32[768,3,384]{2,1,0:T(4,128)} %reshape.96) | data formatting | bytes 7077888
  302.5 3.0 bitcast_convert_fusion.1
  305.5 2.7 bitcast_convert_fusion
  308.4 1.7 copy.58
  (87 shorter events, 5.1 us)
Async XLA Ops:
  4.9 9.2 %copy-start.12 = (f32[2,384]{1,0:T(2,128)S(1)}, f32[2,384]{1,0:T(2,128)}, u32[]{:S(2)}) copy-start(f32[2,384]{1,0:T(2,128)} %param.25) | copy-start | bytes 9220
  4.9 9.2 %copy-start = (bf16[1024,768]{1,0:T(8,128)(2,1)S(1)}, bf16[1024,768]{1,0:T(8,128)(2,1)}, u32[]{:S(2)}) copy-start(bf16[1024,768]{1,0:T(8,128)(2,1)} %refs_9_.1) | copy-start | bytes 4718596
  4.9 14.0 %collective-permute-start.1 = (f32[6144]{0:T(1024)S(1)}, f32[6144]{0:T(1024)S(1)}, u32[]{:S(2)}, u32[]{:S(2)}) collective-permute-start(f32[6144]{0:T(1024)S(1)} %constant_dynamic-update-slice_fusion.8), channel_id=1, source_target_pairs={{0,1},{1,0},{2,3},{3,2},{4,5},{5,4},{6,7},{7,6},{8,9},{9,8},{10,11... | collective-permute-start | bytes 73736 | tf_op jit(solution)/shard_map/ppermute | solution.py:848
  5.3 14.9 %collective-permute-start.2 = (bf16[384,768]{1,0:T(8,128)(2,1)}, bf16[384,768]{1,0:T(8,128)(2,1)}, u32[]{:S(2)}, u32[]{:S(2)}) collective-permute-start(bf16[384,768]{1,0:T(8,128)(2,1)} %param.28), channel_id=1, source_target_pairs={{0,1},{1,0},{2,3},{3,2},{4,5},{5,4},{6,7},{7,6},{8,9},{9,8},{10,11... | collective-permute-start | bytes 1769480 | tf_op jit(solution)/shard_map/ppermute | solution.py:848
  13.1 9.5 %collective-permute-start = (bf16[768,1152]{1,0:T(8,128)(2,1)}, bf16[768,1152]{1,0:T(8,128)(2,1)}, u32[]{:S(2)}, u32[]{:S(2)}) collective-permute-start(bf16[768,1152]{1,0:T(8,128)(2,1)} %copy.43), channel_id=1, source_target_pairs={{0,1},{1,0},{2,3},{3,2},{4,5},{5,4},{6,7},{7,6},{8,9},{9,8},{10,11... | collective-permute-start | bytes 5308424 | tf_op jit(solution)/shard_map/ppermute | solution.py:848
  13.5 40.5 %collective-permute-start.3 = (bf16[768,1536]{1,0:T(8,128)(2,1)}, bf16[768,1536]{1,0:T(8,128)(2,1)}, u32[]{:S(2)}, u32[]{:S(2)}) collective-permute-start(bf16[768,1536]{1,0:T(8,128)(2,1)} %param.32), channel_id=1, source_target_pairs={{0,1},{1,0},{2,3},{3,2},{4,5},{5,4},{6,7},{7,6},{8,9},{9,8},{10,11... | collective-permute-start | bytes 7077896 | tf_op jit(solution)/shard_map/ppermute | solution.py:848
  13.6 44.9 %collective-permute-start.4 = (bf16[1536,768]{1,0:T(8,128)(2,1)}, bf16[1536,768]{1,0:T(8,128)(2,1)}, u32[]{:S(2)}, u32[]{:S(2)}) collective-permute-start(bf16[1536,768]{1,0:T(8,128)(2,1)} %param.36), channel_id=1, source_target_pairs={{0,1},{1,0},{2,3},{3,2},{4,5},{5,4},{6,7},{7,6},{8,9},{9,8},{10,11... | collective-permute-start | bytes 7077896 | tf_op jit(solution)/shard_map/ppermute | solution.py:848
  14.1 1.7 copy-start.11
  14.1 1.7 copy-start.15
  14.9 3.3 %copy-start.16 = (f32[768]{0:T(1024)S(1)}, f32[768]{0:T(1024)}, u32[]{:S(2)}) copy-start(f32[768]{0:T(1024)} %param.29) | copy-start | bytes 9220
  14.9 3.3 %copy-start.17 = (f32[768]{0:T(1024)S(1)}, f32[768]{0:T(1024)}, u32[]{:S(2)}) copy-start(f32[768]{0:T(1024)} %param.30) | copy-start | bytes 9220
  14.9 3.3 %copy-start.18 = (f32[768]{0:T(1024)S(1)}, f32[768]{0:T(1024)}, u32[]{:S(2)}) copy-start(f32[768]{0:T(1024)} %param.31) | copy-start | bytes 9220
  14.9 3.3 %copy-start.19 = (f32[768]{0:T(1024)S(1)}, f32[768]{0:T(1024)}, u32[]{:S(2)}) copy-start(f32[768]{0:T(1024)} %param.37) | copy-start | bytes 9220
  14.9 3.3 %copy-start.24 = (s32[2]{0:T(128)S(1)}, s32[2]{0:T(128)}, u32[]{:S(2)}) copy-start(s32[2]{0:T(128)} %param.21) | copy-start | bytes 28
  14.9 3.9 %copy-start.13 = (f32[384]{0:T(512)S(1)}, f32[384]{0:T(512)}, u32[]{:S(2)}) copy-start(f32[384]{0:T(512)} %param.26) | copy-start | bytes 4612
  15.0 3.9 %copy-start.14 = (f32[384]{0:T(512)S(1)}, f32[384]{0:T(512)}, u32[]{:S(2)}) copy-start(f32[384]{0:T(512)} %param.27) | copy-start | bytes 4612
  15.0 4.6 %copy-start.8 = (f32[1536]{0:T(1024)S(1)}, f32[1536]{0:T(1024)}, u32[]{:S(2)}) copy-start(f32[1536]{0:T(1024)} %param.33) | copy-start | bytes 18436
  15.0 4.6 %copy-start.9 = (f32[1536]{0:T(1024)S(1)}, f32[1536]{0:T(1024)}, u32[]{:S(2)}) copy-start(f32[1536]{0:T(1024)} %param.34) | copy-start | bytes 18436
  15.0 4.6 %copy-start.10 = (f32[1536]{0:T(1024)S(1)}, f32[1536]{0:T(1024)}, u32[]{:S(2)}) copy-start(f32[1536]{0:T(1024)} %param.35) | copy-start | bytes 18436
  15.7 6.9 %copy-start.1 = (bf16[768,1152]{1,0:T(8,128)(2,1)S(1)}, bf16[768,1152]{1,0:T(8,128)(2,1)}, u32[]{:S(2)}) copy-start(bf16[768,1152]{1,0:T(8,128)(2,1)} %copy.43) | copy-start | bytes 5308420
  50.3 3.7 %copy-start.5 = (bf16[768,1536]{1,0:T(8,128)(2,1)S(1)}, bf16[768,1536]{1,0:T(8,128)(2,1)}, u32[]{:S(2)}) copy-start(bf16[768,1536]{1,0:T(8,128)(2,1)} %param.32) | copy-start | bytes 7077892
  54.0 4.5 %copy-start.6 = (bf16[1536,768]{1,0:T(8,128)(2,1)S(1)}, bf16[1536,768]{1,0:T(8,128)(2,1)}, u32[]{:S(2)}) copy-start(bf16[1536,768]{1,0:T(8,128)(2,1)} %param.36) | copy-start | bytes 7077892
  62.5 44.8 %copy-start.7 = (bf16[1024,768]{1,0:T(8,128)(2,1)S(1)}, bf16[1024,768]{1,0:T(8,128)(2,1)}, u32[]{:S(2)}) copy-start(bf16[1024,768]{1,0:T(8,128)(2,1)} %g_ref.1) | copy-start | bytes 4718596
  107.4 9.8 %copy-start.22 = (bf16[1024,768]{1,0:T(8,128)(2,1)S(1)}, bf16[1024,768]{1,0:T(8,128)(2,1)}, u32[]{:S(2)}) copy-start(bf16[1024,768]{1,0:T(8,128)(2,1)} %get-tuple-element.46) | copy-start | bytes 4718596
  107.4 9.8 %copy-start.23 = (bf16[1024,768]{1,0:T(8,128)(2,1)S(1)}, bf16[1024,768]{1,0:T(8,128)(2,1)}, u32[]{:S(2)}) copy-start(bf16[1024,768]{1,0:T(8,128)(2,1)} %get-tuple-element.47) | copy-start | bytes 4718596
  107.4 12.3 %copy-start.21 = (bf16[1024,768]{1,0:T(8,128)(2,1)S(1)}, bf16[1024,768]{1,0:T(8,128)(2,1)}, u32[]{:S(2)}) copy-start(bf16[1024,768]{1,0:T(8,128)(2,1)} %get-tuple-element.44) | copy-start | bytes 4718596
  117.2 3.2 %copy-start.20 = (bf16[1024,3072]{1,0:T(8,128)(2,1)S(1)}, bf16[1024,3072]{1,0:T(8,128)(2,1)}, u32[]{:S(2)}) copy-start(bf16[1024,3072]{1,0:T(8,128)(2,1)} %get-tuple-element.45) | copy-start | bytes 18874372
  298.0 4.5 %copy-start.4 = (bf16[4,2,2,48,1536]{4,3,2,1,0:T(8,128)(2,1)S(1)}, bf16[4,2,2,48,1536]{4,3,2,1,0:T(8,128)(2,1)}, u32[]{:S(2)}) copy-start(bf16[4,2,2,48,1536]{4,3,2,1,0:T(8,128)(2,1)} %get-tuple-element.52) | copy-start | bytes 7077892
  302.5 3.0 copy-start.3
  305.5 2.9 copy-start.2

commit v4 on v3

--- a/solution.py
+++ b/solution.py
@@ -190,12 +190,28 @@
 
 
 def mid_kernel(
-    x_ref, att_ref, g_ref, vec_ref, wide_ref, wo_ref, wu_ref, wd_ref,
+    x_ref, att_ref, g_ref, vec_ref, wide_ref, near_wo, far_wo, near_wu, far_wu, near_wd, far_wd,
     out_ref, n2_ref, n3_ref, n4_ref, gh_ref, gm_ref, gml_ref, ga_ref, svec_ref, swide_ref,
-    act_ref, slope_ref,
+    act_ref, slope_ref, wo_ref, wu_ref, wd_ref, sem,
 ):
-    @pl.when(pl.program_id(0) == 0)
+    first = pl.program_id(0) == 0
+    half, ff_half = near_wo.shape[0], near_wu.shape[1]
+    moves = (
+        (near_wo, wo_ref.at[:half]), (far_wo, wo_ref.at[half:]), (near_wu, wu_ref.at[:, :ff_half]), (far_wu, wu_ref.at[:, ff_half:]),
+        (near_wd, wd_ref.at[:ff_half]), (far_wd, wd_ref.at[ff_half:]),
+    )
+    moves = [pltpu.make_async_copy(a, b, sem.at[i]) for i, (a, b) in enumerate(moves)]
+
+    def arrive(some):
+        @pl.when(first)
+        def _():
+            for copy in some:
+                copy.wait()
+
+    @pl.when(first)
     def _():
+        for copy in moves:
+            copy.start()
         svec_ref[...] = jnp.zeros_like(svec_ref)
         swide_ref[...] = jnp.zeros_like(swide_ref)
 
@@ -204,10 +220,12 @@
     xhat2, inv2 = normed(att_ref[...])
     n2 = (xhat2 * sub_gain + sub_bias).astype(BF16)
     n2_ref[...] = n2
+    arrive(moves[:2])
     middle = x_ref[...].astype(F32) + nn(n2, wo_ref[...]) + out_bias
     xhat3, inv3 = normed(middle)
     n3 = (xhat3 * ffn_gain + ffn_bias).astype(BF16)
     n3_ref[...] = n3
+    arrive(moves[2:4])
     hidden = nn(n3, wu_ref[...]) + up_bias
     half = 0.5 + 0.5 * lax.erf(hidden * (2.0**-0.5))
     act_ref[...] = hidden * half
@@ -216,6 +234,7 @@
     n4 = (xhat4 * inner_gain + inner_bias).astype(BF16)
     n4_ref[...] = n4
     act_ref[...] = xhat4
+    arrive(moves[4:])
     out_ref[...] = (middle + nn(n4, wd_ref[...]) + down_bias).astype(BF16)
     g = g_ref[...]
     e = nt(g, wd_ref[...])
@@ -244,36 +263,32 @@
 
 def middle_stage(x, att, g, vecs, wides, wo, wu, wd, block=256):
     rows = x.shape[0]
-    ff = wu.shape[1]
+    ff = 2 * wu[0].shape[1]
     row = lambda n: pl.BlockSpec((block, n), lambda i: (i, 0))
     whole = lambda s: pl.BlockSpec(s, lambda i: (0,) * len(s), pipeline_mode=pl.Buffered(1))
     sds = jax.ShapeDtypeStruct
     return pl.pallas_call(
         mid_kernel,
         grid=(rows // block,),
-        in_specs=[row(D), row(D), row(D), whole(vecs.shape), whole(wides.shape), whole(wo.shape), whole(wu.shape), whole(wd.shape)],
+        in_specs=[row(D), row(D), row(D), whole(vecs.shape), whole(wides.shape)] + [pl.BlockSpec(memory_space=pl.ANY)] * 6,
         out_specs=[row(D), row(D), row(D), row(ff), row(ff), row(D), row(D), row(D), whole((6, 8, D)), whole((3, 8, ff))],
         out_shape=[
             sds((rows, D), BF16), sds((rows, D), BF16), sds((rows, D), BF16), sds((rows, ff), BF16), sds((rows, ff), BF16),
             sds((rows, D), F32), sds((rows, D), BF16), sds((rows, D), BF16), sds((6, 8, D), F32), sds((3, 8, ff), F32),
         ],
-        scratch_shapes=[pltpu.VMEM((block, ff), F32), pltpu.VMEM((block, ff), F32)],
+        scratch_shapes=[pltpu.VMEM((block, ff), F32), pltpu.VMEM((block, ff), F32), pltpu.VMEM((D, D), BF16), pltpu.VMEM((D, ff), BF16), pltpu.VMEM((ff, D), BF16), pltpu.SemaphoreType.DMA((6,))],
         compiler_params=pltpu.CompilerParams(vmem_limit_bytes=62 * 2**20),
         name="middle_stage",
-    )(x, att, g, vecs, wides, wo, wu, wd)
-
-
-def front(tokens, grad_out, prefix, pre_gain, pre_bias, wqkv, bias, vecs, wides, wo, wu, wd):
-    x = tokens.astype(F32)
-    xhat1, _ = normed(x)
-    n1 = (xhat1 * pre_gain + pre_bias).astype(BF16)
-    qkv = (nn(n1, wqkv) + bias).astype(BF16)
+    )(x, att, g, vecs, wides, *wo, *wu, *wd)
+
+
+def front(tokens, grad_out, prefix, qkv, vecs, wides, wo, wu, wd):
     attended, lse = attn_fwd(prefix, qkv)
     out, n2, n3, n4, gh, gm, gml, ga, svec, swide = middle_stage(tokens, attended, grad_out, vecs, wides, wo, wu, wd)
     g_down = tn(n4, grad_out).astype(BF16)
     g_up = tn(n3, gh).astype(BF16)
     g_out = tn(n2, gml).astype(BF16)
-    return n1, qkv, attended, lse, out, gm, ga, svec, swide, g_down, g_up, g_out
+    return attended, lse, out, gm, ga, svec, swide, g_down, g_up, g_out
 
 
 def back(prefix, tokens, pre_gain, wqkv, n1, qkv, attended, lse, gm, ga):
@@ -688,10 +703,17 @@
                 pair=lambda s=pair, c=cols, a=near: c(s, a), total=lambda s=total, c=cols, a=near: c(s, a),
                 out=lambda s=out, c=cols, a=near: c(s, a),
             )
+            if name == "qkv":
+                views["out"] = lambda s=out, c=cols, a=near: c(s.at[a // (D // 2)], a % (D // 2))
+        elif name == "out":
+            views = dict(
+                near=lambda s=src, c=cols, a=near: c(s.at[0], a), far=lambda s=src, c=cols, a=near: c(s.at[1], a),
+                mine=lambda s=mine, c=cols, a=near: c(s, a), pair=lambda s=pair, c=cols, a=near: c(s, a),
+                total=lambda s=total, c=cols, a=near: c(s, a), out=lambda s=out, c=cols, a=near: c(s, a),
+            )
         else:
             views = dict(
-                near=None if name == "small" else (lambda s=src: s.at[0]), far=lambda s=src: s.at[1],
-                mine=(lambda s=mine: s.at[0]) if name == "small" else (lambda s=mine: s),
+                near=None, far=lambda s=src: s.at[1], mine=lambda s=mine: s.at[0],
                 pair=lambda s=pair: s, total=lambda s=total: s, out=lambda s=out: s,
             )
         bufs = [(lambda b=b: b) for b in bufs[:3]] + [bufs[3]]
@@ -768,10 +790,12 @@
         table += [("down", 0, a, D // 2, "x"), ("down", 1, a, D // 2, "y")]
     for a in (0, half // 2):
         table += [("up", ff, a, half // 2, "x"), ("up", ff, half + a, half // 2, "y")]
-    table += [("out", 0, 0, D, "y")]
-    table += [("qkv", wide, 0, 384, "x"), ("qkv", wide, 640, 256, "y"), ("qkv", wide, 384, 256, "x"), ("qkv", wide, 896, 256, "y")]
+    third = D // 2
+    table += [("out", 0, 0, third, "x"), ("out", 0, third, third, "y")]
+    table += [("qkv", wide, 0, third, "x"), ("qkv", wide, 2 * third, third, "y")]
+    table += [("qkv", wide, third, 256, "x"), ("qkv", wide, third + 256, 128, "y")]
     table += [("small", 0, 0, 128, "x")]
-    groups = [(0, 1), (2, 3), (4, 5), (6, 7), (8,), (9, 10), (11, 12), (13,)]
+    groups = [(0, 1), (2, 3), (4, 5), (6, 7), (8, 9), (10, 11), (12, 13), (14,)]
     enter = [0, 1, 2, 3, 4, 5, 6, 7]
     count = PAIRS + 1 + length // BLOCK
     at_step = [0, 0, 1, 3, 5, 7, 7, 10]
@@ -796,6 +820,7 @@
         "down": (2, nz, ny, nx, rows, D), "up": (nz, ny, nx, rows, ff), "out": (nz, ny, nx, rows // 2, D),
         "qkv": (nz, ny, nx, rows, wide), "small": (nz, ny, nx, small_rows, 128),
     }
+    landed = {n: (3,) + v[:4] + (wide // 3,) if n == "qkv" else v for n, v in shapes.items()}
     kinds = {n: F32 if n == "small" else BF16 for n in shapes}
     scratch += [pltpu.VMEM(shapes[n], kinds[n]) for n in ("down", "up", "out")]
     scratch += [pltpu.VMEM(shapes[n], kinds[n]) for n in ("down", "up", "out", "qkv", "small")]
@@ -821,15 +846,108 @@
             whole(svec), whole(swide), hbm, hbm, hbm,
         ],
         out_specs=[block] + [hbm] * 5,
-        out_shape=[sds((length, D), F32)] + [sds(shapes[n], kinds[n]) for n in order],
+        out_shape=[sds((length, D), F32)] + [sds(landed[n], kinds[n]) for n in order],
         scratch_shapes=scratch,
         compiler_params=pltpu.CompilerParams(collective_id=1, has_side_effects=True, vmem_limit_bytes=63 * 2**20),
         name="tail_stage",
     )(prefix, qkv, qkv, qkv, attended, ga, lse, n1t, wqkv, tokens, gm, gain, svec, swide, down, up, out)
     input_grad, t_down, t_up, t_qkv, t_out, t_small = results
     return (
-        input_grad, t_down.reshape(ff, D).astype(F32), t_up.reshape(D, ff).astype(F32), t_qkv.reshape(D, wide).astype(F32),
+        input_grad, t_down.reshape(ff, D).astype(F32), t_up.reshape(D, ff).astype(F32), t_qkv.reshape(3, D, wide // 3).astype(F32),
         t_out.reshape(D // 2, D).astype(F32), t_small.reshape(-1),
+    )
+
+
+def head_kernel(
+    x_ref, gain_ref, bias_ref, w_ref, wo_ref, sub_gain, sub_bias, up_bias, inner_gain, inner_bias, qv_ref,
+    out_bias, ffn_gain, ffn_bias, down_bias,
+    qkv_ref, n1t_ref, wall_ref, far_wo, vec_ref, wide_ref,
+    near_sem, send_sem, recv_sem, norm_ref, far_small, far_wide, far_qv,
+):
+    index, side = lax.axis_index("dp"), lax.axis_index("tensor")
+    other = (index, 1 - side)
+    mesh_id = pl.DeviceIdType.MESH
+    barrier = pltpu.get_barrier_semaphore()
+    pl.semaphore_signal(barrier, inc=1, device_id=other, device_id_type=mesh_id)
+    half = D // 2
+    wide = 3 * half
+    here = [pltpu.make_async_copy(w_ref.at[c], wall_ref.at[:, c * half : (c + 1) * half], near_sem.at[c]) for c in range(3)]
+    for copy in here:
+        copy.start()
+    pl.semaphore_wait(barrier, 1)
+    away = [(w_ref.at[c], wall_ref.at[:, wide + c * half : wide + (c + 1) * half]) for c in range(3)]
+    away += [(qv_ref, far_qv), (sub_gain, far_small.at[0]), (sub_bias, far_small.at[1])]
+    away += [(up_bias, far_wide.at[0]), (inner_gain, far_wide.at[1]), (inner_bias, far_wide.at[2]), (wo_ref, far_wo)]
+    away = [
+        pltpu.make_async_remote_copy(
+            src_ref=a, dst_ref=b, send_sem=send_sem.at[i], recv_sem=recv_sem.at[i], device_id=other, device_id_type=mesh_id
+        )
+        for i, (a, b) in enumerate(away)
+    ]
+    for copy in away:
+        copy.start()
+    length = x_ref.shape[0]
+    block = 256
+
+    def norm(i, _):
+        rows = pl.ds(pl.multiple_of(i * block, block), block)
+        xhat, _ = normed(x_ref[rows, :].astype(F32))
+        n1 = (xhat * gain_ref[...] + bias_ref[...]).astype(BF16)
+        norm_ref[rows, :] = n1
+        n1t_ref[:, rows] = n1.T
+        return 0
+
+    lax.fori_loop(0, length // block, norm, 0)
+
+    def product(first, biases):
+        weight = wall_ref[:, first : first + wide]
+        bias = jnp.concatenate([biases[0:1, :], jnp.zeros((1, half), F32), biases[1:2, :]], axis=1)
+
+        def rows(i, _):
+            at = pl.ds(pl.multiple_of(i * block, block), block)
+            qkv_ref[at, first : first + wide] = (nn(norm_ref[at, :], weight) + bias).astype(BF16)
+            return 0
+
+        lax.fori_loop(0, length // block, rows, 0)
+
+    for copy in here:
+        copy.wait()
+    product(0, qv_ref[...])
+    for copy in away:
+        copy.wait()
+    product(wide, far_qv[...])
+    vec_ref[0:1, :] = jnp.concatenate([sub_gain[...], far_small[0]], axis=1)
+    vec_ref[1:2, :] = jnp.concatenate([sub_bias[...], far_small[1]], axis=1)
+    for i, v in enumerate((out_bias, ffn_gain, ffn_bias, down_bias)):
+        vec_ref[i + 2 : i + 3, :] = v[...]
+    for i, v in enumerate((up_bias, inner_gain, inner_bias)):
+        wide_ref[i : i + 1, :] = jnp.concatenate([v[...], far_wide[i]], axis=1)
+
+
+def head_stage(tokens, pre_gain, pre_bias, w3, wo, sub_gain, sub_bias, up_bias, inner_gain, inner_bias, qv_bias, *rest):
+    length = tokens.shape[0]
+    row = lambda v: v.reshape(1, -1)
+    ff_half = up_bias.shape[0]
+    half = D // 2
+    sds = jax.ShapeDtypeStruct
+    vmem, hbm = pl.BlockSpec(memory_space=pltpu.VMEM), pl.BlockSpec(memory_space=pl.ANY)
+    return pl.pallas_call(
+        head_kernel,
+        in_specs=[vmem] * 3 + [hbm] * 2 + [vmem] * 10,
+        out_specs=[vmem] * 3 + [hbm] + [vmem] * 2,
+        out_shape=[
+            sds((length, 3 * D), BF16), sds((D, length), BF16), sds((D, 3 * D), BF16), sds(wo.shape, BF16),
+            sds((6, D), F32), sds((3, 2 * ff_half), F32),
+        ],
+        scratch_shapes=[
+            pltpu.SemaphoreType.DMA((3,)), pltpu.SemaphoreType.DMA((10,)), pltpu.SemaphoreType.DMA((10,)),
+            pltpu.VMEM((length, D), BF16), pltpu.VMEM((2, 1, half), F32), pltpu.VMEM((3, 1, ff_half), F32), pltpu.VMEM((2, half), F32),
+        ],
+        compiler_params=pltpu.CompilerParams(collective_id=2, has_side_effects=True, vmem_limit_bytes=40 * 2**20),
+        name="head_stage",
+    )(
+        tokens, row(pre_gain), row(pre_bias), w3, wo, row(sub_gain), row(sub_bias), row(up_bias), row(inner_gain), row(inner_bias),
+        qv_bias, *[row(v) for v in rest],
     )
 
 
@@ -854,38 +972,30 @@
 ):
     side = lax.axis_index("tensor")
     local = lax.dynamic_slice_in_dim(prefix, side, 1)
-    both = lambda v, axis: jnp.concatenate([v, swap(v)], axis=axis)
     half, ff_half = D // 2, up_bias.shape[0]
-    wqkv = both(qkv_weight.reshape(D, 3 * half), 1)
-    wo = both(out_weight, 0)
-    wu = both(up_weight, 1)
-    wd = both(down_weight, 0)
-    near = jnp.concatenate([qv_bias.reshape(-1), sub_gain, sub_bias, up_bias, inner_gain, inner_bias])
-    far = swap(near)
-    cut = lambda start, size: jnp.concatenate([near[start : start + size], far[start : start + size]])
-    zero = jnp.zeros((half,), F32)
-    bias = jnp.concatenate([p for v in (near, far) for p in (v[:half], zero, v[half : 2 * half])])
-    sgain, sbias = [cut(i * half, half) for i in (2, 3)]
-    ub, ig, ib = [cut(4 * half + i * ff_half, ff_half) for i in range(3)]
-    vecs = jnp.stack([sgain, sbias, out_bias, ffn_gain, ffn_bias, down_bias])
-    wides = jnp.stack([ub, ig, ib])
-    n1, qkv, attended, lse, out, gm, ga, svec, swide, g_down, g_up, g_out = front(
-        tokens, grad_out, local, pre_gain, pre_bias, wqkv, bias, vecs, wides, wo, wu, wd
+    wu, wd = (up_weight, swap(up_weight)), (down_weight, swap(down_weight))
+    qkv, n1t, wqkv, far_wo, vecs, wides = head_stage(
+        tokens, pre_gain, pre_bias, qkv_weight.transpose(1, 0, 2), out_weight, sub_gain, sub_bias, up_bias, inner_gain, inner_bias,
+        qv_bias, out_bias, ffn_gain, ffn_bias, down_bias,
     )
-    if D // 2 % (16 * math.prod(dims) // 2) == 0 and D // math.prod(dims) % 16 == 0:
+    attended, lse, out, gm, ga, svec, swide, g_down, g_up, g_out = front(
+        tokens, grad_out, local, qkv, vecs, wides, (out_weight, far_wo), wu, wd
+    )
+    if D // math.prod(dims) % 16 == 0:
         input_grad, g_down, g_up, g_qkv, g_out, small = tail_stage(
-            dims, local, qkv, attended, ga, lse, n1.T, wqkv, tokens, gm, pre_gain, svec, swide, g_down, g_up, g_out
+            dims, local, qkv, attended, ga, lse, n1t, wqkv, tokens, gm, pre_gain, svec, swide, g_down, g_up, g_out
         )
     else:
-        input_grad, g_pre, g_qkv, g_qv = back(local, tokens, pre_gain, wqkv, n1, qkv, attended, lse, gm, ga)
+        input_grad, g_pre, g_qkv, g_qv = back(local, tokens, pre_gain, wqkv, n1t.T, qkv, attended, lse, gm, ga)
         small = pack_small(dims, g_qv, jnp.sum(svec, 1), jnp.sum(swide, 1), g_pre)
         g_down, g_up, g_qkv, g_out, small = all_reduce(dims, (g_down, g_up, g_qkv, g_out), small)
+        g_qkv = g_qkv.reshape(D, 3, half).transpose(1, 0, 2)
     r = lambda i: small[i * half : (i + 1) * half]
     w = lambda i: small[4 * half + i * ff_half : 4 * half + (i + 1) * ff_half]
     base = 4 * half + 3 * ff_half
     f = lambda i: small[base + i * D : base + (i + 1) * D]
     return (
-        out, input_grad, f(0), f(1), g_qkv.reshape(D, 3, half), small[: 2 * half].reshape(2, half), r(2), r(3), g_out,
+        out, input_grad, f(0), f(1), g_qkv.transpose(1, 0, 2), small[: 2 * half].reshape(2, half), r(2), r(3), g_out,
         f(2), f(3), f(4), g_up, w(0), w(1), w(2), g_down, f(5),
     )
 

time: 316 us -> 284 us (0.90); the launches traced: 310 us -> 282 us
  matrix products: 36.2 us -> 19.1 us
  other arithmetic: 25.5 us -> 10 us
  Pallas kernels: 214 us -> 222 us
    concatenate x7 -> x0, other arithmetic: 14.5 us -> none  [the longest x4 14.5 us: body(): both = lambda v, axis: jnp.concatenate([v, swap(v)], axis=axis)]
    dot_general x3, matrix products: 28.3 us -> 19.1 us  [tn(): lax.dot_general(a, b, (((0,), (0,)), ((), ())), preferred_element_type=F32)]
    pallas_call x0 -> x1, Pallas kernels: none -> 8.14 us  [head_stage(): pl.pallas_call(head_kernel, in_specs=[vmem] * 3 + [hbm] * 2 + [vmem] * 10...]
    dot_general x1 -> x0, matrix products: 7.85 us -> none  [nn(): lax.dot_general(a, b, (((1,), (0,)), ((), ())), preferred_element_type=F32)]
    convert_element_type x1 -> x0, local copies, waits for them, and re-layouts: 5.66 us -> none  [tail_stage(): t_qkv.reshape(D, wide).astype(F32)]
    reshape x2 -> x11, local copies, waits for them, and re-layouts: 4.55 us -> 7.6 us  [head_stage(): row = lambda v: v.reshape(1, -1)]
    unnamed x64 -> x43, local copies, waits for them, and re-layouts: 14.7 us -> 16 us
  transfers between devices with their start and end apart: 5 -> 2, of which waited for: 0 -> 0; matrix products, arithmetic and copies ran while one was open for 10% -> 3% of each run, Pallas kernels for 6% -> 10%
where the time goes in v4:
time: 284 us; the launch traced here: 282 us
  Pallas kernels  222 us (78%)
  local copies, waits for them, and re-layouts  29.7 us (10%)
  matrix products  19.1 us (7%)
  other arithmetic  10 us (4%)
    pallas_call x1, Pallas kernels, tail_stage(): pl.pallas_call(functools.partial(tail_kernel, dims, table, late, schedule...  147 us
    pallas_call x1, Pallas kernels, middle_stage(): pl.pallas_call(mid_kernel, grid=(rows // block,), in_specs=[row(D), row(D...  47 us
    pallas_call x1, Pallas kernels, attn_fwd(): pl.pallas_call(attn_fwd_kernel, grid=(pairs,), in_specs=[pl.BlockSpec(mem...  19.9 us
    dot_general x3, matrix products, tn(): lax.dot_general(a, b, (((0,), (0,)), ((), ())), preferred_element_type=F32)  19.1 us
    unnamed x43, local copies, waits for them, and re-layouts  16 us
    pallas_call x1, Pallas kernels, head_stage(): pl.pallas_call(head_kernel, in_specs=[vmem] * 3 + [hbm] * 2 + [vmem] * 10...  8.14 us
    reshape x11, local copies, waits for them, and re-layouts, head_stage(): row = lambda v: v.reshape(1, -1)  7.6 us
  transfers between devices with their start and end apart: 2, of which 0 were waited for; matrix products, arithmetic and copies ran while one was open for 3% of the time, Pallas kernels for 10%

profile of v4, /device:TPU:0, one launch (start us, length us, event | category | flops | bytes accessed | tf_op | source)
XLA Modules:
  0.0 281.8 jit_solution(8368439548914336783)
XLA Ops:
  2.7 0.7 reshape.97.gain_ref.refs_11_
  3.4 0.7 reshape.98.bias_ref
  4.0 0.7 reshape.104.out_bias
  6.1 0.7 reshape.107.down_bias
  6.8 0.7 reshape.101.up_bias
  7.5 0.7 reshape.102.inner_gain
  8.2 0.7 reshape.103.inner_bias
  8.9 1.2 dynamic_slice.3.prefix_ref.refs_0_
  10.1 1.4 copy-done.1
  11.6 1.1 copy-done.3
  12.6 1.5 copy-done.4
  14.8 8.1 %head_stage.1 = (bf16[1024,2304]{1,0:T(8,128)(2,1)S(1)}, bf16[768,1024]{1,0:T(8,128)(2,1)S(1)}, bf16[768,2304]{1,0:T(8,128)(2,1)S(1)}, bf16[384,768]{1,0:T(8,128...) custom-call(bf16[1024,768]{1,0:T(8,128)(2,1)S(1)} %copy-done.1, f32[1,768]{1,0:T(1,128)S(1)} %reshape.97.gain_ref.refs_11_, ...), custom_call_target="tpu_custom_call" | custom-call | tf_op jit(solution)/shard_map/head_stage/pallas_call | solution.py:934
  22.9 2.2 copy-done
  25.1 1.8 copy-done.2
  26.9 1.1 copy-done.5
  28.1 0.8 copy-done.6
  30.1 19.9 %attn_fwd.1 = (f32[1024,768]{1,0:T(8,128)}, f32[6,8,1024]{2,1,0:T(8,128)}) custom-call(s32[1]{0:T(128)} %dynamic_slice.3.prefix_ref.refs_0_, bf16[1024,2304]{1,0:T(8,128)(2,1)} %copy-done, bf16[1024,2304]{1,0:T(8,128)(2,1)} %copy-done, bf16[1024,2304]{1,0:T(8,128)(2,1)} %copy-done), custom_call_target="tpu_custom_call" | custom-call | tf_op jit(solution)/shard_map/attn_fwd/pallas_call | solution.py:91
  50.0 1.4 copy-done.14
  51.4 47.0 %middle_stage.1 = (bf16[1024,768]{1,0:T(8,128)(2,1)}, bf16[1024,768]{1,0:T(8,128)(2,1)}, bf16[1024,768]{1,0:T(8,128)(2,1)}, bf16[1024,3072]{1,0:T(8,128)(2,1)}, ...) custom-call(bf16[1024,768]{1,0:T(8,128)(2,1)} %refs_9_.1, ...), custom_call_target="tpu_custom_call" | custom-call | tf_op jit(solution)/shard_map/middle_stage/pallas_call | solution.py:270
  98.5 9.8 %convolution_convert_fusion.1 = bf16[3072,768]{1,0:T(8,128)(2,1)} fusion(bf16[1024,3072]{1,0:T(8,128)(2,1)} %get-tuple-element.55, bf16[1024,768]{1,0:T(8,128)(2,1)S(1)} %copy-done.16), kind=kOutput, calls=%fused_computation.1 | convolution fusion | flops 4834197504 | bytes 12582912 | tf_op jit(solution)/shard_map/dot_general | solution.py:29
  108.3 2.5 convolution_convert_fusion.2
  110.8 0.7 copy-done.17
  111.5 6.9 %convolution_convert_fusion = bf16[768,3072]{1,0:T(8,128)(2,1)} fusion(bf16[1024,768]{1,0:T(8,128)(2,1)S(1)} %copy-done.18, bf16[1024,3072]{1,0:T(8,128)(2,1)S(1)} %copy-done.17), kind=kOutput, calls=%fused_computation | convolution fusion | flops 4834197504 | bytes 12582912 | tf_op jit(solution)/shard_map/dot_general | solution.py:29
  118.4 146.5 %tail_stage.1 = (f32[1024,768]{1,0:T(8,128)}, bf16[2,4,2,2,48,768]{5,4,3,2,1,0:T(8,128)(2,1)}, bf16[4,2,2,48,1536]{4,3,2,1,0:T(8,128)(2,1)}, bf16[3,4,2,2,48,384...) custom-call(s32[1]{0:T(128)} %dynamic_slice.3.prefix_ref.refs_0_, ...), custom_call_target="tpu_custom_call" | custom-call | tf_op jit(solution)/shard_map/tail_stage/pallas_call | solution.py:840
  264.9 1.4 fusion.2
  266.3 1.4 fusion.1
  267.7 1.4 fusion
  269.7 2.2 bitcast_convert_fusion.2
  271.9 2.2 convert_bitcast_fusion
  274.2 3.0 %bitcast_convert_fusion.1 = f32[768,1536]{1,0:T(8,128)} fusion(bf16[4,2,2,48,1536]{4,3,2,1,0:T(8,128)(2,1)S(1)} %copy-done.13), kind=kLoop, calls=%fused_computation.4 | loop fusion | flops 1179648 | bytes 7077888 | tf_op jit(solution)/shard_map/convert_element_type | solution.py:856
  277.2 2.7 bitcast_convert_fusion
  280.2 1.7 copy.38
  (42 shorter events, 6.3 us)
Async XLA Ops:
  0.7 49.3 %collective-permute-start = (bf16[768,1536]{1,0:T(8,128)(2,1)}, bf16[768,1536]{1,0:T(8,128)(2,1)S(1)}, u32[]{:S(2)}, u32[]{:S(2)}) collective-permute-start(bf16[768,1536]{1,0:T(8,128)(2,1)} %near_wu.1), channel_id=1, source_target_pairs={{0,1},{1,0},{2,3},{3,2},{4,5},{5,4},{6,7},{7,6},{8,9},{9,8},{10,11... | collective-permute-start | bytes 7077896 | tf_op jit(solution)/shard_map/ppermute | solution.py:966
  1.2 50.2 %collective-permute-start.1 = (bf16[1536,768]{1,0:T(8,128)(2,1)}, bf16[1536,768]{1,0:T(8,128)(2,1)}, u32[]{:S(2)}, u32[]{:S(2)}) collective-permute-start(bf16[1536,768]{1,0:T(8,128)(2,1)} %near_wd.1), channel_id=1, source_target_pairs={{0,1},{1,0},{2,3},{3,2},{4,5},{5,4},{6,7},{7,6},{8,9},{9,8},{10,11... | collective-permute-start | bytes 7077896 | tf_op jit(solution)/shard_map/ppermute | solution.py:966
  3.3 46.6 %copy-start.8 = (f32[1,768]{1,0:T(1,128)}, f32[1,768]{1,0:T(1,128)S(1)}, u32[]{:S(2)}) copy-start(f32[1,768]{1,0:T(1,128)S(1)} %reshape.97.gain_ref.refs_11_) | copy-start | bytes 9220
  10.1 1.4 copy-start.1
  11.6 1.1 copy-start.3
  12.6 1.5 copy-start.4
  14.1 0.7 copy-start.10
  22.9 2.2 copy-start
  25.1 1.8 copy-start.2
  26.9 1.1 copy-start.5
  28.1 0.8 copy-start.6
  28.9 0.6 copy-start.7
  29.5 0.6 copy-start.9
  50.0 1.4 copy-start.14
  51.4 47.1 %copy-start.16 = (bf16[1024,768]{1,0:T(8,128)(2,1)S(1)}, bf16[1024,768]{1,0:T(8,128)(2,1)}, u32[]{:S(2)}) copy-start(bf16[1024,768]{1,0:T(8,128)(2,1)} %g_ref.1) | copy-start | bytes 4718596
  98.5 9.8 %copy-start.19 = (bf16[1024,768]{1,0:T(8,128)(2,1)S(1)}, bf16[1024,768]{1,0:T(8,128)(2,1)}, u32[]{:S(2)}) copy-start(bf16[1024,768]{1,0:T(8,128)(2,1)} %get-tuple-element.58) | copy-start | bytes 4718596
  98.5 9.8 %copy-start.20 = (bf16[1024,768]{1,0:T(8,128)(2,1)S(1)}, bf16[1024,768]{1,0:T(8,128)(2,1)}, u32[]{:S(2)}) copy-start(bf16[1024,768]{1,0:T(8,128)(2,1)} %get-tuple-element.59) | copy-start | bytes 4718596
  98.5 12.3 %copy-start.18 = (bf16[1024,768]{1,0:T(8,128)(2,1)S(1)}, bf16[1024,768]{1,0:T(8,128)(2,1)}, u32[]{:S(2)}) copy-start(bf16[1024,768]{1,0:T(8,128)(2,1)} %get-tuple-element.56) | copy-start | bytes 4718596
  108.3 3.2 %copy-start.17 = (bf16[1024,3072]{1,0:T(8,128)(2,1)S(1)}, bf16[1024,3072]{1,0:T(8,128)(2,1)}, u32[]{:S(2)}) copy-start(bf16[1024,3072]{1,0:T(8,128)(2,1)} %get-tuple-element.57) | copy-start | bytes 18874372
  264.9 7.0 %copy-start.15 = (bf16[3,4,2,2,48,384]{5,4,3,2,1,0:T(8,128)(2,1)S(1)}, bf16[3,4,2,2,48,384]{5,4,3,2,1,0:T(8,128)(2,1)}, u32[]{:S(2)}) copy-start(bf16[3,4,2,2,48,384]{5,4,3,2,1,0:T(8,128)(2,1)} %get-tuple-element.62) | copy-start | bytes 5308420
  271.9 2.4 copy-start.13
  274.2 3.0 %copy-start.12 = (bf16[2,4,2,2,48,768]{5,4,3,2,1,0:T(8,128)(2,1)S(1)}, bf16[2,4,2,2,48,768]{5,4,3,2,1,0:T(8,128)(2,1)}, u32[]{:S(2)}) copy-start(bf16[2,4,2,2,48,768]{5,4,3,2,1,0:T(8,128)(2,1)} %get-tuple-element.65) | copy-start | bytes 7077892
  277.2 2.9 %copy-start.11 = (f32[1024,768]{1,0:T(8,128)S(1)}, f32[1024,768]{1,0:T(8,128)}, u32[]{:S(2)}) copy-start(f32[1024,768]{1,0:T(8,128)} %get-tuple-element.97) | copy-start | bytes 9437188

commit v5 on v4

--- a/solution.py
+++ b/solution.py
@@ -15,6 +15,7 @@
 F32 = jnp.float32
 BF16 = jnp.bfloat16
 QB = 512
+VMEM = 67043328
 
 
 def nn(a, b):
@@ -58,9 +59,26 @@
     return i // each * 3 * each + c * each + lax.rem(i, each)
 
 
-def attn_fwd_kernel(prefix_ref, q_ref, k_ref, v_ref, o_ref, lse_ref):
+def attn_fwd_kernel(prefix_ref, q_ref, k_ref, v_ref, wu_ref, wd_ref, o_ref, lse_ref, far_wu, far_wd, send_sem, recv_sem):
+    pid = pl.program_id(0)
+    other = (lax.axis_index("dp"), 1 - lax.axis_index("tensor"))
+
+    def exchange(i, src, dst):
+        return pltpu.make_async_remote_copy(
+            src_ref=src, dst_ref=dst, send_sem=send_sem.at[i], recv_sem=recv_sem.at[i], device_id=other,
+            device_id_type=pl.DeviceIdType.MESH,
+        )
+
+    @pl.when(pid == 0)
+    def _():
+        barrier = pltpu.get_barrier_semaphore()
+        pl.semaphore_signal(barrier, inc=1, device_id=other, device_id_type=pl.DeviceIdType.MESH)
+        pl.semaphore_wait(barrier, 1)
+        exchange(0, wu_ref, far_wu).start()
+        exchange(1, wd_ref, far_wd).start()
+
     length = q_ref.shape[0]
-    prefix = prefix_ref[0]
+    prefix = prefix_ref[lax.axis_index("tensor")]
     keys = halves(k_ref[...])
     value_t = v_ref[...].T
     for start in range(0, length, QB):
@@ -83,30 +101,42 @@
             lse_ref[0, head : head + 1, start : start + QB] = peak + jnp.log(total)
         o_ref[start : start + QB, :] = jnp.concatenate(parts, axis=0).T
 
-
-def attn_fwd(prefix, qkv):
+    @pl.when(pid == pl.num_programs(0) - 1)
+    def _():
+        exchange(0, wu_ref, far_wu).wait()
+        exchange(1, wd_ref, far_wd).wait()
+
+
+def attn_fwd(prefix, qkv, wu, wd):
     length = qkv.shape[0]
     pairs = D // 128
     col = lambda c: pl.BlockSpec((length, 128), lambda i, c=c: (0, head_block(i, c)))
+    hbm = pl.BlockSpec(memory_space=pl.ANY)
     return pl.pallas_call(
         attn_fwd_kernel,
         grid=(pairs,),
-        in_specs=[pl.BlockSpec(memory_space=pltpu.SMEM), col(0), col(1), col(2)],
+        in_specs=[pl.BlockSpec(memory_space=pltpu.SMEM), col(0), col(1), col(2), hbm, hbm],
         out_specs=[
             pl.BlockSpec((length, 128), lambda i: (0, i)),
             pl.BlockSpec((1, 8, length), lambda i: (i, 0, 0)),
+            hbm,
+            hbm,
         ],
         out_shape=[
             jax.ShapeDtypeStruct((length, D), F32),
             jax.ShapeDtypeStruct((pairs, 8, length), F32),
+            jax.ShapeDtypeStruct(wu.shape, BF16),
+            jax.ShapeDtypeStruct(wd.shape, BF16),
         ],
+        scratch_shapes=[pltpu.SemaphoreType.DMA((2,))] * 2,
+        compiler_params=pltpu.CompilerParams(collective_id=4, has_side_effects=True, vmem_limit_bytes=VMEM),
         name="attn_fwd",
-    )(prefix, qkv, qkv, qkv)
+    )(prefix, qkv, qkv, qkv, wu, wd)
 
 
 def attn_bwd_kernel(prefix_ref, q_ref, k_ref, v_ref, o_ref, g_ref, lse_ref, dq_ref, dk_ref, dv_ref, bias_ref):
     length = q_ref.shape[0]
-    prefix = prefix_ref[0]
+    prefix = prefix_ref[lax.axis_index("tensor")]
     scale = HEAD_DIM**-0.5
     keys = halves(k_ref[...])
     values = halves(v_ref[...])
@@ -219,12 +249,12 @@
     up_bias, inner_gain, inner_bias = [wide_ref[i : i + 1, :] for i in range(3)]
     xhat2, inv2 = normed(att_ref[...])
     n2 = (xhat2 * sub_gain + sub_bias).astype(BF16)
-    n2_ref[...] = n2
+    n2_ref[...] = n2.T
     arrive(moves[:2])
     middle = x_ref[...].astype(F32) + nn(n2, wo_ref[...]) + out_bias
     xhat3, inv3 = normed(middle)
     n3 = (xhat3 * ffn_gain + ffn_bias).astype(BF16)
-    n3_ref[...] = n3
+    n3_ref[...] = n3.T
     arrive(moves[2:4])
     hidden = nn(n3, wu_ref[...]) + up_bias
     half = 0.5 + 0.5 * lax.erf(hidden * (2.0**-0.5))
@@ -265,30 +295,22 @@
     rows = x.shape[0]
     ff = 2 * wu[0].shape[1]
     row = lambda n: pl.BlockSpec((block, n), lambda i: (i, 0))
+    turned = pl.BlockSpec((D, block), lambda i: (0, i))
     whole = lambda s: pl.BlockSpec(s, lambda i: (0,) * len(s), pipeline_mode=pl.Buffered(1))
     sds = jax.ShapeDtypeStruct
     return pl.pallas_call(
         mid_kernel,
         grid=(rows // block,),
         in_specs=[row(D), row(D), row(D), whole(vecs.shape), whole(wides.shape)] + [pl.BlockSpec(memory_space=pl.ANY)] * 6,
-        out_specs=[row(D), row(D), row(D), row(ff), row(ff), row(D), row(D), row(D), whole((6, 8, D)), whole((3, 8, ff))],
+        out_specs=[row(D), turned, turned, row(ff), row(ff), row(D), row(D), row(D), whole((6, 8, D)), whole((3, 8, ff))],
         out_shape=[
-            sds((rows, D), BF16), sds((rows, D), BF16), sds((rows, D), BF16), sds((rows, ff), BF16), sds((rows, ff), BF16),
+            sds((rows, D), BF16), sds((D, rows), BF16), sds((D, rows), BF16), sds((rows, ff), BF16), sds((rows, ff), BF16),
             sds((rows, D), F32), sds((rows, D), BF16), sds((rows, D), BF16), sds((6, 8, D), F32), sds((3, 8, ff), F32),
         ],
         scratch_shapes=[pltpu.VMEM((block, ff), F32), pltpu.VMEM((block, ff), F32), pltpu.VMEM((D, D), BF16), pltpu.VMEM((D, ff), BF16), pltpu.VMEM((ff, D), BF16), pltpu.SemaphoreType.DMA((6,))],
-        compiler_params=pltpu.CompilerParams(vmem_limit_bytes=62 * 2**20),
+        compiler_params=pltpu.CompilerParams(vmem_limit_bytes=VMEM),
         name="middle_stage",
     )(x, att, g, vecs, wides, *wo, *wu, *wd)
-
-
-def front(tokens, grad_out, prefix, qkv, vecs, wides, wo, wu, wd):
-    attended, lse = attn_fwd(prefix, qkv)
-    out, n2, n3, n4, gh, gm, gml, ga, svec, swide = middle_stage(tokens, attended, grad_out, vecs, wides, wo, wu, wd)
-    g_down = tn(n4, grad_out).astype(BF16)
-    g_up = tn(n3, gh).astype(BF16)
-    g_out = tn(n2, gml).astype(BF16)
-    return attended, lse, out, gm, ga, svec, swide, g_down, g_up, g_out
 
 
 def back(prefix, tokens, pre_gain, wqkv, n1, qkv, attended, lse, gm, ga):
@@ -500,9 +522,9 @@
 
 
 class Route:
-    def __init__(self, dims, first, near, far, mine, pair, total, out, bufs, sems):
+    def __init__(self, dims, first, near, far, mine, pair, total, bufs, sems):
         self.dims, self.first, self.near, self.far = dims, first, near, far
-        self.mine, self.pair, self.total, self.out = mine, pair, total, out
+        self.mine, self.pair, self.total = mine, pair, total
         self.land, self.land2, self.land3 = bufs
         self.sems = sems
         self.count = 0
@@ -608,32 +630,29 @@
                     lambda s=s: self.mine().at[peer(0, s), y, x], lambda s=s: self.land3().at[s - 1], lambda s=s: device(0, s)
                 )
 
-        def spread(axis, view):
+        def spread(axis, view, source):
             for s in range(1, self.dims[axis]):
-                self.remote(lambda: view(self.total()), lambda: view(self.total()), lambda s=s: device(axis, s))
+                self.remote(lambda: view(source()), lambda: view(self.total()), lambda s=s: device(axis, s))
 
         def add_three():
             self.settle()
-            mine, land, total = self.mine(), self.land3(), self.total()
+            mine, land = self.mine(), self.land3()
             v = mine[z, y, x].astype(F32)
             for s in range(1, nz):
                 v = v + land[s - 1].astype(F32)
-            total[z, y, x] = v.astype(total.dtype)
-            spread(0, lambda t: t.at[z, y, x])
+            mine[z, y, x] = v.astype(mine.dtype)
+            self.local(lambda: self.mine().at[z, y, x], lambda: self.total().at[z, y, x])
+            spread(0, lambda t: t.at[z, y, x], self.mine)
 
         def wide_two():
             self.settle()
-            spread(two, lambda t: t.at[:, y, x])
+            spread(two, lambda t: t.at[:, y, x], self.total)
 
         def wide_one():
             self.settle()
-            spread(one, lambda t: t.at[:, :, x] if plain else t.at[:, y])
-
-        def leave():
-            self.settle()
-            self.local(lambda: self.total(), lambda: self.out())
-
-        return [start, pair_add, add_one, add_two, add_three, wide_two, wide_one, leave, self.settle]
+            spread(one, lambda t: t.at[:, :, x] if plain else t.at[:, y], self.total)
+
+        return [start, pair_add, add_one, add_two, add_three, wide_two, wide_one, self.settle]
 
 
 def route_buffers(dims, rows, width, dtype, first):
@@ -649,75 +668,77 @@
 BLOCK = 256
 
 
+def greet(dims, place):
+    z, y, x, side, index = place
+    barrier = pltpu.get_barrier_semaphore()
+    peers = [(index, 1 - side)]
+    for axis in range(3):
+        for s in range(1, dims[axis]):
+            at = [z, y, x]
+            at[axis] = lax.rem(at[axis] + s, dims[axis])
+            peers.append(((at[0] * dims[1] + at[1]) * dims[2] + at[2], side))
+    for peer in peers:
+        pl.semaphore_signal(barrier, inc=1, device_id=peer, device_id_type=pl.DeviceIdType.MESH)
+    pl.semaphore_wait(barrier, len(peers))
+
+
+def place_of(dims):
+    index, side = lax.axis_index("dp"), lax.axis_index("tensor")
+    _, ny, nx = dims
+    return (index // (ny * nx), lax.rem(index // nx, ny), lax.rem(index, nx), side, index)
+
+
+def columns(ref, start, width):
+    return ref.at[..., start : start + width]
+
+
+STRIPS = 4
+FIRST_PAIR = STRIPS + 1
+QKV_STEP = FIRST_PAIR + PAIRS
+TAIL_SLOTS = (0, 0, 4, 6, 8, 10, 12, 13)
+
+
 def tail_kernel(dims, table, late, schedule, count, *refs):
     (
         prefix_ref, q_ref, k_ref, v_ref, o_ref, g_ref, lse_ref, n1t_ref, w_ref, x_ref, gm_ref, gain_ref, svec_ref, swide_ref,
-        down_ref, up_ref, outw_ref, ig_ref, odown_ref, oup_ref, oqkv_ref, oout_ref, osmall_ref,
-        gproj, gqkv, bias, sums, small,
-        mdown, mup, mout, pdown, pup, pout, pqkv, psmall, tdown, tup, tqkv, tout, tsmall,
-    ) = refs[:41]
-    scratch = refs[41:]
+        gh_ref, n2t_ref, n3t_ref, gml_ref, down_ref, ig_ref, odown_ref, oup_ref, oqkv_ref, oout_ref, osmall_ref,
+        gproj, gqkv, gup, gout, bias, sums, small, mdown, pdown, pup, pout, pqkv, psmall,
+    ) = refs[:38]
+    scratch = refs[38:]
     pid = pl.program_id(0)
-    index, side = lax.axis_index("dp"), lax.axis_index("tensor")
-    nz, ny, nx = dims
-    place = (index // (ny * nx), lax.rem(index // nx, ny), lax.rem(index, nx), side, index)
-    half = D // 2
+    _, ny, nx = dims
+    place = place_of(dims)
 
     @pl.when(pid == 0)
     def _():
-        barrier = pltpu.get_barrier_semaphore()
-        peers = [(index, 1 - side)]
-        for axis in range(3):
-            for s in range(1, dims[axis]):
-                at = list(place[:3])
-                at[axis] = lax.rem(at[axis] + s, dims[axis])
-                peers.append(((at[0] * ny + at[1]) * nx + at[2], side))
-        for peer in peers:
-            pl.semaphore_signal(barrier, inc=1, device_id=peer, device_id_type=pl.DeviceIdType.MESH)
-        pl.semaphore_wait(barrier, len(peers))
+        greet(dims, place)
         sums[...] = jnp.zeros_like(sums)
 
     homes = {
-        "down": (down_ref, mdown, pdown, tdown, odown_ref),
-        "up": (up_ref, mup, pup, tup, oup_ref),
-        "qkv": (gqkv, gqkv, pqkv, tqkv, oqkv_ref),
-        "out": (outw_ref, mout, pout, tout, oout_ref),
-        "small": (small, small, psmall, tsmall, osmall_ref),
+        "up": (gup, pup, oup_ref),
+        "qkv": (gqkv, pqkv, oqkv_ref),
+        "out": (gout, pout, oout_ref),
+        "small": (small, psmall, osmall_ref),
     }
     plans = []
-    for n, (name, lead, near, width, first) in enumerate(table):
-        src, mine, pair, total, out = homes[name]
+    for n, (name, lead, start, width, first) in enumerate(table):
         bufs = scratch[4 * n : 4 * n + 4]
-        cols = lambda r, a, width=width: r.at[:, :, :, :, a : a + width]
+        cut = lambda r, at=start, width=width: columns(r, at, width)
         if name == "down":
-            views = dict(
-                near=lambda s=src, l=lead, c=cols, a=near: c(s.at[0, l], a), far=lambda s=src, l=lead, c=cols, a=near: c(s.at[1, l], a),
-                mine=lambda s=mine, l=lead, c=cols, a=near: c(s.at[l], a), pair=lambda s=pair, l=lead, c=cols, a=near: c(s.at[l], a),
-                total=lambda s=total, l=lead, c=cols, a=near: c(s.at[l], a), out=lambda s=out, l=lead, c=cols, a=near: c(s.at[l], a),
-            )
-        elif name in ("up", "qkv"):
-            size = lead
-            views = dict(
-                near=None if name == "qkv" else (lambda s=src, c=cols, a=near: c(s, a)),
-                far=lambda s=src, c=cols, a=near, n=size: c(s, a + n), mine=lambda s=mine, c=cols, a=near: c(s, a),
-                pair=lambda s=pair, c=cols, a=near: c(s, a), total=lambda s=total, c=cols, a=near: c(s, a),
-                out=lambda s=out, c=cols, a=near: c(s, a),
-            )
+            views = [down_ref.at[0, lead], down_ref.at[1, lead], mdown.at[lead], pdown.at[lead], odown_ref.at[lead]]
+            views = [lambda v=v, cut=cut: cut(v) for v in views]
+        else:
+            src, pair, total = homes[name]
+            near = lambda s=src, cut=cut: cut(s)
+            far = lambda s=src, at=start + lead, width=width: columns(s, at, width)
+            if name in ("out", "small"):
+                near, far = [lambda s=src, i=i, cut=cut: cut(s.at[i]) for i in (0, 1)]
+            done = lambda t=total, cut=cut: cut(t)
             if name == "qkv":
-                views["out"] = lambda s=out, c=cols, a=near: c(s.at[a // (D // 2)], a % (D // 2))
-        elif name == "out":
-            views = dict(
-                near=lambda s=src, c=cols, a=near: c(s.at[0], a), far=lambda s=src, c=cols, a=near: c(s.at[1], a),
-                mine=lambda s=mine, c=cols, a=near: c(s, a), pair=lambda s=pair, c=cols, a=near: c(s, a),
-                total=lambda s=total, c=cols, a=near: c(s, a), out=lambda s=out, c=cols, a=near: c(s, a),
-            )
-        else:
-            views = dict(
-                near=None, far=lambda s=src: s.at[1], mine=lambda s=mine: s.at[0],
-                pair=lambda s=pair: s, total=lambda s=total: s, out=lambda s=out: s,
-            )
-        bufs = [(lambda b=b: b) for b in bufs[:3]] + [bufs[3]]
-        plans.append(Route(dims, first, bufs=bufs[:3], sems=bufs[3], **views).steps(place))
+                third = D // 2
+                done = lambda t=total, at=start, width=width: columns(t.at[at // third], at % third, width)
+            views = [None, far, near, lambda p=pair, cut=cut: cut(p), done]
+        plans.append(Route(dims, first, *views, [(lambda b=b: b) for b in bufs[:3]], bufs[3]).steps(place))
 
     def advance(step):
         for n, k in schedule.get(step, ()):
@@ -727,15 +748,26 @@
         if schedule.get(step):
             pl.when(pid == step)(functools.partial(advance, step))
 
-    @pl.when(pid < PAIRS)
+    @pl.when(pid < STRIPS)
     def _():
-        column = lambda c: gproj.at[:, pl.ds(pl.multiple_of(head_block(pid, c) * 128, 128), 128)]
+        width = gh_ref.shape[1]
+        at = pl.ds(pl.multiple_of(pid * width, width), width)
+        gup[:, :, :, :, at] = nn(n3t_ref[...], gh_ref[...]).astype(BF16).reshape(gup.shape[:4] + (width,))
+
+    @pl.when(pid == STRIPS)
+    def _():
+        gout[...] = nn(n2t_ref[...], gml_ref[...]).reshape(gout.shape).astype(BF16)
+
+    @pl.when((pid >= FIRST_PAIR) & (pid < QKV_STEP))
+    def _():
+        i = pid - FIRST_PAIR
+        column = lambda c: gproj.at[:, pl.ds(pl.multiple_of(head_block(i, c) * 128, 128), 128)]
         attn_bwd_kernel(
             prefix_ref, q_ref, k_ref, v_ref, o_ref, g_ref, lse_ref, column(0), column(1), column(2),
-            bias.at[:, pl.ds(pl.multiple_of(pid * 128, 128), 128)],
+            bias.at[:, pl.ds(pl.multiple_of(i * 128, 128), 128)],
         )
 
-    @pl.when(pid == PAIRS)
+    @pl.when(pid == QKV_STEP)
     def _():
         def body(c, _):
             at = pl.ds(pl.multiple_of(c * D, 128), D)
@@ -745,14 +777,14 @@
 
         lax.fori_loop(0, 3, body, 0)
 
-    @pl.when(pid > PAIRS)
+    @pl.when(pid > QKV_STEP)
     def _():
-        rows = pl.ds(pl.multiple_of((pid - PAIRS - 1) * BLOCK, BLOCK), BLOCK)
+        rows = pl.ds(pl.multiple_of((pid - QKV_STEP - 1) * BLOCK, BLOCK), BLOCK)
         e = nt(gproj[rows, :], w_ref[...])
         xhat, inv = normed(x_ref[...].astype(F32))
         sums[0] += colsum(e * xhat)
         sums[1] += colsum(e)
-        ig_ref[...] = gm_ref[...] + normed_back(e * gain_ref[...], xhat, inv)
+        ig_ref[...] = gm_ref[...] + normed_back(e * gain_ref[...].reshape(1, D), xhat, inv)
 
     @pl.when(pid == count - 1)
     def _():
@@ -773,96 +805,126 @@
             plans[n][k]()
 
 
-def tail_stage(dims, prefix, qkv, attended, ga, lse, n1t, wqkv, tokens, gm, pre_gain, svec, swide, g_down, g_up, g_out):
+def tail_stage(dims, prefix, qkv, attended, ga, lse, n1t, wqkv, tokens, gm, pre_gain, svec, swide, gh, n2t, n3t, gml, g_down):
     nz, ny, nx = dims
     parts = nz * ny * nx
     length = qkv.shape[0]
-    ff = g_down.shape[0] // 2
-    half = ff // 2
+    ff = gh.shape[1] // 2
+    half, third = ff // 2, D // 2
     rows = D // parts
     wide = 3 * D // 2
     small_rows = 8
     down = g_down.reshape(2, 2, nz, ny, nx, rows, D)
-    up = g_up.reshape(nz, ny, nx, rows, 2 * ff)
-    out = g_out.reshape(2, nz, ny, nx, rows // 2, D)
     table = []
     for a in (0, D // 2):
         table += [("down", 0, a, D // 2, "x"), ("down", 1, a, D // 2, "y")]
     for a in (0, half // 2):
         table += [("up", ff, a, half // 2, "x"), ("up", ff, half + a, half // 2, "y")]
-    third = D // 2
     table += [("out", 0, 0, third, "x"), ("out", 0, third, third, "y")]
     table += [("qkv", wide, 0, third, "x"), ("qkv", wide, 2 * third, third, "y")]
     table += [("qkv", wide, third, 256, "x"), ("qkv", wide, third + 256, 128, "y")]
     table += [("small", 0, 0, 128, "x")]
-    groups = [(0, 1), (2, 3), (4, 5), (6, 7), (8, 9), (10, 11), (12, 13), (14,)]
-    enter = [0, 1, 2, 3, 4, 5, 6, 7]
-    count = PAIRS + 1 + length // BLOCK
-    at_step = [0, 0, 1, 3, 5, 7, 7, 10]
+    groups = [((0, 1), 0), ((2, 3), 1), ((4, 5), 2), ((6, 7), 3), ((8, 9), 4), ((10, 11), 6), ((12, 13), 7), ((14,), 8)]
+    depth = 8
+    count = QKV_STEP + 1 + length // BLOCK
     schedule, late = {}, []
-    depth = 9
-    for slot in range(enter[-1] + depth):
-        for g, members in enumerate(groups):
-            k = slot - enter[g]
-            if not 0 <= k < depth:
-                continue
-            for n in members:
-                if slot < len(at_step) - 1:
-                    schedule.setdefault(at_step[slot], []).append((n, k))
-                else:
-                    late.append((n, k))
+    for slot in range(groups[-1][1] + depth):
+        for members, enter in groups:
+            k = slot - enter
+            if 0 <= k < depth:
+                where = schedule.setdefault(TAIL_SLOTS[slot], []) if slot < len(TAIL_SLOTS) else late
+                where.extend((n, k) for n in members)
     sds = jax.ShapeDtypeStruct
+    box = (nz, ny, nx)
+    shapes = {
+        "down": (2, *box, rows, D), "up": (*box, rows, ff), "qkv": (*box, rows, wide), "out": (*box, rows // 2, D),
+        "small": (*box, small_rows, 128),
+    }
+    kinds = {n: F32 if n == "small" else BF16 for n in shapes}
+    landed = dict(shapes, qkv=(3, *box, rows, third))
     scratch = [
-        pltpu.VMEM((length, 3 * D), BF16), pltpu.VMEM((nz, ny, nx, rows, 3 * D), BF16), pltpu.VMEM((8, D), F32),
-        pltpu.VMEM((2, 8, D), F32), pltpu.VMEM((2, nz, ny, nx, small_rows, 128), F32),
+        pltpu.VMEM((length, 3 * D), BF16), pltpu.VMEM((*box, rows, 3 * D), BF16), pltpu.VMEM((*box, rows, 2 * ff), BF16),
+        pltpu.VMEM((2, *box, rows // 2, D), BF16), pltpu.VMEM((8, D), F32), pltpu.VMEM((2, 8, D), F32),
+        pltpu.VMEM((2, *box, small_rows, 128), F32), pltpu.VMEM(shapes["down"], BF16),
     ]
-    shapes = {
-        "down": (2, nz, ny, nx, rows, D), "up": (nz, ny, nx, rows, ff), "out": (nz, ny, nx, rows // 2, D),
-        "qkv": (nz, ny, nx, rows, wide), "small": (nz, ny, nx, small_rows, 128),
-    }
-    landed = {n: (3,) + v[:4] + (wide // 3,) if n == "qkv" else v for n, v in shapes.items()}
-    kinds = {n: F32 if n == "small" else BF16 for n in shapes}
-    scratch += [pltpu.VMEM(shapes[n], kinds[n]) for n in ("down", "up", "out")]
     scratch += [pltpu.VMEM(shapes[n], kinds[n]) for n in ("down", "up", "out", "qkv", "small")]
-    scratch += [pltpu.VMEM(shapes[n], kinds[n]) for n in ("down", "up", "qkv", "out", "small")]
     heights = {"down": rows, "up": rows, "qkv": rows, "out": rows // 2, "small": small_rows}
     for name, _, _, width, first in table:
         scratch += route_buffers(dims, heights[name], width, kinds[name], first)
-    pair_at = lambda i: jnp.minimum(i, PAIRS - 1)
-    block_at = lambda i: jnp.maximum(i - PAIRS - 1, 0)
+    pair_at = lambda i: jnp.clip(i - FIRST_PAIR, 0, PAIRS - 1)
+    block_at = lambda i: jnp.maximum(i - QKV_STEP - 1, 0)
     col = lambda c: pl.BlockSpec((length, 128), lambda i, c=c: (0, head_block(pair_at(i), c)))
     one = pl.BlockSpec((length, 128), lambda i: (0, pair_at(i)))
     block = pl.BlockSpec((BLOCK, D), lambda i: (block_at(i), 0))
+    strip = pl.BlockSpec((length, 2 * ff // STRIPS), lambda i: (0, jnp.minimum(i, STRIPS - 1)))
     whole = lambda v: pl.BlockSpec(v.shape, lambda i, n=v.ndim: (0,) * n, pipeline_mode=pl.Buffered(1))
     hbm = pl.BlockSpec(memory_space=pl.ANY)
-    gain = pre_gain.reshape(1, D)
-    order = ("down", "up", "qkv", "out", "small")
-    results = pl.pallas_call(
+    return pl.pallas_call(
         functools.partial(tail_kernel, dims, table, late, schedule, count),
         grid=(count,),
         in_specs=[
             pl.BlockSpec(memory_space=pltpu.SMEM), col(0), col(1), col(2), one, one,
-            pl.BlockSpec((1, 8, length), lambda i: (pair_at(i), 0, 0)), whole(n1t), whole(wqkv), block, block, whole(gain),
-            whole(svec), whole(swide), hbm, hbm, hbm,
+            pl.BlockSpec((1, 8, length), lambda i: (pair_at(i), 0, 0)), whole(n1t), whole(wqkv), block, block, whole(pre_gain),
+            whole(svec), whole(swide), strip, whole(n2t), whole(n3t), whole(gml), hbm,
         ],
         out_specs=[block] + [hbm] * 5,
-        out_shape=[sds((length, D), F32)] + [sds(landed[n], kinds[n]) for n in order],
+        out_shape=[sds((length, D), F32)] + [sds(landed[n], kinds[n]) for n in ("down", "up", "qkv", "out", "small")],
         scratch_shapes=scratch,
-        compiler_params=pltpu.CompilerParams(collective_id=1, has_side_effects=True, vmem_limit_bytes=63 * 2**20),
+        compiler_params=pltpu.CompilerParams(collective_id=1, has_side_effects=True, vmem_limit_bytes=VMEM),
         name="tail_stage",
-    )(prefix, qkv, qkv, qkv, attended, ga, lse, n1t, wqkv, tokens, gm, gain, svec, swide, down, up, out)
-    input_grad, t_down, t_up, t_qkv, t_out, t_small = results
-    return (
-        input_grad, t_down.reshape(ff, D).astype(F32), t_up.reshape(D, ff).astype(F32), t_qkv.reshape(3, D, wide // 3).astype(F32),
-        t_out.reshape(D // 2, D).astype(F32), t_small.reshape(-1),
+    )(
+        prefix, qkv, qkv, qkv, attended, ga, lse, n1t, wqkv, tokens, gm, pre_gain, svec, swide, gh, n2t, n3t, gml, down,
     )
+
+
+def unpack_kernel(ig_ref, down_ref, up_ref, qkv_ref, out_ref, small_ref, oig, odown, oup, oqkv, oout, *vectors):
+    oig[...] = ig_ref[...]
+    odown[...] = down_ref[...].astype(F32)
+    oup[...] = up_ref[...].astype(F32)
+    oqkv[...] = qkv_ref[...].astype(F32)
+    oout[...] = out_ref[...].astype(F32).reshape(oout.shape)
+
+    @pl.when(pl.program_id(0) == 0)
+    def _():
+        at = 0
+        for ref in vectors:
+            for row in range(ref.shape[0] if ref.ndim == 2 else 1):
+                for c in range(ref.shape[-1] // 128):
+                    lanes = pl.ds(c * 128, 128)
+                    if ref.ndim == 2:
+                        ref[row, lanes] = small_ref[at, :]
+                    else:
+                        ref[lanes] = small_ref[at, :]
+                    at += 1
+
+
+def unpack(input_grad, down, up, qkv, out, small, ff):
+    steps = 8
+    half = D // 2
+    down, up, qkv = down.reshape(ff, D), up.reshape(D, ff), qkv.reshape(3 * D, half)
+    out = out.reshape((-1,) + out.shape[-2:])
+    small = small.reshape(-1, 128)
+    block = lambda v: pl.BlockSpec((v.shape[0] // steps,) + v.shape[1:], lambda i, n=v.ndim: (i,) + (0,) * (n - 1))
+    whole = lambda s: pl.BlockSpec(s, lambda i: (0,) * len(s), pipeline_mode=pl.Buffered(1))
+    sds = lambda s: jax.ShapeDtypeStruct(s, F32)
+    vectors = [(2, half), (half,), (half,), (ff,), (ff,), (ff,)] + [(D,)] * 6
+    shapes = [input_grad.shape, (ff, D), (D, ff), (3 * D, half), (half, D)]
+    return pl.pallas_call(
+        unpack_kernel,
+        grid=(steps,),
+        in_specs=[block(v) for v in (input_grad, down, up, qkv, out)] + [whole(small.shape)],
+        out_specs=[block(sds(s)) for s in shapes] + [whole(s) for s in vectors],
+        out_shape=[sds(s) for s in shapes + vectors],
+        compiler_params=pltpu.CompilerParams(vmem_limit_bytes=VMEM),
+        name="unpack",
+    )(input_grad, down, up, qkv, out, small)
 
 
 def head_kernel(
     x_ref, gain_ref, bias_ref, w_ref, wo_ref, sub_gain, sub_bias, up_bias, inner_gain, inner_bias, qv_ref,
     out_bias, ffn_gain, ffn_bias, down_bias,
     qkv_ref, n1t_ref, wall_ref, far_wo, vec_ref, wide_ref,
-    near_sem, send_sem, recv_sem, norm_ref, far_small, far_wide, far_qv,
+    near_sem, send_sem, recv_sem, norm_ref, far_sg, far_sb, far_ub, far_ig, far_ib, far_qv,
 ):
     index, side = lax.axis_index("dp"), lax.axis_index("tensor")
     other = (index, 1 - side)
@@ -876,8 +938,8 @@
         copy.start()
     pl.semaphore_wait(barrier, 1)
     away = [(w_ref.at[c], wall_ref.at[:, wide + c * half : wide + (c + 1) * half]) for c in range(3)]
-    away += [(qv_ref, far_qv), (sub_gain, far_small.at[0]), (sub_bias, far_small.at[1])]
-    away += [(up_bias, far_wide.at[0]), (inner_gain, far_wide.at[1]), (inner_bias, far_wide.at[2]), (wo_ref, far_wo)]
+    away += [(qv_ref, far_qv), (sub_gain, far_sg), (sub_bias, far_sb)]
+    away += [(up_bias, far_ub), (inner_gain, far_ig), (inner_bias, far_ib), (wo_ref, far_wo)]
     away = [
         pltpu.make_async_remote_copy(
             src_ref=a, dst_ref=b, send_sem=send_sem.at[i], recv_sem=recv_sem.at[i], device_id=other, device_id_type=mesh_id
@@ -888,11 +950,13 @@
         copy.start()
     length = x_ref.shape[0]
     block = 256
+    line = lambda ref: ref[...].reshape(1, -1)
+    gain, bias = line(gain_ref), line(bias_ref)
 
     def norm(i, _):
         rows = pl.ds(pl.multiple_of(i * block, block), block)
         xhat, _ = normed(x_ref[rows, :].astype(F32))
-        n1 = (xhat * gain_ref[...] + bias_ref[...]).astype(BF16)
+        n1 = (xhat * gain + bias).astype(BF16)
         norm_ref[rows, :] = n1
         n1t_ref[:, rows] = n1.T
         return 0
@@ -916,17 +980,17 @@
     for copy in away:
         copy.wait()
     product(wide, far_qv[...])
-    vec_ref[0:1, :] = jnp.concatenate([sub_gain[...], far_small[0]], axis=1)
-    vec_ref[1:2, :] = jnp.concatenate([sub_bias[...], far_small[1]], axis=1)
+    both = lambda near, far: jnp.concatenate([line(near), line(far)], axis=1)
+    vec_ref[0:1, :] = both(sub_gain, far_sg)
+    vec_ref[1:2, :] = both(sub_bias, far_sb)
     for i, v in enumerate((out_bias, ffn_gain, ffn_bias, down_bias)):
-        vec_ref[i + 2 : i + 3, :] = v[...]
-    for i, v in enumerate((up_bias, inner_gain, inner_bias)):
-        wide_ref[i : i + 1, :] = jnp.concatenate([v[...], far_wide[i]], axis=1)
+        vec_ref[i + 2 : i + 3, :] = line(v)
+    for i, (near, far) in enumerate(((up_bias, far_ub), (inner_gain, far_ig), (inner_bias, far_ib))):
+        wide_ref[i : i + 1, :] = both(near, far)
 
 
 def head_stage(tokens, pre_gain, pre_bias, w3, wo, sub_gain, sub_bias, up_bias, inner_gain, inner_bias, qv_bias, *rest):
     length = tokens.shape[0]
-    row = lambda v: v.reshape(1, -1)
     ff_half = up_bias.shape[0]
     half = D // 2
     sds = jax.ShapeDtypeStruct
@@ -941,14 +1005,12 @@
         ],
         scratch_shapes=[
             pltpu.SemaphoreType.DMA((3,)), pltpu.SemaphoreType.DMA((10,)), pltpu.SemaphoreType.DMA((10,)),
-            pltpu.VMEM((length, D), BF16), pltpu.VMEM((2, 1, half), F32), pltpu.VMEM((3, 1, ff_half), F32), pltpu.VMEM((2, half), F32),
+            pltpu.VMEM((length, D), BF16), *[pltpu.VMEM((half,), F32)] * 2,
+            *[pltpu.VMEM((ff_half,), F32)] * 3, pltpu.VMEM((2, half), F32),
         ],
-        compiler_params=pltpu.CompilerParams(collective_id=2, has_side_effects=True, vmem_limit_bytes=40 * 2**20),
+        compiler_params=pltpu.CompilerParams(collective_id=2, has_side_effects=True, vmem_limit_bytes=VMEM),
         name="head_stage",
-    )(
-        tokens, row(pre_gain), row(pre_bias), w3, wo, row(sub_gain), row(sub_bias), row(up_bias), row(inner_gain), row(inner_bias),
-        qv_bias, *[row(v) for v in rest],
-    )
+    )(tokens, pre_gain, pre_bias, w3, wo, sub_gain, sub_bias, up_bias, inner_gain, inner_bias, qv_bias, *rest)
 
 
 def pack_small(dims, g_qv, g_vec, g_wide, g_pre):
@@ -962,41 +1024,43 @@
     return jnp.stack([pack(0), pack(1)]).reshape((2,) + dims + (rows, 128))
 
 
-def swap(value):
-    return lax.ppermute(value, "tensor", ((0, 1), (1, 0)))
-
-
 def body(
     dims, tokens, grad_out, prefix, pre_gain, pre_bias, qkv_weight, qv_bias, sub_gain, sub_bias, out_weight, out_bias,
     ffn_gain, ffn_bias, up_weight, up_bias, inner_gain, inner_bias, down_weight, down_bias,
 ):
-    side = lax.axis_index("tensor")
-    local = lax.dynamic_slice_in_dim(prefix, side, 1)
     half, ff_half = D // 2, up_bias.shape[0]
-    wu, wd = (up_weight, swap(up_weight)), (down_weight, swap(down_weight))
-    qkv, n1t, wqkv, far_wo, vecs, wides = head_stage(
+    qkv, n1t, wqkv, wo_far, vecs, wides = head_stage(
         tokens, pre_gain, pre_bias, qkv_weight.transpose(1, 0, 2), out_weight, sub_gain, sub_bias, up_bias, inner_gain, inner_bias,
         qv_bias, out_bias, ffn_gain, ffn_bias, down_bias,
     )
-    attended, lse, out, gm, ga, svec, swide, g_down, g_up, g_out = front(
-        tokens, grad_out, local, qkv, vecs, wides, (out_weight, far_wo), wu, wd
-    )
+    attended, lse, wu_far, wd_far = attn_fwd(prefix, qkv, up_weight, down_weight)
+    wo, wu, wd = (out_weight, wo_far), (up_weight, wu_far), (down_weight, wd_far)
+    out, n2t, n3t, n4, gh, gm, gml, ga, svec, swide = middle_stage(tokens, attended, grad_out, vecs, wides, wo, wu, wd)
+    g_down = tn(n4, grad_out).astype(BF16)
     if D // math.prod(dims) % 16 == 0:
-        input_grad, g_down, g_up, g_qkv, g_out, small = tail_stage(
-            dims, local, qkv, attended, ga, lse, n1t, wqkv, tokens, gm, pre_gain, svec, swide, g_down, g_up, g_out
+        sums = tail_stage(
+            dims, prefix, qkv, attended, ga, lse, n1t, wqkv, tokens, gm, pre_gain, svec, swide, gh, n2t, n3t, gml, g_down
         )
+        input_grad, g_down, g_up, g_qkv, g_out, *vectors = unpack(*sums, ff_half)
+        g_qv, g_sub_gain, g_sub_bias, g_up_bias, g_inner_gain, g_inner_bias = vectors[:6]
+        g_pre_gain, g_pre_bias, g_out_bias, g_ffn_gain, g_ffn_bias, g_down_bias = vectors[6:]
+        g_qkv = g_qkv.reshape(3, D, half)
     else:
-        input_grad, g_pre, g_qkv, g_qv = back(local, tokens, pre_gain, wqkv, n1t.T, qkv, attended, lse, gm, ga)
+        g_up, g_out = nn(n3t, gh).astype(BF16), nn(n2t, gml).astype(BF16)
+        input_grad, g_pre, g_qkv, g_qv = back(prefix, tokens, pre_gain, wqkv, n1t.T, qkv, attended, lse, gm, ga)
         small = pack_small(dims, g_qv, jnp.sum(svec, 1), jnp.sum(swide, 1), g_pre)
         g_down, g_up, g_qkv, g_out, small = all_reduce(dims, (g_down, g_up, g_qkv, g_out), small)
         g_qkv = g_qkv.reshape(D, 3, half).transpose(1, 0, 2)
-    r = lambda i: small[i * half : (i + 1) * half]
-    w = lambda i: small[4 * half + i * ff_half : 4 * half + (i + 1) * ff_half]
-    base = 4 * half + 3 * ff_half
-    f = lambda i: small[base + i * D : base + (i + 1) * D]
+        g_qv = small[: 2 * half].reshape(2, half)
+        g_sub_gain, g_sub_bias = [small[i * half : (i + 1) * half] for i in (2, 3)]
+        g_up_bias, g_inner_gain, g_inner_bias = [small[4 * half + i * ff_half : 4 * half + (i + 1) * ff_half] for i in range(3)]
+        base = 4 * half + 3 * ff_half
+        g_pre_gain, g_pre_bias, g_out_bias, g_ffn_gain, g_ffn_bias, g_down_bias = [
+            small[base + i * D : base + (i + 1) * D] for i in range(6)
+        ]
     return (
-        out, input_grad, f(0), f(1), g_qkv.transpose(1, 0, 2), small[: 2 * half].reshape(2, half), r(2), r(3), g_out,
-        f(2), f(3), f(4), g_up, w(0), w(1), w(2), g_down, f(5),
+        out, input_grad, g_pre_gain, g_pre_bias, g_qkv.transpose(1, 0, 2), g_qv, g_sub_gain, g_sub_bias, g_out, g_out_bias,
+        g_ffn_gain, g_ffn_bias, g_up, g_up_bias, g_inner_gain, g_inner_bias, g_down, g_down_bias,
     )
 
 

time: 284 us -> 259 us (0.912)
  local copies, waits for them, and re-layouts: 29.7 us -> 0 us
  Pallas kernels: 222 us -> 249 us
  other arithmetic: 10 us -> 0 us
  matrix products: 19.1 us -> 9.13 us
    unnamed x43 -> x0, local copies, waits for them, and re-layouts: 16 us -> none
    pallas_call x0 -> x1, Pallas kernels: none -> 11.3 us  [unpack(): pl.pallas_call(unpack_kernel, grid=(steps,), in_specs=[block(v) for v in...]
    dot_general x3 -> x1, matrix products: 19.1 us -> 9.13 us  [tn(): lax.dot_general(a, b, (((0,), (0,)), ((), ())), preferred_element_type=F32)]
    pallas_call x1, Pallas kernels: 147 us -> 156 us  [tail_stage(): pl.pallas_call(functools.partial(tail_kernel, dims, table, late, schedule...]
    reshape x12 -> x0, local copies, waits for them, and re-layouts: 8.19 us -> none  [the longest x11 7.6 us: head_stage(): row = lambda v: v.reshape(1, -1)]
    convert_element_type x3 -> x0, other arithmetic: 7.83 us -> none  [the longest x1 2.98 us: tail_stage(): t_up.reshape(D, ff).astype(F32)]
    pallas_call x1, Pallas kernels: 8.14 us -> 12.9 us  [head_stage(): pl.pallas_call(head_kernel, in_specs=[vmem] * 3 + [hbm] * 2 + [vmem] * 10...]
    slice x3 -> x0, local copies, waits for them, and re-layouts: 4.2 us -> none  [the longest x1 1.42 us: body(): r = lambda i: small[i * half:(i + 1) * half]]
  transfers between devices with their start and end apart: 2 -> 0, of which waited for: 0 -> 0; matrix products, arithmetic and copies ran while one was open for 3% -> 0% of each run, Pallas kernels for 10% -> 0%
where the time goes in v5:
time: 259 us
  Pallas kernels  249 us (96%)
  matrix products  9.13 us (4%)
    pallas_call x1, Pallas kernels, tail_stage(): pl.pallas_call(functools.partial(tail_kernel, dims, table, late, schedule...  156 us
    pallas_call x1, Pallas kernels, middle_stage(): pl.pallas_call(mid_kernel, grid=(rows // block,), in_specs=[row(D), row(D...  48.1 us
    pallas_call x1, Pallas kernels, attn_fwd(): pl.pallas_call(attn_fwd_kernel, grid=(pairs,), in_specs=[pl.BlockSpec(mem...  20.1 us
    pallas_call x1, Pallas kernels, head_stage(): pl.pallas_call(head_kernel, in_specs=[vmem] * 3 + [hbm] * 2 + [vmem] * 10...  12.9 us
    pallas_call x1, Pallas kernels, unpack(): pl.pallas_call(unpack_kernel, grid=(steps,), in_specs=[block(v) for v in...  11.3 us
    dot_general x1, matrix products, tn(): lax.dot_general(a, b, (((0,), (0,)), ((), ())), preferred_element_type=F32)  9.13 us

profile of v5, /device:TPU:0, one launch (start us, length us, event | category | flops | bytes accessed | tf_op | source)
XLA Modules:
  0.0 258.7 jit_solution(8159669510427648794)
XLA Ops:
  0.7 12.9 %head_stage.1 = (bf16[1024,2304]{1,0:T(8,128)(2,1)}, bf16[768,1024]{1,0:T(8,128)(2,1)}, bf16[768,2304]{1,0:T(8,128)(2,1)}, bf16[384,768]{1,0:T(8,128)(2,1)}, f32[6,768]{1,0:T(8,128)}, /*index=5*/f32[3,3072]{1,0:T(4,128)}) custom-call(bf16[1024,768]{1,0:T(8,128)(2,1)} %refs_9_.1, f32[768]{0:T(1024)} %refs_11_.1, f32[768]{0:T(1024)} %bias_ref.1, ...), custom_call_target="tpu_custom_call" | custom-call | tf_op jit(solution)/shard_map/head_stage/pallas_call | solution.py:998
  13.6 20.1 %attn_fwd.1 = (f32[1024,768]{1,0:T(8,128)}, f32[6,8,1024]{2,1,0:T(8,128)}, bf16[768,1536]{1,0:T(8,128)(2,1)}, bf16[1536,768]{1,0:T(8,128)(2,1)}) custom-call(s32[2]{0:T(128)} %refs_0_.1, bf16[1024,2304]{1,0:T(8,128)(2,1)} %get-tuple-element.61.q_ref.k_ref.v_ref.refs_1_.refs_2_.refs_3_, ...), custom_call_target="tpu_custom_call" | custom-call | tf_op jit(solution)/shard_map/attn_fwd/pallas_call | solution.py:115
  33.7 48.1 %middle_stage.1 = (bf16[1024,768]{1,0:T(8,128)(2,1)}, bf16[768,1024]{1,0:T(8,128)(2,1)}, bf16[768,1024]{1,0:T(8,128)(2,1)}, bf16[1024,3072]{1,0:T(8,128)(2,1)}, ...) custom-call(bf16[1024,768]{1,0:T(8,128)(2,1)} %refs_9_.1, ...), custom_call_target="tpu_custom_call" | custom-call | tf_op jit(solution)/shard_map/middle_stage/pallas_call | solution.py:301
  81.8 9.1 %convolution_convert_fusion = bf16[3072,768]{1,0:T(8,128)(2,1)} fusion(bf16[1024,3072]{1,0:T(8,128)(2,1)} %get-tuple-element.80, bf16[1024,768]{1,0:T(8,128)(2,1)} %g_ref.1), kind=kOutput, calls=%fused_computation | convolution fusion | flops 4834197504 | bytes 12582912 | tf_op jit(solution)/shard_map/dot_general | solution.py:30
  90.9 156.2 %tail_stage.1 = (f32[1024,768]{1,0:T(8,128)}, bf16[2,4,2,2,48,768]{5,4,3,2,1,0:T(8,128)(2,1)}, bf16[4,2,2,48,1536]{4,3,2,1,0:T(8,128)(2,1)}, bf16[3,4,2,2,48,384...) custom-call(s32[2]{0:T(128)} %refs_0_.1, ...), custom_call_target="tpu_custom_call" | custom-call | tf_op jit(solution)/shard_map/tail_stage/pallas_call | solution.py:862
  247.2 11.3 %unpack.1 = (f32[1024,768]{1,0:T(8,128)}, f32[1536,768]{1,0:T(8,128)}, f32[768,1536]{1,0:T(8,128)}, f32[2304,384]{1,0:T(8,128)}, f32[384,768]{1,0:T(8,128)}, /*i...) custom-call(f32[1024,768]{1,0:T(8,128)} %get-tuple-element.81.ig_ref, ...), custom_call_target="tpu_custom_call" | custom-call | tf_op jit(solution)/shard_map/unpack/pallas_call | solution.py:912

commit v6 on v5

--- a/solution.py
+++ b/solution.py
@@ -695,7 +695,28 @@
 STRIPS = 4
 FIRST_PAIR = STRIPS + 1
 QKV_STEP = FIRST_PAIR + PAIRS
-TAIL_SLOTS = (0, 0, 4, 6, 8, 10, 12, 13)
+ORDER = (
+    (0, 3, 1, 2),
+    (0, 3),
+    (),
+    (2,),
+    (5, 0, 6, 7),
+    (1, 3, 6, 4, 0, 2, 8),
+    (9, 0, 1, 3, 5, 4, 9, 2),
+    (0, 7, 3, 1, 5, 8, 2),
+    (0, 4, 5),
+    (2, 3, 1, 7, 6, 5),
+    (1, 4, 3, 2),
+    (5, 4, 1),
+    (10, 4, 11, 9, 7, 6, 8, 10, 11, 13, 12, 8, 9, 12, 13, 7),
+    (8, 10, 11, 6, 1, 4, 5, 9),
+    (7, 8, 11, 10),
+    (12, 6, 13),
+    (
+        11, 14, 8, 9, 10, 7, 14, 11, 12, 6, 13, 10, 0, 5, 12, 8, 14, 11, 2, 12, 13, 10, 7, 14, 6, 14, 13, 14, 9, 12, 14,
+        13, 10, 9, 11, 4, 3, 12, 13, 14,
+    ),
+)
 
 
 def tail_kernel(dims, table, late, schedule, count, *refs):
@@ -824,16 +845,15 @@
     table += [("qkv", wide, 0, third, "x"), ("qkv", wide, 2 * third, third, "y")]
     table += [("qkv", wide, third, 256, "x"), ("qkv", wide, third + 256, 128, "y")]
     table += [("small", 0, 0, 128, "x")]
-    groups = [((0, 1), 0), ((2, 3), 1), ((4, 5), 2), ((6, 7), 3), ((8, 9), 4), ((10, 11), 6), ((12, 13), 7), ((14,), 8)]
-    depth = 8
     count = QKV_STEP + 1 + length // BLOCK
-    schedule, late = {}, []
-    for slot in range(groups[-1][1] + depth):
-        for members, enter in groups:
-            k = slot - enter
-            if 0 <= k < depth:
-                where = schedule.setdefault(TAIL_SLOTS[slot], []) if slot < len(TAIL_SLOTS) else late
-                where.extend((n, k) for n in members)
+    phase = [0] * len(table)
+    steps = []
+    for pieces in ORDER:
+        steps.append([])
+        for n in pieces:
+            steps[-1].append((n, phase[n]))
+            phase[n] += 1
+    schedule, late = dict(enumerate(steps[:count])), steps[count]
     sds = jax.ShapeDtypeStruct
     box = (nz, ny, nx)
     shapes = {

time: 259 us -> 240 us (0.927)
  Pallas kernels: 249 us -> 229 us
    pallas_call x1, Pallas kernels: 156 us -> 137 us  [tail_stage(): pl.pallas_call(functools.partial(tail_kernel, dims, table, late, schedule...]
where the time goes in v6:
time: 240 us; the launch traced here: 239 us
  Pallas kernels  229 us (95%)
  matrix products  9.13 us (4%)
    pallas_call x1, Pallas kernels, tail_stage(): pl.pallas_call(functools.partial(tail_kernel, dims, table, late, schedule...  137 us
    pallas_call x1, Pallas kernels, middle_stage(): pl.pallas_call(mid_kernel, grid=(rows // block,), in_specs=[row(D), row(D...  48.1 us
    pallas_call x1, Pallas kernels, attn_fwd(): pl.pallas_call(attn_fwd_kernel, grid=(pairs,), in_specs=[pl.BlockSpec(mem...  20.1 us
    pallas_call x1, Pallas kernels, head_stage(): pl.pallas_call(head_kernel, in_specs=[vmem] * 3 + [hbm] * 2 + [vmem] * 10...  12.9 us
    pallas_call x1, Pallas kernels, unpack(): pl.pallas_call(unpack_kernel, grid=(steps,), in_specs=[block(v) for v in...  11.3 us
    dot_general x1, matrix products, tn(): lax.dot_general(a, b, (((0,), (0,)), ((), ())), preferred_element_type=F32)  9.13 us

profile of v6, /device:TPU:0, one launch (start us, length us, event | category | flops | bytes accessed | tf_op | source)
XLA Modules:
  0.0 239.3 jit_solution(1251130481932189107)
XLA Ops:
  0.7 12.9 %head_stage.1 = (bf16[1024,2304]{1,0:T(8,128)(2,1)}, bf16[768,1024]{1,0:T(8,128)(2,1)}, bf16[768,2304]{1,0:T(8,128)(2,1)}, bf16[384,768]{1,0:T(8,128)(2,1)}, f32[6,768]{1,0:T(8,128)}, /*index=5*/f32[3,3072]{1,0:T(4,128)}) custom-call(bf16[1024,768]{1,0:T(8,128)(2,1)} %refs_9_.1, f32[768]{0:T(1024)} %refs_11_.1, f32[768]{0:T(1024)} %bias_ref.1, ...), custom_call_target="tpu_custom_call" | custom-call | tf_op jit(solution)/shard_map/head_stage/pallas_call | solution.py:1018
  13.6 20.1 %attn_fwd.1 = (f32[1024,768]{1,0:T(8,128)}, f32[6,8,1024]{2,1,0:T(8,128)}, bf16[768,1536]{1,0:T(8,128)(2,1)}, bf16[1536,768]{1,0:T(8,128)(2,1)}) custom-call(s32[2]{0:T(128)} %refs_0_.1, bf16[1024,2304]{1,0:T(8,128)(2,1)} %get-tuple-element.61.q_ref.k_ref.v_ref.refs_1_.refs_2_.refs_3_, ...), custom_call_target="tpu_custom_call" | custom-call | tf_op jit(solution)/shard_map/attn_fwd/pallas_call | solution.py:115
  33.7 48.1 %middle_stage.1 = (bf16[1024,768]{1,0:T(8,128)(2,1)}, bf16[768,1024]{1,0:T(8,128)(2,1)}, bf16[768,1024]{1,0:T(8,128)(2,1)}, bf16[1024,3072]{1,0:T(8,128)(2,1)}, ...) custom-call(bf16[1024,768]{1,0:T(8,128)(2,1)} %refs_9_.1, ...), custom_call_target="tpu_custom_call" | custom-call | tf_op jit(solution)/shard_map/middle_stage/pallas_call | solution.py:301
  81.8 9.1 %convolution_convert_fusion = bf16[3072,768]{1,0:T(8,128)(2,1)} fusion(bf16[1024,3072]{1,0:T(8,128)(2,1)} %get-tuple-element.80, bf16[1024,768]{1,0:T(8,128)(2,1)} %g_ref.1), kind=kOutput, calls=%fused_computation | convolution fusion | flops 4834197504 | bytes 12582912 | tf_op jit(solution)/shard_map/dot_general | solution.py:30
  90.9 136.8 %tail_stage.1 = (f32[1024,768]{1,0:T(8,128)}, bf16[2,4,2,2,48,768]{5,4,3,2,1,0:T(8,128)(2,1)}, bf16[4,2,2,48,1536]{4,3,2,1,0:T(8,128)(2,1)}, bf16[3,4,2,2,48,384...) custom-call(s32[2]{0:T(128)} %refs_0_.1, ...), custom_call_target="tpu_custom_call" | custom-call | tf_op jit(solution)/shard_map/tail_stage/pallas_call | solution.py:882
  227.8 11.3 %unpack.1 = (f32[1024,768]{1,0:T(8,128)}, f32[1536,768]{1,0:T(8,128)}, f32[768,1536]{1,0:T(8,128)}, f32[2304,384]{1,0:T(8,128)}, f32[384,768]{1,0:T(8,128)}, /*i...) custom-call(f32[1024,768]{1,0:T(8,128)} %get-tuple-element.81.ig_ref, ...), custom_call_target="tpu_custom_call" | custom-call | tf_op jit(solution)/shard_map/unpack/pallas_call | solution.py:932

commit v7 on v6

--- a/solution.py
+++ b/solution.py
@@ -81,25 +81,35 @@
     prefix = prefix_ref[lax.axis_index("tensor")]
     keys = halves(k_ref[...])
     value_t = v_ref[...].T
-    for start in range(0, length, QB):
+    units = [(start, head) for start in range(0, length, QB) for head in range(2)]
+
+    def score(start, head):
         query = q_ref[start : start + QB, :] * jnp.asarray(HEAD_DIM**-0.5, BF16)
-        parts = []
-        for head in range(2):
-            scores = []
-            for first, last, mask in spans(start, length, QB):
-                s = nt(keys[head][first:last], query)
-                scores.append(masked(s, first, start, prefix) if mask else s)
-            peak = functools.reduce(jnp.maximum, [jnp.max(s, axis=0, keepdims=True) for s in scores])
-            total = jnp.zeros_like(peak)
-            mixed = jnp.zeros((HEAD_DIM, QB), F32)
-            rows = slice(head * HEAD_DIM, (head + 1) * HEAD_DIM)
-            for s, (first, last, _) in zip(scores, spans(start, length, QB)):
-                w = jnp.exp(s - peak)
-                total = total + jnp.sum(w, axis=0, keepdims=True)
-                mixed = mixed + nn(value_t[rows, first:last], w.astype(BF16))
-            parts.append(mixed / total)
-            lse_ref[0, head : head + 1, start : start + QB] = peak + jnp.log(total)
-        o_ref[start : start + QB, :] = jnp.concatenate(parts, axis=0).T
+        scores = []
+        for first, last, mask in spans(start, length, QB):
+            s = nt(keys[head][first:last], query)
+            scores.append(masked(s, first, start, prefix) if mask else s)
+        return scores
+
+    parts = []
+    ahead = score(*units[0])
+    for unit, (start, head) in enumerate(units):
+        scores = ahead
+        if unit + 1 < len(units):
+            ahead = score(*units[unit + 1])
+        peak = functools.reduce(jnp.maximum, [jnp.max(s, axis=0, keepdims=True) for s in scores])
+        total = jnp.zeros_like(peak)
+        mixed = jnp.zeros((HEAD_DIM, QB), F32)
+        rows = slice(head * HEAD_DIM, (head + 1) * HEAD_DIM)
+        for s, (first, last, _) in zip(scores, spans(start, length, QB)):
+            w = jnp.exp(s - peak)
+            total = total + jnp.sum(w, axis=0, keepdims=True)
+            mixed = mixed + nn(value_t[rows, first:last], w.astype(BF16))
+        parts.append(mixed / total)
+        lse_ref[0, head : head + 1, start : start + QB] = peak + jnp.log(total)
+        if head == 1:
+            o_ref[start : start + QB, :] = jnp.concatenate(parts, axis=0).T
+            parts = []
 
     @pl.when(pid == pl.num_programs(0) - 1)
     def _():
@@ -245,18 +255,19 @@
         svec_ref[...] = jnp.zeros_like(svec_ref)
         swide_ref[...] = jnp.zeros_like(swide_ref)
 
+    arrive(moves)
     sub_gain, sub_bias, out_bias, ffn_gain, ffn_bias, down_bias = [vec_ref[i : i + 1, :] for i in range(6)]
     up_bias, inner_gain, inner_bias = [wide_ref[i : i + 1, :] for i in range(3)]
     xhat2, inv2 = normed(att_ref[...])
     n2 = (xhat2 * sub_gain + sub_bias).astype(BF16)
     n2_ref[...] = n2.T
-    arrive(moves[:2])
     middle = x_ref[...].astype(F32) + nn(n2, wo_ref[...]) + out_bias
     xhat3, inv3 = normed(middle)
     n3 = (xhat3 * ffn_gain + ffn_bias).astype(BF16)
     n3_ref[...] = n3.T
-    arrive(moves[2:4])
+    g = g_ref[...]
     hidden = nn(n3, wu_ref[...]) + up_bias
+    e = nt(g, wd_ref[...])
     half = 0.5 + 0.5 * lax.erf(hidden * (2.0**-0.5))
     act_ref[...] = hidden * half
     slope_ref[...] = half + hidden * (jnp.exp(-0.5 * hidden * hidden) * 0.3989422804014327)
@@ -264,10 +275,7 @@
     n4 = (xhat4 * inner_gain + inner_bias).astype(BF16)
     n4_ref[...] = n4
     act_ref[...] = xhat4
-    arrive(moves[4:])
     out_ref[...] = (middle + nn(n4, wd_ref[...]) + down_bias).astype(BF16)
-    g = g_ref[...]
-    e = nt(g, wd_ref[...])
     xhat4 = act_ref[...]
     swide_ref[1] += colsum(e * xhat4)
     swide_ref[2] += colsum(e)

time: 240 us -> 232 us (0.967)
  Pallas kernels: 229 us -> 221 us
    pallas_call x1, Pallas kernels: 48.1 us -> 43 us  [middle_stage(): pl.pallas_call(mid_kernel, grid=(rows // block,), in_specs=[row(D), row(D...]
    pallas_call x1, Pallas kernels: 20.1 us -> 17.1 us  [attn_fwd(): pl.pallas_call(attn_fwd_kernel, grid=(pairs,), in_specs=[pl.BlockSpec(mem...]
where the time goes in v7:
time: 232 us; the launch traced here: 231 us
  Pallas kernels  221 us (95%)
  matrix products  9.13 us (4%)
    pallas_call x1, Pallas kernels, tail_stage(): pl.pallas_call(functools.partial(tail_kernel, dims, table, late, schedule...  137 us
    pallas_call x1, Pallas kernels, middle_stage(): pl.pallas_call(mid_kernel, grid=(rows // block,), in_specs=[row(D), row(D...  43 us
    pallas_call x1, Pallas kernels, attn_fwd(): pl.pallas_call(attn_fwd_kernel, grid=(pairs,), in_specs=[pl.BlockSpec(mem...  17.1 us
    pallas_call x1, Pallas kernels, head_stage(): pl.pallas_call(head_kernel, in_specs=[vmem] * 3 + [hbm] * 2 + [vmem] * 10...  12.9 us
    pallas_call x1, Pallas kernels, unpack(): pl.pallas_call(unpack_kernel, grid=(steps,), in_specs=[block(v) for v in...  11.3 us
    dot_general x1, matrix products, tn(): lax.dot_general(a, b, (((0,), (0,)), ((), ())), preferred_element_type=F32)  9.13 us

profile of v7, /device:TPU:0, one launch (start us, length us, event | category | flops | bytes accessed | tf_op | source)
XLA Modules:
  0.0 231.2 jit_solution(10721525505159389324)
XLA Ops:
  0.7 12.9 %head_stage.1 = (bf16[1024,2304]{1,0:T(8,128)(2,1)}, bf16[768,1024]{1,0:T(8,128)(2,1)}, bf16[768,2304]{1,0:T(8,128)(2,1)}, bf16[384,768]{1,0:T(8,128)(2,1)}, f32[6,768]{1,0:T(8,128)}, /*index=5*/f32[3,3072]{1,0:T(4,128)}) custom-call(bf16[1024,768]{1,0:T(8,128)(2,1)} %refs_9_.1, f32[768]{0:T(1024)} %refs_11_.1, f32[768]{0:T(1024)} %bias_ref.1, ...), custom_call_target="tpu_custom_call" | custom-call | tf_op jit(solution)/shard_map/head_stage/pallas_call | solution.py:1026
  13.6 17.1 %attn_fwd.1 = (f32[1024,768]{1,0:T(8,128)}, f32[6,8,1024]{2,1,0:T(8,128)}, bf16[768,1536]{1,0:T(8,128)(2,1)}, bf16[1536,768]{1,0:T(8,128)(2,1)}) custom-call(s32[2]{0:T(128)} %refs_0_.1, bf16[1024,2304]{1,0:T(8,128)(2,1)} %get-tuple-element.61.q_ref.k_ref.v_ref.refs_1_.refs_2_.refs_3_, ...), custom_call_target="tpu_custom_call" | custom-call | tf_op jit(solution)/shard_map/attn_fwd/pallas_call | solution.py:125
  30.7 43.0 %middle_stage.1 = (bf16[1024,768]{1,0:T(8,128)(2,1)}, bf16[768,1024]{1,0:T(8,128)(2,1)}, bf16[768,1024]{1,0:T(8,128)(2,1)}, bf16[1024,3072]{1,0:T(8,128)(2,1)}, ...) custom-call(bf16[1024,768]{1,0:T(8,128)(2,1)} %refs_9_.1, ...), custom_call_target="tpu_custom_call" | custom-call | tf_op jit(solution)/shard_map/middle_stage/pallas_call | solution.py:309
  73.7 9.1 %convolution_convert_fusion = bf16[3072,768]{1,0:T(8,128)(2,1)} fusion(bf16[1024,3072]{1,0:T(8,128)(2,1)} %get-tuple-element.80, bf16[1024,768]{1,0:T(8,128)(2,1)} %g_ref.1), kind=kOutput, calls=%fused_computation | convolution fusion | flops 4834197504 | bytes 12582912 | tf_op jit(solution)/shard_map/dot_general | solution.py:30
  82.8 136.8 %tail_stage.1 = (f32[1024,768]{1,0:T(8,128)}, bf16[2,4,2,2,48,768]{5,4,3,2,1,0:T(8,128)(2,1)}, bf16[4,2,2,48,1536]{4,3,2,1,0:T(8,128)(2,1)}, bf16[3,4,2,2,48,384...) custom-call(s32[2]{0:T(128)} %refs_0_.1, ...), custom_call_target="tpu_custom_call" | custom-call | tf_op jit(solution)/shard_map/tail_stage/pallas_call | solution.py:890
  219.7 11.3 %unpack.1 = (f32[1024,768]{1,0:T(8,128)}, f32[1536,768]{1,0:T(8,128)}, f32[768,1536]{1,0:T(8,128)}, f32[2304,384]{1,0:T(8,128)}, f32[384,768]{1,0:T(8,128)}, /*i...) custom-call(f32[1024,768]{1,0:T(8,128)} %get-tuple-element.81.ig_ref, ...), custom_call_target="tpu_custom_call" | custom-call | tf_op jit(solution)/shard_map/unpack/pallas_call | solution.py:940
